TPU v7x, 32 devices: a whole 2x2x4 slice. The times are simulated.
32 devices in a mesh: groups: 2 (over x), slab: 16 (over z, y, core).
Axes of the slice: x: 2, y: 2, z: 4, core: 2. Of those that a mesh axis runs over, the one named last changes fastest.
Arguments:
- adjoint_now: float32 [128, 320, 320], P(('groups', 'slab')), parts along dimension 0, may hold values from -6 to 6
- adjoint_prior: float32 [128, 320, 320], P(('groups', 'slab')), parts along dimension 0, may hold values from -6 to 6
- velocity_term: float32 [128, 320, 320], P(('groups', 'slab')), parts along dimension 0, may hold values from 0.04 to 0.2
- forward_field: float32 [2, 128, 320, 320], P(None, ('groups', 'slab')), parts along dimension 1, may hold values from -6 to 6
- traces: bfloat16 [2048, 2048], P(('groups', 'slab')), parts along dimension 0, may hold values from -6 to 6
- time_filter: bfloat16 [2, 2048], replicated, may hold values from -0.125 to 0.125
- slab_of_trace: int32 [2048, 1], P(('groups', 'slab')), parts along dimension 0, may hold values from 0 to 15; in each aligned block of 64 rows (0 to 63, 64 to 127, ...) at most 4 rows name the same one
- cell_index: int32 [2048], P(('groups', 'slab')), parts along dimension 0, may hold values from 0 to 409599
Outputs:
- gradient_image: float32 [128, 320, 320], P(('groups', 'slab')), parts along dimension 0
- adjoint_last: float32 [128, 320, 320], P(('groups', 'slab')), parts along dimension 0
- adjoint_before: float32 [128, 320, 320], P(('groups', 'slab')), parts along dimension 0
There are 2 independent parts, one for each index of `groups`. A program takes and returns all parts, laid end to end along the dimension named above; an argument that names none is the same for every part. Nothing has to cross between parts.
Inputs may be any that keep to these rules, and one draw needn't show every extreme that they name: `slab_of_trace`: of one device's 64 rows at most 4 name the same slab, and in every draw some device sends exactly 4 rows to one slab.
All inputs are finite; a program needn't handle non-finite values.
Results may differ from a plain program's by a relative error of at most 0.0003.
Values may be sent and summed in bfloat16 or wider, within the bound.
No kernel may reach another device: no remote copies, remote signals or barrier semaphores. Data moves between devices by JAX's collectives and lax.ppermute only.
A program may use at most 128 MiB of HBM per device.

v0:
```python
import jax
import jax.numpy as jnp
from jax import lax
from jax.sharding import PartitionSpec as P

CAP = 4
STEPS = 2


STENCIL_WEIGHTS = (-205.0 / 72.0, 8.0 / 5.0, -1.0 / 5.0, 8.0 / 315.0, -1.0 / 560.0)


def with_halo(x, sides, width):
    for axis, dim in sides:
        devices, length = (lax.axis_size(axis), x.shape[dim])
        up = [(i, (i + 1) % devices) for i in range(devices - 1)]
        down = [(j, i) for i, j in up]
        last = lax.slice_in_dim(x, length - width, length, axis=dim)
        leading = lax.slice_in_dim(x, 0, width, axis=dim)
        before = lax.ppermute(last, axis, up)
        after = lax.ppermute(leading, axis, down)
        x = jnp.concatenate([before, x, after], axis=dim)
    return x


def laplace(extended):
    widened = jnp.pad(extended, ((0, 0), (4, 4), (4, 4)))
    inner = extended.shape[0] - 8
    width_x = extended.shape[1]
    width_y = extended.shape[2]
    centre = widened[4 : 4 + inner, 4 : 4 + width_x, 4 : 4 + width_y]
    summed = 3.0 * STENCIL_WEIGHTS[0] * centre
    for offset in range(1, 5):
        pair = widened[4 + offset : 4 + offset + inner, 4 : 4 + width_x, 4 : 4 + width_y]
        pair = pair + widened[4 - offset : 4 - offset + inner, 4 : 4 + width_x, 4 : 4 + width_y]
        pair = pair + widened[4 : 4 + inner, 4 + offset : 4 + offset + width_x, 4 : 4 + width_y]
        pair = pair + widened[4 : 4 + inner, 4 - offset : 4 - offset + width_x, 4 : 4 + width_y]
        pair = pair + widened[4 : 4 + inner, 4 : 4 + width_x, 4 + offset : 4 + offset + width_y]
        pair = pair + widened[4 : 4 + inner, 4 : 4 + width_x, 4 - offset : 4 - offset + width_y]
        summed = summed + STENCIL_WEIGHTS[offset] * pair
    return summed


def on_device(
    adjoint_now,
    adjoint_prior,
    velocity_term,
    forward_field,
    traces,
    time_filter,
    slab_of_trace,
    cell_index,
):
    slab_count = lax.axis_size("slab")
    depth, width_x, width_y = adjoint_now.shape
    target = slab_of_trace[:, 0]
    onehot = (target[:, None] == jnp.arange(slab_count, dtype=jnp.int32)[None, :]).astype(jnp.int32)
    before = jnp.cumsum(onehot, axis=0) - onehot
    slot_rank = jnp.sum(before * onehot, axis=1)
    cell_buffer = jnp.zeros((slab_count, CAP), jnp.int32).at[target, slot_rank].set(cell_index)
    own_sources = jnp.dot(traces, time_filter.T, preferred_element_type=jnp.float32)
    source_buffer = (
        jnp.zeros((slab_count, CAP, STEPS), jnp.float32).at[target, slot_rank].set(own_sources)
    )
    sources, slot_cells = (
        lax.all_to_all(source_buffer, "slab", split_axis=0, concat_axis=0, tiled=True),
        lax.all_to_all(cell_buffer, "slab", split_axis=0, concat_axis=0, tiled=True),
    )
    flat_cells = slot_cells.reshape(-1)
    flat_sources = sources.reshape(-1, STEPS)
    current = adjoint_now
    previous = adjoint_prior
    image_sum = jnp.zeros(adjoint_now.shape, jnp.float32)
    for section_index in range(STEPS):
        inject = (
            jnp.zeros((depth * width_x * width_y,), jnp.float32)
            .at[flat_cells]
            .add(flat_sources[:, section_index])
        )
        inject = inject.reshape(depth, width_x, width_y)
        extended = with_halo(current, (("slab", 0),), 4)
        advanced = 2.0 * current - previous + velocity_term * (laplace(extended) + inject)
        image_sum = image_sum + forward_field[section_index] * advanced
        previous = current
        current = advanced
    return (image_sum, current, previous)


def solution(mesh):
    return jax.shard_map(
        on_device,
        mesh=mesh,
        in_specs=(
            P(("groups", "slab"), None, None),
            P(("groups", "slab"), None, None),
            P(("groups", "slab"), None, None),
            P(None, ("groups", "slab"), None, None),
            P(("groups", "slab"), None),
            P(),
            P(("groups", "slab"), None),
            P(("groups", "slab")),
        ),
        out_specs=(
            P(("groups", "slab"), None, None),
            P(("groups", "slab"), None, None),
            P(("groups", "slab"), None, None),
        ),
        check_vma=False,
    )
```

profile of v0, /device:TPU:9, one launch (start us, length us, event | category | flops | bytes accessed | tf_op | source)
XLA Modules:
  0.0 167.1 jit_solution(10611496506758131491)
XLA Ops:
  0.6 0.0 copy-start
  0.6 3.8 %collective-permute-start.1 = (f32[4,320,320]{2,1,0:T(8,128)}, f32[4,320,320]{2,1,0:T(8,128)}, u32[]{:S(2)}, u32[]{:S(2)}) collective-permute-start(f32[4,320,320]{2,1,0:T(8,128)} %param.8), channel_id=1, source_target_pairs={{0,1},{1,2},{2,3},{3,4},{4,5},{5,6},{6,7},{7,8},{8,9},{9,10},{10,1... | collective-permute-start | bytes 4915208 | tf_op jit(solution)/shard_map/ppermute | solution.py:20
  4.5 1.9 %collective-permute-start = (f32[4,320,320]{2,1,0:T(8,128)}, f32[4,320,320]{2,1,0:T(8,128)}, u32[]{:S(2)}, u32[]{:S(2)}) collective-permute-start(f32[4,320,320]{2,1,0:T(8,128)} %param.8), channel_id=1, source_target_pairs={{1,0},{2,1},{3,2},{4,3},{5,4},{6,5},{7,6},{8,7},{9,8},{10,9},{11,1... | collective-permute-start | bytes 4915208 | tf_op jit(solution)/shard_map/ppermute | solution.py:21
  6.4 0.7 fusion.45
  7.2 0.1 reduce_window_sum.11
  7.3 0.8 select_reduce_fusion
  8.1 0.7 fusion.48
  8.8 5.8 %scatter_fusion = s32[16,4]{0,1:T(4,128)S(1)} fusion(s32[16,4]{0,1:T(4,128)S(1)} %broadcast_in_dim.4, s32[64]{0:T(128)S(1)} %fusion.48, s32[64]{0:T(128)} %param.15), kind=kCustom, calls=%fused_computation | custom fusion | bytes 1280 | tf_op jit(solution)/shard_map/scatter | solution.py:60
  14.5 0.7 copy.15
  15.2 6.5 %all-to-all-start = ((s32[16,1,4]{2,1,0:T(1,128)}), s32[16,1,4]{2,1,0:T(1,128)S(1)}, u32[]{:S(2)}, u32[]{:S(2)}) async-start(s32[16,1,4]{2,1,0:T(1,128)} %copy.15), calls=%async_computation | async-start | bytes 16384 | tf_op jit(solution)/shard_map/all_to_all | solution.py:67
  21.7 0.0 copy-done
  21.7 0.9 fusion.50
  22.6 3.6 %scatter_fusion.1 = f32[16,4,2]{2,1,0:T(4,128)S(1)} fusion(f32[16,4,2]{2,1,0:T(4,128)S(1)} %broadcast_in_dim.5, s32[64]{0:T(128)S(1)} %fusion.48, f32[64,2]{1,0:T(8,128)S(1)} %fusion.50), kind=kCustom, calls=%fused_computation.1 | custom fusion | bytes 2048 | tf_op jit(solution)/shard_map/scatter | solution.py:63
  26.2 0.8 copy.17
  27.0 22.0 %all-to-all-done = s32[16,1,4]{2,1,0:T(1,128)S(1)} async-done(((s32[16,1,4]{2,1,0:T(1,128)}), s32[16,1,4]{2,1,0:T(1,128)S(1)}, u32[]{:S(2)}, u32[]{:S(2)}) %all-to-all-start) | async-done | bytes 288 | tf_op jit(solution)/shard_map/all_to_all | solution.py:67
  49.1 5.5 %all-to-all-start.1 = ((f32[16,4,2]{1,2,0:T(2,128)}), f32[16,4,2]{1,2,0:T(2,128)S(1)}, u32[]{:S(2)}, u32[]{:S(2)}) async-start(f32[16,4,2]{1,2,0:T(2,128)} %copy.17), calls=%async_computation.1 | async-start | bytes 32768 | tf_op jit(solution)/shard_map/all_to_all | solution.py:66
  54.6 0.5 broadcast.184
  55.1 0.7 reduce.3
  55.8 0.1 reshape.62
  55.9 3.7 %all-to-all-done.1 = f32[16,4,2]{1,2,0:T(2,128)S(1)} async-done(((f32[16,4,2]{1,2,0:T(2,128)}), f32[16,4,2]{1,2,0:T(2,128)S(1)}, u32[]{:S(2)}, u32[]{:S(2)}) %all-to-all-start.1) | async-done | bytes 544 | tf_op jit(solution)/shard_map/all_to_all | solution.py:66
  59.6 0.1 reshape.63
  59.7 1.3 scatter_custom_fusion.2
  61.1 2.0 %reshape.64 = f32[4,320,320]{2,1,0:T(8,128)} reshape(f32[409600]{0:T(1024)S(1)} %scatter_custom_fusion.2) | data formatting | bytes 3276800 | tf_op jit(solution)/shard_map/reshape | solution.py:80
  63.0 0.0 copy-start.1
  63.0 0.0 collective-permute-done.1
  63.0 3.1 %constant_dynamic-update-slice_fusion.3 = f32[8,320,320]{2,1,0:T(8,128)} fusion(f32[4,320,320]{2,1,0:T(8,128)} %collective-permute-done.1), kind=kLoop, calls=%fused_computation.102 | loop fusion | bytes 3604480
  66.1 0.0 copy-done.1
  66.1 2.3 %constant_dynamic-update-slice_fusion.1 = (f32[8,320,320]{2,1,0:T(8,128)}, f32[8,320,320]{2,1,0:T(8,128)}) fusion(f32[4,320,320]{2,1,0:T(8,128)S(1)} %copy-done.1, f32[8,320,320]{2,1,0:T(8,128)} %constant_dynamic-update-slice_fusion.3), kind=kLoop, calls=%fused_computation.100 | loop fusion | bytes 5570560
  68.4 0.0 collective-permute-done
  68.4 6.2 %select_maximum_fusion.2 = f32[12,328,328]{2,1,0:T(8,128)} fusion(f32[4,320,320]{2,1,0:T(8,128)} %collective-permute-done, f32[4,320,320]{2,1,0:T(8,128)S(1)} %copy-done.1, f32[4,320,320]{2,1,0:T(8,128)} %collective-permute-done.1), kind=kLoop, calls=%fused_computation.10 | loop fusion | flops 19365120 | bytes 10079232 | tf_op jit(solution)/shard_map/concatenate | solution.py:22
  74.6 3.0 %constant_dynamic-update-slice_fusion = f32[8,320,320]{2,1,0:T(8,128)} fusion(f32[8,320,320]{2,1,0:T(8,128)} %get-tuple-element.5, f32[4,320,320]{2,1,0:T(8,128)} %collective-permute-done), kind=kLoop, calls=%fused_computation.99 | loop fusion | bytes 3932160 | tf_op jit(solution)/shard_map/concatenate | solution.py:22
  77.6 25.9 %fusion.33 = f32[4,320,320]{2,1,0:T(8,128)} fusion(f32[4,320,320]{2,1,0:T(8,128)} %param.10, f32[4,320,320]{2,1,0:T(8,128)} %reshape.64, f32[12,328,328]{2,1,0:T(8,128)} %select_maximum_fusion.2, f32[8,320,320]{2,1,0:T(8,128)} %get-tuple-element.6, f32[8,320,320]{2,1,0:T(8,128)} %constant_dynamic-update-slice_fusion, ...), kind=kLoop, calls=%fused_computation.64 | loop fusion | flops 13926400 | bytes 47513600 | tf_op jit(solution)/shard_map/add | solution.py:82
  103.5 2.3 %collective-permute-start.2 = (f32[4,320,320]{2,1,0:T(8,128)}, f32[4,320,320]{2,1,0:T(8,128)}, u32[]{:S(2)}, u32[]{:S(2)}) collective-permute-start(f32[4,320,320]{2,1,0:T(8,128)} %fusion.33), channel_id=1, source_target_pairs={{1,0},{2,1},{3,2},{4,3},{5,4},{6,5},{7,6},{8,7},{9,8},{10,9},{11,1... | collective-permute-start | bytes 4915208 | tf_op jit(solution)/shard_map/ppermute | solution.py:21
  105.9 3.3 %collective-permute-start.3 = (f32[4,320,320]{2,1,0:T(8,128)}, f32[4,320,320]{2,1,0:T(8,128)}, u32[]{:S(2)}, u32[]{:S(2)}) collective-permute-start(f32[4,320,320]{2,1,0:T(8,128)} %fusion.33), channel_id=1, source_target_pairs={{0,1},{1,2},{2,3},{3,4},{4,5},{5,6},{6,7},{7,8},{8,9},{9,10},{10,1... | collective-permute-start | bytes 4915208 | tf_op jit(solution)/shard_map/ppermute | solution.py:20
  109.1 2.1 %scatter_custom_fusion.3 = f32[409600]{0:T(1024)} fusion(s32[64]{0:T(128)S(1)} %fusion.47, f32[64]{0:T(128)S(1)} %get-tuple-element.7, f32[]{:T(128)} %constant.13.clone.1), kind=kCustom, calls=%fused_computation.92 | custom fusion | flops 64 | bytes 1638404 | tf_op jit(solution)/shard_map/scatter-add | solution.py:78
  111.3 2.9 %reshape.65 = f32[4,320,320]{2,1,0:T(8,128)} reshape(f32[409600]{0:T(1024)} %scatter_custom_fusion.3) | data formatting | bytes 3276800 | tf_op jit(solution)/shard_map/reshape | solution.py:80
  114.1 0.0 copy-start.2
  114.1 0.0 copy-start.3
  114.1 0.0 copy-start.4
  114.1 36.7 %collective-permute-done.2 = f32[4,320,320]{2,1,0:T(8,128)} collective-permute-done((f32[4,320,320]{2,1,0:T(8,128)}, f32[4,320,320]{2,1,0:T(8,128)}, u32[]{:S(2)}, u32[]{:S(2)}) %collective-permute-start.2) | collective-permute-done | bytes 1638432 | tf_op jit(solution)/shard_map/ppermute | solution.py:21
  150.9 0.0 collective-permute-done.3
  150.9 0.0 copy-start.5
  150.9 5.1 %select_maximum_fusion = f32[12,328,328]{2,1,0:T(8,128)S(1)} fusion(f32[4,320,320]{2,1,0:T(8,128)} %collective-permute-done.2, f32[4,320,320]{2,1,0:T(8,128)} %fusion.33, f32[4,320,320]{2,1,0:T(8,128)} %collective-permute-done.3), kind=kLoop, calls=%fused_computation.8 | loop fusion | flops 19365120 | bytes 10079232 | tf_op jit(solution)/shard_map/concatenate | solution.py:22
  155.9 0.0 copy-done.2
  156.0 0.0 copy-done.3
  156.0 0.0 copy-done.4
  156.0 0.0 copy-done.5
  156.0 11.1 %fusion.40 = (f32[4,320,320]{2,1,0:T(8,128)}, f32[4,320,320]{2,1,0:T(8,128)}) fusion(f32[4,320,320]{2,1,0:T(8,128)S(1)} %copy-done.2, f32[2,4,320,320]{3,2,1,0:T(8,128)S(1)} %copy-done.5, f32[4,320,320]{2,1,0:T(8,128)S(1)} %copy-done.3, f32[4,320,320]{2,1,0:T(8,128)S(1)} %copy-done.4, f32[12,328,328]{2,1,0:T(8,128)S(1)} %select_maximum_fusion, ...), kind=kLoop, calls=%fused_computation.90 | loop fusion | flops 17612800 | bytes 42598400 | tf_op jit(solution)/shard_map/add | solution.py:83
  (5 shorter events, 0.0 us)
Async XLA Ops:
  0.6 21.1 %copy-start = (bf16[64,2048]{1,0:T(8,128)(2,1)S(1)}, bf16[64,2048]{1,0:T(8,128)(2,1)}, u32[]{:S(2)}) copy-start(bf16[64,2048]{1,0:T(8,128)(2,1)} %param.12) | copy-start | bytes 786436
  0.6 62.4 %collective-permute-start.1 = (f32[4,320,320]{2,1,0:T(8,128)}, f32[4,320,320]{2,1,0:T(8,128)}, u32[]{:S(2)}, u32[]{:S(2)}) collective-permute-start(f32[4,320,320]{2,1,0:T(8,128)} %param.8), channel_id=1, source_target_pairs={{0,1},{1,2},{2,3},{3,4},{4,5},{5,6},{6,7},{7,8},{8,9},{9,10},{10,1... | collective-permute-start | bytes 4915208 | tf_op jit(solution)/shard_map/ppermute | solution.py:20
  4.5 63.9 %collective-permute-start = (f32[4,320,320]{2,1,0:T(8,128)}, f32[4,320,320]{2,1,0:T(8,128)}, u32[]{:S(2)}, u32[]{:S(2)}) collective-permute-start(f32[4,320,320]{2,1,0:T(8,128)} %param.8), channel_id=1, source_target_pairs={{1,0},{2,1},{3,2},{4,3},{5,4},{6,5},{7,6},{8,7},{9,8},{10,9},{11,1... | collective-permute-start | bytes 4915208 | tf_op jit(solution)/shard_map/ppermute | solution.py:21
  15.2 33.9 %all-to-all-start = ((s32[16,1,4]{2,1,0:T(1,128)}), s32[16,1,4]{2,1,0:T(1,128)S(1)}, u32[]{:S(2)}, u32[]{:S(2)}) async-start(s32[16,1,4]{2,1,0:T(1,128)} %copy.15), calls=%async_computation | async-start | bytes 16384 | tf_op jit(solution)/shard_map/all_to_all | solution.py:67
  49.1 10.6 %all-to-all-start.1 = ((f32[16,4,2]{1,2,0:T(2,128)}), f32[16,4,2]{1,2,0:T(2,128)S(1)}, u32[]{:S(2)}, u32[]{:S(2)}) async-start(f32[16,4,2]{1,2,0:T(2,128)} %copy.17), calls=%async_computation.1 | async-start | bytes 32768 | tf_op jit(solution)/shard_map/all_to_all | solution.py:66
  63.0 3.1 %copy-start.1 = (f32[4,320,320]{2,1,0:T(8,128)S(1)}, f32[4,320,320]{2,1,0:T(8,128)}, u32[]{:S(2)}) copy-start(f32[4,320,320]{2,1,0:T(8,128)} %param.8) | copy-start | bytes 4915204
  103.5 47.3 %collective-permute-start.2 = (f32[4,320,320]{2,1,0:T(8,128)}, f32[4,320,320]{2,1,0:T(8,128)}, u32[]{:S(2)}, u32[]{:S(2)}) collective-permute-start(f32[4,320,320]{2,1,0:T(8,128)} %fusion.33), channel_id=1, source_target_pairs={{1,0},{2,1},{3,2},{4,3},{5,4},{6,5},{7,6},{8,7},{9,8},{10,9},{11,1... | collective-permute-start | bytes 4915208 | tf_op jit(solution)/shard_map/ppermute | solution.py:21
  105.9 45.0 %collective-permute-start.3 = (f32[4,320,320]{2,1,0:T(8,128)}, f32[4,320,320]{2,1,0:T(8,128)}, u32[]{:S(2)}, u32[]{:S(2)}) collective-permute-start(f32[4,320,320]{2,1,0:T(8,128)} %fusion.33), channel_id=1, source_target_pairs={{0,1},{1,2},{2,3},{3,4},{4,5},{5,6},{6,7},{7,8},{8,9},{9,10},{10,1... | collective-permute-start | bytes 4915208 | tf_op jit(solution)/shard_map/ppermute | solution.py:20
  114.1 41.8 %copy-start.2 = (f32[4,320,320]{2,1,0:T(8,128)S(1)}, f32[4,320,320]{2,1,0:T(8,128)}, u32[]{:S(2)}) copy-start(f32[4,320,320]{2,1,0:T(8,128)} %fusion.33) | copy-start | bytes 4915204
  114.1 41.8 %copy-start.3 = (f32[4,320,320]{2,1,0:T(8,128)S(1)}, f32[4,320,320]{2,1,0:T(8,128)}, u32[]{:S(2)}) copy-start(f32[4,320,320]{2,1,0:T(8,128)} %param.10) | copy-start | bytes 4915204
  114.1 41.8 %copy-start.4 = (f32[4,320,320]{2,1,0:T(8,128)S(1)}, f32[4,320,320]{2,1,0:T(8,128)}, u32[]{:S(2)}) copy-start(f32[4,320,320]{2,1,0:T(8,128)} %reshape.65) | copy-start | bytes 4915204
  150.9 5.1 %copy-start.5 = (f32[2,4,320,320]{3,2,1,0:T(8,128)S(1)}, f32[2,4,320,320]{3,2,1,0:T(8,128)}, u32[]{:S(2)}) copy-start(f32[2,4,320,320]{3,2,1,0:T(8,128)} %param.11) | copy-start | bytes 9830404
where the time goes:
time: 169 us; the launch traced here: 167 us
  waiting for transfers between devices  62.5 us (37%)
  other arithmetic  54.7 us (32%)
  local copies, waits for them, and re-layouts  24.8 us (15%)
  starting transfers between devices  23.4 us (14%)
    ppermute x2, waiting for transfers between devices, with_halo(): after = lax.ppermute(leading, axis, down)  36.7 us
    add x1, other arithmetic, on_device(): 2.0 * current - previous + velocity_term * (laplace(extended) + inject)  25.9 us
    all_to_all x1, waiting for transfers between devices, on_device(): lax.all_to_all(cell_buffer, 'slab', split_axis=0, concat_axis=0, tiled=True)  22 us
    concatenate x2, other arithmetic, with_halo(): x = jnp.concatenate([before, x, after], axis=dim)  11.2 us
    add x1, other arithmetic, on_device(): image_sum = image_sum + forward_field[section_index] * advanced  11.1 us
    ppermute x2, starting transfers between devices, with_halo(): before = lax.ppermute(last, axis, up)  7.1 us
    all_to_all x1, starting transfers between devices, on_device(): lax.all_to_all(cell_buffer, 'slab', split_axis=0, concat_axis=0, tiled=True)  6.51 us
    scatter x1, local copies, waits for them, and re-layouts, on_device(): jnp.zeros((slab_count, CAP), jnp.int32).at[target, slot_rank]  5.75 us
  transfers between devices with their start and end apart: 6, of which 3 were waited for; matrix products, arithmetic and copies ran while one was open for 17% of the time, Pallas kernels for 0%

commit v1 on v0

v1 whole, which is shorter than its diff:
```python
import functools

import jax
import jax.numpy as jnp
from jax import lax
from jax.experimental import pallas as pl
from jax.experimental.pallas import tpu as pltpu
from jax.sharding import PartitionSpec as P

CAP = 4
STEPS = 2
W = (-205.0 / 72.0, 8.0 / 5.0, -1.0 / 5.0, 8.0 / 315.0, -1.0 / 560.0)
HALO = 4
ROWS = 16
LANES = 128
F32 = jnp.float32
BF16 = jnp.bfloat16
VMEM = pl.BlockSpec(memory_space=pltpu.VMEM)
SMEM = pl.BlockSpec(memory_space=pltpu.SMEM)


def params():
    return pltpu.CompilerParams(vmem_limit_bytes=24 << 20)


def payload_lanes(width):
    full = width // LANES * LANES
    rest = width - full
    if rest == 0:
        return HALO * full
    return HALO * full + (2 * LANES if rest * 2 <= LANES else HALO * LANES)


def depth_at(j, depth):
    odd = lax.rem(lax.axis_index("slab"), 2)
    return j + (1 - odd) * (depth - 1 - 2 * j)


def encode(u):
    t1 = u[0].astype(BF16).astype(F32)
    e1 = u[0] - t1
    t2 = (u[1] + (W[2] / W[3]) * e1).astype(BF16).astype(F32)
    t3 = u[2].astype(BF16).astype(F32)
    t0 = W[1] * e1 + W[2] * (u[1] - t2) + W[3] * (u[2] - t3) + W[4] * u[3]
    return (t0, t1, t2, t3)


def decode(t):
    t0, t1, t2, t3 = t
    return (
        t0 + W[1] * t1 + W[2] * t2 + W[3] * t3,
        W[2] * t1 + W[3] * t2 + W[4] * t3,
        W[3] * t1 + W[4] * t2,
        W[4] * t1,
    )


def put(ref, rows, t):
    width = t[0].shape[1]
    full = width // LANES * LANES
    rest = width - full
    for k in range(HALO):
        ref[rows, k * full : (k + 1) * full] = t[k][:, :full].astype(BF16)
    if rest == 0:
        return
    base = HALO * full
    if rest * 2 <= LANES:
        half = LANES // 2
        for k in range(0, HALO, 2):
            a = jnp.pad(t[k][:, full:], ((0, 0), (0, half - rest)))
            b = jnp.pad(t[k + 1][:, full:], ((0, 0), (0, half - rest)))
            ref[rows, base : base + LANES] = jnp.concatenate([a, b], axis=1).astype(BF16)
            base += LANES
    else:
        for k in range(HALO):
            tail = jnp.pad(t[k][:, full:], ((0, 0), (0, LANES - rest)))
            ref[rows, base : base + LANES] = tail.astype(BF16)
            base += LANES


def take(ref, rows, width):
    full = width // LANES * LANES
    rest = width - full
    main = [ref[rows, k * full : (k + 1) * full].astype(F32) for k in range(HALO)]
    if rest == 0:
        return main
    base = HALO * full
    tails = []
    if rest * 2 <= LANES:
        half = LANES // 2
        for k in range(0, HALO, 2):
            both = ref[rows, base : base + LANES].astype(F32)
            tails.append(both[:, :rest])
            tails.append(pltpu.roll(both, half, 1)[:, :rest])
            base += LANES
    else:
        for k in range(HALO):
            tails.append(ref[rows, base : base + LANES].astype(F32)[:, :rest])
            base += LANES
    return [jnp.concatenate([m, t], axis=1) for m, t in zip(main, tails)]


def row_loop(count, body):
    def step(i, carry):
        body(pl.multiple_of(i * ROWS, ROWS))
        return carry

    lax.fori_loop(0, count // ROWS, step, 0)


def pack_kernel(now, on_ref, off_ref):
    depth, width_x, _ = now.shape

    def body(r):
        rows = pl.ds(r, ROWS)
        u = [now[depth_at(j, depth), rows, :] for j in range(depth)]
        put(off_ref, rows, encode(u[::-1][:HALO]))
        put(on_ref, rows, encode(u[:HALO]))

    row_loop(width_x, body)


def route_kernel(slabs, width_y, traces, weights, target, cell, out):
    rows = traces.shape[0]
    lane = lax.broadcasted_iota(jnp.int32, (rows, rows), 1)
    row = lax.broadcasted_iota(jnp.int32, (rows, rows), 0)
    eye = lane == row
    target_row = jnp.broadcast_to(target[...], (rows, rows))
    cell_row = jnp.broadcast_to(cell[...], (rows, rows))
    target_col = jnp.sum(jnp.where(eye, target_row, 0), axis=1, keepdims=True)
    cell_col = jnp.sum(jnp.where(eye, cell_row, 0), axis=1, keepdims=True)
    same = (target_row == target_col) & (lane < row)
    rank = jnp.sum(jnp.where(same, 1, 0), axis=1, keepdims=True)
    values = traces[...].astype(F32)
    columns = [
        jnp.sum(values * weights[s : s + 1, :].astype(F32), axis=1, keepdims=True)
        for s in range(STEPS)
    ]
    cell_line = cell_col // width_y
    columns.append(cell_line.astype(F32))
    columns.append((cell_col - cell_line * width_y).astype(F32))
    spot = lax.broadcasted_iota(jnp.int32, (rows, LANES), 1)
    spread = jnp.zeros((rows, LANES), F32)
    for j, column in enumerate(columns):
        spread = jnp.where(spot == j * CAP + rank, column, spread)
    taker = lax.broadcasted_iota(jnp.int32, (slabs, rows), 0)
    chosen = (taker == jnp.broadcast_to(target[...], (slabs, rows))).astype(F32)
    picked = jnp.dot(
        chosen, spread, precision=lax.Precision.HIGHEST, preferred_element_type=F32
    )
    out[...] = picked.reshape(out.shape)


def fill(pad, source):
    depth, width_x, width_y = source.shape
    lanes = pad.shape[2]
    for z in range(depth):
        pad[z, 0:8, :] = jnp.zeros((8, lanes), F32)
        pad[z, 8 + width_x : 16 + width_x, :] = jnp.zeros((8, lanes), F32)

    def body(r):
        for z in range(depth):
            value = source[z, pl.ds(r, ROWS), :]
            pad[z, pl.ds(r + 8, ROWS), :] = jnp.pad(value, ((0, 0), (0, lanes - width_y)))

    row_loop(width_x, body)


def own_laplace(pad, r):
    depth = pad.shape[0]
    span = ROWS + 16
    blocks = [pad[z, pl.ds(r, span), :] for z in range(depth)]
    centre = [block[8 : 8 + ROWS, :] for block in blocks]
    lanes = pad.shape[2]
    out = []
    for z in range(depth):
        total = 3.0 * W[0] * centre[z]
        for k in range(1, HALO + 1):
            pair = pltpu.roll(blocks[z], k, 0)[8 : 8 + ROWS, :]
            pair = pair + pltpu.roll(blocks[z], span - k, 0)[8 : 8 + ROWS, :]
            pair = pair + pltpu.roll(centre[z], k, 1) + pltpu.roll(centre[z], lanes - k, 1)
            if z - k >= 0:
                pair = pair + centre[z - k]
            if z + k < depth:
                pair = pair + centre[z + k]
            total = total + W[k] * pair
        out.append(total)
    return centre, out


def inject(step, got, velocity, grid):
    depth, width_x, width_y = grid.shape
    lane = lax.broadcasted_iota(jnp.int32, (1, width_y), 1)

    def body(i, carry):
        for slot in range(CAP):
            source = got[i, 0, step * CAP + slot]
            line = got[i, 0, STEPS * CAP + slot].astype(jnp.int32)
            column = got[i, 0, (STEPS + 1) * CAP + slot].astype(jnp.int32)
            z = lax.div(line, jnp.int32(width_x))
            row = pl.ds(line - z * width_x, 1)
            extra = jnp.where(lane == column, velocity[z, row, :] * source, 0.0)
            grid[z, row, :] = grid[z, row, :] + extra
        return carry

    lax.fori_loop(0, got.shape[0], body, 0)


def own_kernel(now, prior, velocity, out, pad):
    depth, width_x, width_y = now.shape
    fill(pad, now)

    def body(r):
        rows = pl.ds(r, ROWS)
        centre, lap = own_laplace(pad, r)
        for z in range(depth):
            c, l = centre[z][:, :width_y], lap[z][:, :width_y]
            out[z, rows, :] = 2.0 * c - prior[z, rows, :] + velocity[z, rows, :] * l

    row_loop(width_x, body)


def inject_kernel(step, got, velocity, grid_in, out):
    del grid_in
    inject(step, got, velocity, out)


def halo_sum(got_on, got_off, rows, width_y, depth):
    near = decode(take(got_on, rows, width_y))
    far = decode(take(got_off, rows, width_y))
    out = []
    for j in range(depth):
        terms = [near[j]] if j < HALO else []
        if depth - 1 - j < HALO:
            terms.append(far[depth - 1 - j])
        out.append(functools.reduce(lambda a, b: a + b, terms) if terms else None)
    return out


def close_kernel(partial, velocity, got_on, got_off, out, on_ref, off_ref):
    depth, width_x, width_y = out.shape

    def body(r):
        rows = pl.ds(r, ROWS)
        halo = halo_sum(got_on, got_off, rows, width_y, depth)
        u = []
        for j in range(depth):
            z = depth_at(j, depth)
            value = partial[z, rows, :]
            if halo[j] is not None:
                value = value + velocity[z, rows, :] * halo[j]
            out[z, rows, :] = value
            u.append(value)
        put(off_ref, rows, encode(u[::-1][:HALO]))
        put(on_ref, rows, encode(u[:HALO]))

    row_loop(width_x, body)


def second_kernel(got, current, previous, velocity, forward, out, image, pad):
    depth, width_x, width_y = current.shape
    fill(pad, current)

    def body(r):
        rows = pl.ds(r, ROWS)
        centre, lap = own_laplace(pad, r)
        for z in range(depth):
            c, l = centre[z][:, :width_y], lap[z][:, :width_y]
            out[z, rows, :] = 2.0 * c - previous[z, rows, :] + velocity[z, rows, :] * l

    row_loop(width_x, body)
    inject(1, got, velocity, out)

    def body_image(r):
        rows = pl.ds(r, ROWS)
        for z in range(depth):
            image[z, rows, :] = (
                forward[0, z, rows, :] * current[z, rows, :]
                + forward[1, z, rows, :] * out[z, rows, :]
            )

    row_loop(width_x, body_image)


def last_kernel(partial, image_in, velocity, forward, got_on, got_off, out, image):
    depth, width_x, width_y = out.shape

    def body(r):
        rows = pl.ds(r, ROWS)
        halo = halo_sum(got_on, got_off, rows, width_y, depth)
        for j in range(depth):
            z = depth_at(j, depth)
            extra = velocity[z, rows, :] * halo[j] if halo[j] is not None else 0.0
            out[z, rows, :] = partial[z, rows, :] + extra
            image[z, rows, :] = image_in[z, rows, :] + forward[1, z, rows, :] * extra

    row_loop(width_x, body)


def on_device(now, prior, velocity, forward, traces, weights, target, cell):
    slabs = lax.axis_size("slab")
    depth, width_x, width_y = now.shape
    rows = traces.shape[0]
    lanes = -(-(width_y + HALO) // LANES) * LANES
    field = jax.ShapeDtypeStruct(now.shape, F32)
    face = jax.ShapeDtypeStruct((width_x, payload_lanes(width_y)), BF16)
    pad = pltpu.VMEM((depth, width_x + 16, lanes), F32)
    on_pairs = [(i, j) for i, j in ((k, k ^ 1) for k in range(slabs)) if j < slabs]
    off_pairs = [(i + 1, j + 1) for i, j in ((k, k ^ 1) for k in range(slabs)) if i + 1 < slabs and j + 1 < slabs]

    def call(kernel, ins, outs, scratch=(), **kw):
        return pl.pallas_call(
            kernel,
            in_specs=ins,
            out_specs=[VMEM] * len(outs),
            out_shape=outs,
            scratch_shapes=scratch,
            compiler_params=params(),
            **kw,
        )

    def swap(on_face, off_face):
        off = lax.ppermute(off_face, "slab", off_pairs)
        on = lax.ppermute(on_face, "slab", on_pairs)
        return on, off

    on_face, off_face = call(pack_kernel, [VMEM], [face, face])(now)
    (sent,) = call(
        functools.partial(route_kernel, slabs, width_y),
        [VMEM] * 4,
        [jax.ShapeDtypeStruct((slabs, 1, LANES), F32)],
    )(traces, weights, target.reshape(1, rows), cell.reshape(1, rows))
    got_on, got_off = swap(on_face, off_face)
    got = lax.all_to_all(sent, "slab", split_axis=0, concat_axis=0, tiled=True)
    (partial,) = call(own_kernel, [VMEM] * 3, [field], (pad,))(now, prior, velocity)
    (partial,) = call(
        functools.partial(inject_kernel, 0),
        [SMEM, VMEM, VMEM],
        [field],
        input_output_aliases={2: 0},
    )(got, velocity, partial)
    first, on_face, off_face = call(close_kernel, [VMEM] * 4, [field, face, face])(
        partial, velocity, got_on, got_off
    )
    got_on, got_off = swap(on_face, off_face)
    partial, image = call(second_kernel, [SMEM] + [VMEM] * 4, [field, field], (pad,))(
        got, first, now, velocity, forward
    )
    second, image = call(last_kernel, [VMEM] * 6, [field, field])(
        partial, image, velocity, forward, got_on, got_off
    )
    return (image, second, first)


def solution(mesh):
    split = P(("groups", "slab"), None, None)
    return jax.shard_map(
        on_device,
        mesh=mesh,
        in_specs=(
            split,
            split,
            split,
            P(None, ("groups", "slab"), None, None),
            P(("groups", "slab"), None),
            P(),
            P(("groups", "slab"), None),
            P(("groups", "slab")),
        ),
        out_specs=(split, split, split),
        check_vma=False,
    )
```

time: 169 us -> 67.8 us (0.40)
  other arithmetic: 54.7 us -> 0 us
  waiting for transfers between devices: 62.5 us -> 12.2 us
  Pallas kernels: 0 us -> 28.5 us
  starting transfers between devices: 23.4 us -> 12.2 us
  local copies, waits for them, and re-layouts: 24.8 us -> 13.7 us
    add x2 -> x0, other arithmetic: 37 us -> none  [the longest x1 25.9 us: on_device(): 2.0 * current - previous + velocity_term * (laplace(extended) + inject)]
    pallas_call x0 -> x7, Pallas kernels: none -> 28.5 us  [the longest x1 7.7 us: on_device(): call(second_kernel, [SMEM] + [VMEM] * 4, [field, field], (pad,))]
    ppermute x4, waiting for transfers between devices: 36.7 us -> 10.6 us  [the longest x2 10.6 us: swap(): off = lax.ppermute(off_face, 'slab', off_pairs)]
    all_to_all x2 -> x1, waiting for transfers between devices: 25.8 us -> 1.58 us  [on_device(): got = lax.all_to_all(sent, 'slab', split_axis=0, concat_axis=0, tiled=True)]
    concatenate x3 -> x0, other arithmetic: 11.9 us -> none  [the longest x2 11.2 us: with_halo(): x = jnp.concatenate([before, x, after], axis=dim)]
    scatter x3 -> x0, local copies, waits for them, and re-layouts: 10.1 us -> none  [the longest x1 5.75 us: on_device(): jnp.zeros((slab_count, CAP), jnp.int32).at[target, slot_rank]]
    unnamed x14 -> x30, local copies, waits for them, and re-layouts: 5.42 us -> 13.7 us
    all_to_all x2 -> x1, starting transfers between devices: 12 us -> 5.39 us  [on_device(): got = lax.all_to_all(sent, 'slab', split_axis=0, concat_axis=0, tiled=True)]
  transfers between devices with their start and end apart: 6 -> 5, of which waited for: 3 -> 2; matrix products, arithmetic and copies ran while one was open for 17% -> 0% of each run, Pallas kernels for 0% -> 24%
where the time goes in v1:
time: 67.8 us; the launch traced here: 67.4 us
  Pallas kernels  28.5 us (42%)
  local copies, waits for them, and re-layouts  13.7 us (20%)
  starting transfers between devices  12.2 us (18%)
  waiting for transfers between devices  12.2 us (18%)
  between operations  0.78 us (1%)
    unnamed x30, local copies, waits for them, and re-layouts  13.7 us
    ppermute x2, waiting for transfers between devices, swap(): off = lax.ppermute(off_face, 'slab', off_pairs)  10.6 us
    pallas_call x1, Pallas kernels, on_device(): call(second_kernel, [SMEM] + [VMEM] * 4, [field, field], (pad,))  7.7 us
    pallas_call x1, Pallas kernels, on_device(): call(own_kernel, [VMEM] * 3, [field], (pad,))(now, prior, velocity)  5.8 us
    pallas_call x1, Pallas kernels, on_device(): call(close_kernel, [VMEM] * 4, [field, face, face])  5.63 us
    ppermute x2, starting transfers between devices, swap(): off = lax.ppermute(off_face, 'slab', off_pairs)  5.58 us
    all_to_all x1, starting transfers between devices, on_device(): got = lax.all_to_all(sent, 'slab', split_axis=0, concat_axis=0, tiled=True)  5.39 us
    pallas_call x1, Pallas kernels, on_device(): call(last_kernel, [VMEM] * 6, [field, field])  3.91 us
  transfers between devices with their start and end apart: 5, of which 2 were waited for; matrix products, arithmetic and copies ran while one was open for 0% of the time, Pallas kernels for 24%

profile of v1, /device:TPU:9, one launch (start us, length us, event | category | flops | bytes accessed | tf_op | source)
XLA Modules:
  0.0 67.4 jit_solution(17214664605080450668)
XLA Ops:
  0.6 0.0 copy-start
  0.6 0.0 copy-start.1
  0.7 1.7 %copy-done.1 = f32[4,320,320]{2,1,0:T(8,128)S(1)} copy-done((f32[4,320,320]{2,1,0:T(8,128)S(1)}, f32[4,320,320]{2,1,0:T(8,128)}, u32[]{:S(2)}) %copy-start.1) | copy-done | bytes 1638424
  2.3 0.0 copy-start.13
  2.3 0.0 copy-start.14
  2.3 3.1 %shard_map.106 = (bf16[320,1280]{1,0:T(8,128)(2,1)}, bf16[320,1280]{1,0:T(8,128)(2,1)}) custom-call(f32[4,320,320]{2,1,0:T(8,128)S(1)} %copy-done.1), custom_call_target="tpu_custom_call" | custom-call | tf_op jit(solution)/shard_map/pallas_call | solution.py:327
  5.5 0.7 %collective-permute-start = (bf16[320,1280]{1,0:T(8,128)(2,1)}, bf16[320,1280]{1,0:T(8,128)(2,1)S(1)}, u32[]{:S(2)}, u32[]{:S(2)}) collective-permute-start(bf16[320,1280]{1,0:T(8,128)(2,1)} %get-tuple-element.12), channel_id=1, source_target_pairs={{0,1},{1,0},{2,3},{3,2},{4,5},{5,4},{6,7},{7,6},{8,9},{9,8},{10,11... | collective-permute-start | bytes 2457608 | tf_op jit(solution)/shard_map/ppermute | solution.py:324
  6.1 3.0 %collective-permute-start.1 = (bf16[320,1280]{1,0:T(8,128)(2,1)}, bf16[320,1280]{1,0:T(8,128)(2,1)}, u32[]{:S(2)}, u32[]{:S(2)}) collective-permute-start(bf16[320,1280]{1,0:T(8,128)(2,1)} %get-tuple-element.13), channel_id=1, source_target_pairs={{1,2},{2,1},{3,4},{4,3},{5,6},{6,5},{7,8},{8,7},{9,10},{10,9},{11,... | collective-permute-start | bytes 2457608 | tf_op jit(solution)/shard_map/ppermute | solution.py:323
  9.2 0.0 copy-done.13
  9.2 0.0 copy-done.14
  9.2 0.0 copy-start.11
  9.2 0.9 %copy-done.11 = bf16[64,2048]{1,0:T(8,128)(2,1)S(1)} copy-done((bf16[64,2048]{1,0:T(8,128)(2,1)S(1)}, bf16[64,2048]{1,0:T(8,128)(2,1)}, u32[]{:S(2)}) %copy-start.11) | copy-done | bytes 262168
  10.2 0.0 copy-start.12
  10.2 0.7 %copy-done.12 = bf16[2,2048]{1,0:T(2,128)(2,1)S(1)} copy-done((bf16[2,2048]{1,0:T(2,128)(2,1)S(1)}, bf16[2,2048]{1,0:T(2,128)(2,1)}, u32[]{:S(2)}) %copy-start.12) | copy-done | bytes 8216
  10.9 1.0 %shard_map.103 = f32[16,1,128]{2,1,0:T(1,128)} custom-call(bf16[64,2048]{1,0:T(8,128)(2,1)S(1)} %copy-done.11, bf16[2,2048]{1,0:T(2,128)(2,1)S(1)} %copy-done.12, s32[1,64]{1,0:T(1,128)S(1)} %bitcast.2, s32[1,64]{1,0:T(1,128)S(1)} %bitcast.3), custom_call_target="tpu_custom_call" | custom-call | tf_op jit(solution)/shard_map/pallas_call | solution.py:328
  11.8 5.4 %all-to-all-start = ((f32[16,1,128]{2,1,0:T(1,128)}), f32[16,1,128]{2,1,0:T(1,128)S(1)}, u32[]{:S(2)}, u32[]{:S(2)}) async-start(f32[16,1,128]{2,1,0:T(1,128)} %shard_map.103), calls=%async_computation | async-start | bytes 16384 | tf_op jit(solution)/shard_map/all_to_all | solution.py:334
  17.2 0.0 copy-done
  17.2 0.0 copy-start.2
  17.2 1.5 %copy-done.2 = f32[4,320,320]{2,1,0:T(8,128)S(1)} copy-done((f32[4,320,320]{2,1,0:T(8,128)S(1)}, f32[4,320,320]{2,1,0:T(8,128)}, u32[]{:S(2)}) %copy-start.2) | copy-done | bytes 1638424
  18.8 0.0 copy-start.10
  18.8 1.5 %copy-done.10 = f32[4,320,320]{2,1,0:T(8,128)S(1)} copy-done((f32[4,320,320]{2,1,0:T(8,128)S(1)}, f32[4,320,320]{2,1,0:T(8,128)}, u32[]{:S(2)}) %copy-start.10) | copy-done | bytes 1638424
  20.3 5.8 %shard_map.104.grid_in = f32[4,320,320]{2,1,0:T(8,128)S(1)} custom-call(f32[4,320,320]{2,1,0:T(8,128)S(1)} %copy-done.2, f32[4,320,320]{2,1,0:T(8,128)S(1)} %copy-done.10, f32[4,320,320]{2,1,0:T(8,128)S(1)} %copy-done), custom_call_target="tpu_custom_call" | custom-call | tf_op jit(solution)/shard_map/pallas_call | solution.py:335
  26.1 0.0 copy-start.4
  26.1 1.3 %copy-done.4 = f32[4,320,320]{2,1,0:T(8,128)} copy-done((f32[4,320,320]{2,1,0:T(8,128)}, f32[4,320,320]{2,1,0:T(8,128)S(1)}, u32[]{:S(2)}) %copy-start.4) | copy-done | bytes 1638424
  27.4 1.6 %all-to-all-done.got = f32[16,1,128]{2,1,0:T(1,128)S(1)} async-done(((f32[16,1,128]{2,1,0:T(1,128)}), f32[16,1,128]{2,1,0:T(1,128)S(1)}, u32[]{:S(2)}, u32[]{:S(2)}) %all-to-all-start) | async-done | bytes 8224 | tf_op jit(solution)/shard_map/all_to_all | solution.py:334
  29.0 0.0 copy-start.5
  29.0 1.5 %copy-done.5 = f32[4,320,320]{2,1,0:T(8,128)S(1)} copy-done((f32[4,320,320]{2,1,0:T(8,128)S(1)}, f32[4,320,320]{2,1,0:T(8,128)}, u32[]{:S(2)}) %copy-start.5) | copy-done | bytes 1638424
  30.5 0.0 copy-start.8
  30.5 1.4 %shard_map.105.partial = f32[4,320,320]{2,1,0:T(8,128)S(1)} custom-call(f32[16,1,128]{2,1,0:T(1,128)S(1)} %all-to-all-done.got, f32[4,320,320]{2,1,0:T(8,128)S(1)} %copy-done, f32[4,320,320]{2,1,0:T(8,128)S(1)} %copy-done.5), custom_call_target="tpu_custom_call", output_to_operand_aliasing={{}: (2, {})} | custom-call | tf_op jit(solution)/shard_map/pallas_call | solution.py:336
  31.9 0.0 copy-start.6
  31.9 1.3 %copy-done.6 = f32[4,320,320]{2,1,0:T(8,128)} copy-done((f32[4,320,320]{2,1,0:T(8,128)}, f32[4,320,320]{2,1,0:T(8,128)S(1)}, u32[]{:S(2)}) %copy-start.6) | copy-done | bytes 1638424
  33.2 0.0 copy-start.3
  33.2 0.0 collective-permute-done.got_on
  33.2 0.0 collective-permute-done.1.got_off
  33.2 0.0 copy-start.7
  33.2 1.7 %copy-done.7 = f32[4,320,320]{2,1,0:T(8,128)S(1)} copy-done((f32[4,320,320]{2,1,0:T(8,128)S(1)}, f32[4,320,320]{2,1,0:T(8,128)}, u32[]{:S(2)}) %copy-start.7) | copy-done | bytes 1638424
  34.9 5.6 %shard_map.107 = (f32[4,320,320]{2,1,0:T(8,128)}, bf16[320,1280]{1,0:T(8,128)(2,1)S(1)}, bf16[320,1280]{1,0:T(8,128)(2,1)S(1)}) custom-call(f32[4,320,320]{2,1,0:T(8,128)S(1)} %copy-done.7, f32[4,320,320]{2,1,0:T(8,128)S(1)} %copy-done, bf16[320,1280]{1,0:T(8,128)(2,1)S(1)} %collective-permute-done.got_on, bf16[320,1280]{1,0:T(8,128)(2,1)} %collective-permute-done.1.got_off), custom_call_target="tpu_custom_call" | custom-call | tf_op jit(solution)/shard_map/pallas_call | solution.py:342
  40.5 0.6 collective-permute-start.2
  41.1 2.5 %collective-permute-start.3 = (bf16[320,1280]{1,0:T(8,128)(2,1)S(1)}, bf16[320,1280]{1,0:T(8,128)(2,1)S(1)}, u32[]{:S(2)}, u32[]{:S(2)}) collective-permute-start(bf16[320,1280]{1,0:T(8,128)(2,1)S(1)} %get-tuple-element.18), channel_id=1, source_target_pairs={{1,2},{2,1},{3,4},{4,3},{5,6},{6,5},{7,8},{8,7},{9,10},{10,9},{11,... | collective-permute-start | bytes 2457608 | tf_op jit(solution)/shard_map/ppermute | solution.py:323
  43.7 0.0 copy-done.8
  43.7 0.0 copy-done.3
  43.7 0.0 copy-start.9
  43.7 1.5 %copy-done.9 = f32[4,320,320]{2,1,0:T(8,128)S(1)} copy-done((f32[4,320,320]{2,1,0:T(8,128)S(1)}, f32[4,320,320]{2,1,0:T(8,128)}, u32[]{:S(2)}) %copy-start.9) | copy-done | bytes 1638424
  45.2 7.7 %shard_map.108 = (f32[4,320,320]{2,1,0:T(8,128)S(1)}, f32[4,320,320]{2,1,0:T(8,128)S(1)}) custom-call(f32[16,1,128]{2,1,0:T(1,128)S(1)} %all-to-all-done.got, f32[4,320,320]{2,1,0:T(8,128)S(1)} %copy-done.9, f32[4,320,320]{2,1,0:T(8,128)S(1)} %copy-done.3, f32[4,320,320]{2,1,0:T(8,128)S(1)} %copy-done, f32[2,4,320,320]{3,2,1,0:T(8,128)S(1)} %copy-done.8), custom_call_target="tpu_custom_call" | custom-call | tf_op jit(solution)/shard_map/pallas_call | solution.py:346
  52.9 0.0 collective-permute-done.2.got_on
  52.9 10.6 %collective-permute-done.3.got_off = bf16[320,1280]{1,0:T(8,128)(2,1)S(1)} collective-permute-done((bf16[320,1280]{1,0:T(8,128)(2,1)S(1)}, bf16[320,1280]{1,0:T(8,128)(2,1)S(1)}, u32[]{:S(2)}, u32[]{:S(2)}) %collective-permute-start.3) | collective-permute-done | bytes 819232 | tf_op jit(solution)/shard_map/ppermute | solution.py:323
  63.5 3.9 %shard_map.109 = (f32[4,320,320]{2,1,0:T(8,128)}, f32[4,320,320]{2,1,0:T(8,128)}) custom-call(f32[4,320,320]{2,1,0:T(8,128)S(1)} %get-tuple-element.15.partial, f32[4,320,320]{2,1,0:T(8,128)S(1)} %get-tuple-element.16.image_in, f32[4,320,320]{2,1,0:T(8,128)S(1)} %copy-done, f32[2,4,320,320]{3,2,1,0:T(8,128)S(1)} %copy-done.8, ...), custom_call_target="tpu_custom_call" | custom-call | tf_op jit(solution)/shard_map/pallas_call | solution.py:349
Async XLA Ops:
  0.6 16.6 %copy-start = (f32[4,320,320]{2,1,0:T(8,128)S(1)}, f32[4,320,320]{2,1,0:T(8,128)}, u32[]{:S(2)}) copy-start(f32[4,320,320]{2,1,0:T(8,128)} %velocity.9) | copy-start | bytes 4915204
  0.6 1.7 %copy-start.1 = (f32[4,320,320]{2,1,0:T(8,128)S(1)}, f32[4,320,320]{2,1,0:T(8,128)}, u32[]{:S(2)}) copy-start(f32[4,320,320]{2,1,0:T(8,128)} %previous.1) | copy-start | bytes 4915204
  2.3 6.9 %copy-start.13 = (s32[64,1]{0,1:T(1,128)S(1)}, s32[64,1]{0,1:T(1,128)}, u32[]{:S(2)}) copy-start(s32[64,1]{0,1:T(1,128)} %param.14) | copy-start | bytes 772
  2.3 6.9 %copy-start.14 = (s32[64]{0:T(128)S(1)}, s32[64]{0:T(128)}, u32[]{:S(2)}) copy-start(s32[64]{0:T(128)} %param.15) | copy-start | bytes 772
  5.5 27.7 %collective-permute-start = (bf16[320,1280]{1,0:T(8,128)(2,1)}, bf16[320,1280]{1,0:T(8,128)(2,1)S(1)}, u32[]{:S(2)}, u32[]{:S(2)}) collective-permute-start(bf16[320,1280]{1,0:T(8,128)(2,1)} %get-tuple-element.12), channel_id=1, source_target_pairs={{0,1},{1,0},{2,3},{3,2},{4,5},{5,4},{6,7},{7,6},{8,9},{9,8},{10,11... | collective-permute-start | bytes 2457608 | tf_op jit(solution)/shard_map/ppermute | solution.py:324
  6.1 27.1 %collective-permute-start.1 = (bf16[320,1280]{1,0:T(8,128)(2,1)}, bf16[320,1280]{1,0:T(8,128)(2,1)}, u32[]{:S(2)}, u32[]{:S(2)}) collective-permute-start(bf16[320,1280]{1,0:T(8,128)(2,1)} %get-tuple-element.13), channel_id=1, source_target_pairs={{1,2},{2,1},{3,4},{4,3},{5,6},{6,5},{7,8},{8,7},{9,10},{10,9},{11,... | collective-permute-start | bytes 2457608 | tf_op jit(solution)/shard_map/ppermute | solution.py:323
  9.2 1.0 %copy-start.11 = (bf16[64,2048]{1,0:T(8,128)(2,1)S(1)}, bf16[64,2048]{1,0:T(8,128)(2,1)}, u32[]{:S(2)}) copy-start(bf16[64,2048]{1,0:T(8,128)(2,1)} %traces.1) | copy-start | bytes 786436
  10.2 0.7 %copy-start.12 = (bf16[2,2048]{1,0:T(2,128)(2,1)S(1)}, bf16[2,2048]{1,0:T(2,128)(2,1)}, u32[]{:S(2)}) copy-start(bf16[2,2048]{1,0:T(2,128)(2,1)} %weights.1) | copy-start | bytes 24580
  11.8 17.2 %all-to-all-start = ((f32[16,1,128]{2,1,0:T(1,128)}), f32[16,1,128]{2,1,0:T(1,128)S(1)}, u32[]{:S(2)}, u32[]{:S(2)}) async-start(f32[16,1,128]{2,1,0:T(1,128)} %shard_map.103), calls=%async_computation | async-start | bytes 16384 | tf_op jit(solution)/shard_map/all_to_all | solution.py:334
  17.2 1.5 %copy-start.2 = (f32[4,320,320]{2,1,0:T(8,128)S(1)}, f32[4,320,320]{2,1,0:T(8,128)}, u32[]{:S(2)}) copy-start(f32[4,320,320]{2,1,0:T(8,128)} %previous.1) | copy-start | bytes 4915204
  18.8 1.5 %copy-start.10 = (f32[4,320,320]{2,1,0:T(8,128)S(1)}, f32[4,320,320]{2,1,0:T(8,128)}, u32[]{:S(2)}) copy-start(f32[4,320,320]{2,1,0:T(8,128)} %prior.1) | copy-start | bytes 4915204
  26.1 1.3 %copy-start.4 = (f32[4,320,320]{2,1,0:T(8,128)}, f32[4,320,320]{2,1,0:T(8,128)S(1)}, u32[]{:S(2)}) copy-start(f32[4,320,320]{2,1,0:T(8,128)S(1)} %shard_map.104.grid_in) | copy-start | bytes 4915204
  29.0 1.5 %copy-start.5 = (f32[4,320,320]{2,1,0:T(8,128)S(1)}, f32[4,320,320]{2,1,0:T(8,128)}, u32[]{:S(2)}) copy-start(f32[4,320,320]{2,1,0:T(8,128)} %copy-done.4) | copy-start | bytes 4915204
  30.5 13.2 %copy-start.8 = (f32[2,4,320,320]{3,2,1,0:T(8,128)S(1)}, f32[2,4,320,320]{3,2,1,0:T(8,128)}, u32[]{:S(2)}) copy-start(f32[2,4,320,320]{3,2,1,0:T(8,128)} %forward.3) | copy-start | bytes 9830404
  31.9 1.3 %copy-start.6 = (f32[4,320,320]{2,1,0:T(8,128)}, f32[4,320,320]{2,1,0:T(8,128)S(1)}, u32[]{:S(2)}) copy-start(f32[4,320,320]{2,1,0:T(8,128)S(1)} %shard_map.105.partial) | copy-start | bytes 4915204
  33.2 10.5 %copy-start.3 = (f32[4,320,320]{2,1,0:T(8,128)S(1)}, f32[4,320,320]{2,1,0:T(8,128)}, u32[]{:S(2)}) copy-start(f32[4,320,320]{2,1,0:T(8,128)} %previous.1) | copy-start | bytes 4915204
  33.2 1.7 %copy-start.7 = (f32[4,320,320]{2,1,0:T(8,128)S(1)}, f32[4,320,320]{2,1,0:T(8,128)}, u32[]{:S(2)}) copy-start(f32[4,320,320]{2,1,0:T(8,128)} %copy-done.6) | copy-start | bytes 4915204
  40.5 12.4 %collective-permute-start.2 = (bf16[320,1280]{1,0:T(8,128)(2,1)S(1)}, bf16[320,1280]{1,0:T(8,128)(2,1)S(1)}, u32[]{:S(2)}, u32[]{:S(2)}) collective-permute-start(bf16[320,1280]{1,0:T(8,128)(2,1)S(1)} %get-tuple-element.17), channel_id=1, source_target_pairs={{0,1},{1,0},{2,3},{3,2},{4,5},{5,4},{6,7},{7,6},{8,9},{9,8},{10,11... | collective-permute-start | bytes 2457608 | tf_op jit(solution)/shard_map/ppermute | solution.py:324
  41.1 22.4 %collective-permute-start.3 = (bf16[320,1280]{1,0:T(8,128)(2,1)S(1)}, bf16[320,1280]{1,0:T(8,128)(2,1)S(1)}, u32[]{:S(2)}, u32[]{:S(2)}) collective-permute-start(bf16[320,1280]{1,0:T(8,128)(2,1)S(1)} %get-tuple-element.18), channel_id=1, source_target_pairs={{1,2},{2,1},{3,4},{4,3},{5,6},{6,5},{7,8},{8,7},{9,10},{10,9},{11,... | collective-permute-start | bytes 2457608 | tf_op jit(solution)/shard_map/ppermute | solution.py:323
  43.7 1.5 %copy-start.9 = (f32[4,320,320]{2,1,0:T(8,128)S(1)}, f32[4,320,320]{2,1,0:T(8,128)}, u32[]{:S(2)}) copy-start(f32[4,320,320]{2,1,0:T(8,128)} %get-tuple-element.11.current) | copy-start | bytes 4915204

commit v2 on v1

--- a/solution.py
+++ b/solution.py
@@ -7,20 +7,23 @@
 from jax.experimental.pallas import tpu as pltpu
 from jax.sharding import PartitionSpec as P
 
+
 CAP = 4
 STEPS = 2
 W = (-205.0 / 72.0, 8.0 / 5.0, -1.0 / 5.0, 8.0 / 315.0, -1.0 / 560.0)
 HALO = 4
 ROWS = 16
+BLOCK = 32
 LANES = 128
 F32 = jnp.float32
 BF16 = jnp.bfloat16
 VMEM = pl.BlockSpec(memory_space=pltpu.VMEM)
 SMEM = pl.BlockSpec(memory_space=pltpu.SMEM)
+HBM = pl.BlockSpec(memory_space=pltpu.HBM)
 
 
 def params():
-    return pltpu.CompilerParams(vmem_limit_bytes=24 << 20)
+    return pltpu.CompilerParams(vmem_limit_bytes=12 << 20)
 
 
 def payload_lanes(width):
@@ -88,13 +91,13 @@
     tails = []
     if rest * 2 <= LANES:
         half = LANES // 2
-        for k in range(0, HALO, 2):
+        for _ in range(0, HALO, 2):
             both = ref[rows, base : base + LANES].astype(F32)
             tails.append(both[:, :rest])
             tails.append(pltpu.roll(both, half, 1)[:, :rest])
             base += LANES
     else:
-        for k in range(HALO):
+        for _ in range(HALO):
             tails.append(ref[rows, base : base + LANES].astype(F32)[:, :rest])
             base += LANES
     return [jnp.concatenate([m, t], axis=1) for m, t in zip(main, tails)]
@@ -108,16 +111,38 @@
     lax.fori_loop(0, count // ROWS, step, 0)
 
 
-def pack_kernel(now, on_ref, off_ref):
-    depth, width_x, _ = now.shape
-
-    def body(r):
-        rows = pl.ds(r, ROWS)
-        u = [now[depth_at(j, depth), rows, :] for j in range(depth)]
-        put(off_ref, rows, encode(u[::-1][:HALO]))
-        put(on_ref, rows, encode(u[:HALO]))
-
-    row_loop(width_x, body)
+def fetch(source, buf, sems, first, count):
+    copies = []
+    for i in range(0, count, BLOCK):
+        rows = pl.ds(first + i, BLOCK)
+        copies.append(
+            pltpu.make_async_copy(source.at[:, rows], buf.at[:, pl.ds(i, BLOCK)], sems.at[i // BLOCK])
+        )
+        copies[-1].start()
+    return copies
+
+
+def pack_kernel(first, with_on, now, *refs):
+    refs = list(refs)
+    on_ref = refs.pop(0) if with_on else None
+    off_ref, buf, sems = refs
+    depth = now.shape[0]
+    base = 0 if with_on else first
+    copies = fetch(now, buf, sems, base, buf.shape[1])
+
+    for i, copy in enumerate(copies):
+        copy.wait()
+
+        def body(r):
+            r = r + i * BLOCK
+            rows = pl.ds(r, ROWS)
+            u = [buf[depth_at(j, depth), rows, :] for j in range(depth)]
+            if base + i * BLOCK >= first and base + i * BLOCK < first + off_ref.shape[0]:
+                put(off_ref, pl.ds(r + base - first, ROWS), encode(u[::-1][:HALO]))
+            if with_on:
+                put(on_ref, rows, encode(u[:HALO]))
+
+        row_loop(BLOCK, body)
 
 
 def route_kernel(slabs, width_y, traces, weights, target, cell, out):
@@ -151,19 +176,24 @@
     out[...] = picked.reshape(out.shape)
 
 
-def fill(pad, source):
-    depth, width_x, width_y = source.shape
-    lanes = pad.shape[2]
+def clear(pad, width_x):
+    depth, _, lanes = pad.shape
     for z in range(depth):
         pad[z, 0:8, :] = jnp.zeros((8, lanes), F32)
         pad[z, 8 + width_x : 16 + width_x, :] = jnp.zeros((8, lanes), F32)
 
+
+def fill(pad, first, source, start, count):
+    depth, _, width_y = source.shape
+    lanes = pad.shape[2]
+
     def body(r):
         for z in range(depth):
-            value = source[z, pl.ds(r, ROWS), :]
-            pad[z, pl.ds(r + 8, ROWS), :] = jnp.pad(value, ((0, 0), (0, lanes - width_y)))
-
-    row_loop(width_x, body)
+            value = source[z, pl.ds(r + start, ROWS), :]
+            value = jnp.pad(value, ((0, 0), (0, lanes - width_y)))
+            pad[z, pl.ds(r + (first + 8), ROWS), :] = value
+
+    row_loop(count, body)
 
 
 def own_laplace(pad, r):
@@ -189,7 +219,7 @@
 
 
 def inject(step, got, velocity, grid):
-    depth, width_x, width_y = grid.shape
+    _, width_x, width_y = grid.shape
     lane = lax.broadcasted_iota(jnp.int32, (1, width_y), 1)
 
     def body(i, carry):
@@ -206,28 +236,31 @@
     lax.fori_loop(0, got.shape[0], body, 0)
 
 
-def own_kernel(now, prior, velocity, out, pad):
+def own_kernel(now, prior, velocity, got, out, pad, now_buf, prior_buf, sems):
     depth, width_x, width_y = now.shape
-    fill(pad, now)
+    now_copies = fetch(now, now_buf, sems.at[0], 0, width_x)
+    prior_copies = fetch(prior, prior_buf, sems.at[1], 0, width_x)
+    clear(pad, width_x)
+    for i, copy in enumerate(now_copies):
+        copy.wait()
+        fill(pad, i * BLOCK, now_buf, i * BLOCK, BLOCK)
+    for copy in prior_copies:
+        copy.wait()
 
     def body(r):
         rows = pl.ds(r, ROWS)
         centre, lap = own_laplace(pad, r)
         for z in range(depth):
             c, l = centre[z][:, :width_y], lap[z][:, :width_y]
-            out[z, rows, :] = 2.0 * c - prior[z, rows, :] + velocity[z, rows, :] * l
+            out[z, rows, :] = 2.0 * c - prior_buf[z, rows, :] + velocity[z, rows, :] * l
 
     row_loop(width_x, body)
-
-
-def inject_kernel(step, got, velocity, grid_in, out):
-    del grid_in
-    inject(step, got, velocity, out)
-
-
-def halo_sum(got_on, got_off, rows, width_y, depth):
-    near = decode(take(got_on, rows, width_y))
-    far = decode(take(got_off, rows, width_y))
+    inject(0, got, velocity, out)
+
+
+def halo_sum(got_on, rows_on, got_off, rows_off, width_y, depth):
+    near = decode(take(got_on, rows_on, width_y))
+    far = decode(take(got_off, rows_off, width_y))
     out = []
     for j in range(depth):
         terms = [near[j]] if j < HALO else []
@@ -237,36 +270,51 @@
     return out
 
 
-def close_kernel(partial, velocity, got_on, got_off, out, on_ref, off_ref):
-    depth, width_x, width_y = out.shape
+def close_kernel(first, partial, velocity, got_on, got_off, out, on_ref, off_ref):
+    depth, count, width_y = out.shape
 
     def body(r):
         rows = pl.ds(r, ROWS)
-        halo = halo_sum(got_on, got_off, rows, width_y, depth)
+        whole = pl.ds(r + first, ROWS)
+        halo = halo_sum(got_on, whole, got_off, rows, width_y, depth)
         u = []
         for j in range(depth):
             z = depth_at(j, depth)
-            value = partial[z, rows, :]
+            value = partial[z, whole, :]
             if halo[j] is not None:
-                value = value + velocity[z, rows, :] * halo[j]
+                value = value + velocity[z, whole, :] * halo[j]
             out[z, rows, :] = value
             u.append(value)
         put(off_ref, rows, encode(u[::-1][:HALO]))
         put(on_ref, rows, encode(u[:HALO]))
 
-    row_loop(width_x, body)
-
-
-def second_kernel(got, current, previous, velocity, forward, out, image, pad):
-    depth, width_x, width_y = current.shape
-    fill(pad, current)
+    row_loop(count, body)
+
+
+def second_kernel(starts, *refs):
+    parts, refs = refs[: len(starts)], refs[len(starts) :]
+    now, velocity, forward, got, out, image, current, pad, now_buf, sems, out_sems = refs
+    depth, width_x, width_y = now.shape
+    copies = fetch(now, now_buf, sems, 0, width_x)
+    writes = []
+    for i, (first, part) in enumerate(zip(starts, parts)):
+        write = pltpu.make_async_copy(
+            part, current.at[:, pl.ds(first, part.shape[1])], out_sems.at[i]
+        )
+        write.start()
+        writes.append(write)
+    clear(pad, width_x)
+    for first, part in zip(starts, parts):
+        fill(pad, first, part, 0, part.shape[1])
+    for copy in copies:
+        copy.wait()
 
     def body(r):
         rows = pl.ds(r, ROWS)
         centre, lap = own_laplace(pad, r)
         for z in range(depth):
             c, l = centre[z][:, :width_y], lap[z][:, :width_y]
-            out[z, rows, :] = 2.0 * c - previous[z, rows, :] + velocity[z, rows, :] * l
+            out[z, rows, :] = 2.0 * c - now_buf[z, rows, :] + velocity[z, rows, :] * l
 
     row_loop(width_x, body)
     inject(1, got, velocity, out)
@@ -275,87 +323,146 @@
         rows = pl.ds(r, ROWS)
         for z in range(depth):
             image[z, rows, :] = (
-                forward[0, z, rows, :] * current[z, rows, :]
+                forward[0, z, rows, :] * pad[z, pl.ds(r + 8, ROWS), :][:, :width_y]
                 + forward[1, z, rows, :] * out[z, rows, :]
             )
 
     row_loop(width_x, body_image)
-
-
-def last_kernel(partial, image_in, velocity, forward, got_on, got_off, out, image):
-    depth, width_x, width_y = out.shape
-
-    def body(r):
-        rows = pl.ds(r, ROWS)
-        halo = halo_sum(got_on, got_off, rows, width_y, depth)
-        for j in range(depth):
-            z = depth_at(j, depth)
-            extra = velocity[z, rows, :] * halo[j] if halo[j] is not None else 0.0
-            out[z, rows, :] = partial[z, rows, :] + extra
-            image[z, rows, :] = image_in[z, rows, :] + forward[1, z, rows, :] * extra
-
-    row_loop(width_x, body)
-
-
-def on_device(now, prior, velocity, forward, traces, weights, target, cell):
+    for write in writes:
+        write.wait()
+
+
+def last_kernel(first, count, partial, image_in, velocity, forward, got_on, got_off, *refs):
+    out, image, out_buf, image_buf, sems = refs[-5:]
+    depth, width_y = out.shape[0], out.shape[2]
+    writes = []
+    for i in range(0, count, BLOCK):
+
+        def body(r):
+            rows = pl.ds(r + i, ROWS)
+            whole = pl.ds(r + (first + i), ROWS)
+            halo = halo_sum(got_on, rows, got_off, rows, width_y, depth)
+            for j in range(depth):
+                z = depth_at(j, depth)
+                extra = velocity[z, whole, :] * halo[j] if halo[j] is not None else 0.0
+                out_buf[z, rows, :] = partial[z, whole, :] + extra
+                image_buf[z, rows, :] = image_in[z, whole, :] + forward[1, z, whole, :] * extra
+
+        row_loop(BLOCK, body)
+        for k, (buf, target) in enumerate(((out_buf, out), (image_buf, image))):
+            write = pltpu.make_async_copy(
+                buf.at[:, pl.ds(i, BLOCK)],
+                target.at[:, pl.ds(first + i, BLOCK)],
+                sems.at[k, i // BLOCK],
+            )
+            write.start()
+            writes.append(write)
+    for write in writes:
+        write.wait()
+
+
+def shard(now, prior, velocity, forward, traces, weights, target, cell):
     slabs = lax.axis_size("slab")
     depth, width_x, width_y = now.shape
     rows = traces.shape[0]
     lanes = -(-(width_y + HALO) // LANES) * LANES
+    face_lanes = payload_lanes(width_y)
+    half = width_x // (2 * BLOCK) * BLOCK
+    chunks = ((0, half), (half, width_x - half))
+    starts = tuple(first for first, _ in chunks)
+    blocks = width_x // BLOCK
     field = jax.ShapeDtypeStruct(now.shape, F32)
-    face = jax.ShapeDtypeStruct((width_x, payload_lanes(width_y)), BF16)
     pad = pltpu.VMEM((depth, width_x + 16, lanes), F32)
-    on_pairs = [(i, j) for i, j in ((k, k ^ 1) for k in range(slabs)) if j < slabs]
-    off_pairs = [(i + 1, j + 1) for i, j in ((k, k ^ 1) for k in range(slabs)) if i + 1 < slabs and j + 1 < slabs]
-
-    def call(kernel, ins, outs, scratch=(), **kw):
+    dma = pltpu.SemaphoreType.DMA
+    on_pairs = [(k, k ^ 1) for k in range(slabs) if k ^ 1 < slabs]
+    off_pairs = [(i + 1, j + 1) for i, j in on_pairs if i + 1 < slabs and j + 1 < slabs]
+
+    def plane(count):
+        return jax.ShapeDtypeStruct((count, face_lanes), BF16)
+
+    def buffer(count):
+        return pltpu.VMEM((depth, count, width_y), F32)
+
+    def call(kernel, ins, outs, scratch=(), out_spec=None, **kw):
         return pl.pallas_call(
             kernel,
             in_specs=ins,
-            out_specs=[VMEM] * len(outs),
+            out_specs=out_spec or [VMEM] * len(outs),
             out_shape=outs,
             scratch_shapes=scratch,
             compiler_params=params(),
             **kw,
         )
 
-    def swap(on_face, off_face):
-        off = lax.ppermute(off_face, "slab", off_pairs)
-        on = lax.ppermute(on_face, "slab", on_pairs)
-        return on, off
-
-    on_face, off_face = call(pack_kernel, [VMEM], [face, face])(now)
+    def swap(face, pairs):
+        return lax.ppermute(face, "slab", pairs)
+
+    got_off = []
+    (face,) = call(
+        functools.partial(pack_kernel, 0, False),
+        [HBM],
+        [plane(half)],
+        (buffer(half), dma((half // BLOCK,))),
+    )(now)
+    got_off.append(swap(face, off_pairs))
+    face, traces = lax.optimization_barrier((face, traces))
     (sent,) = call(
         functools.partial(route_kernel, slabs, width_y),
         [VMEM] * 4,
         [jax.ShapeDtypeStruct((slabs, 1, LANES), F32)],
     )(traces, weights, target.reshape(1, rows), cell.reshape(1, rows))
-    got_on, got_off = swap(on_face, off_face)
     got = lax.all_to_all(sent, "slab", split_axis=0, concat_axis=0, tiled=True)
-    (partial,) = call(own_kernel, [VMEM] * 3, [field], (pad,))(now, prior, velocity)
+    sent, later = lax.optimization_barrier((sent, now))
+    on_face, face = call(
+        functools.partial(pack_kernel, half, True),
+        [HBM],
+        [plane(width_x), plane(width_x - half)],
+        (buffer(width_x), dma((blocks,))),
+    )(later)
+    got_off.append(swap(face, off_pairs))
+    got_on = swap(on_face, on_pairs)
     (partial,) = call(
-        functools.partial(inject_kernel, 0),
-        [SMEM, VMEM, VMEM],
+        own_kernel,
+        [HBM, HBM, VMEM, SMEM],
         [field],
-        input_output_aliases={2: 0},
-    )(got, velocity, partial)
-    first, on_face, off_face = call(close_kernel, [VMEM] * 4, [field, face, face])(
-        partial, velocity, got_on, got_off
-    )
-    got_on, got_off = swap(on_face, off_face)
-    partial, image = call(second_kernel, [SMEM] + [VMEM] * 4, [field, field], (pad,))(
-        got, first, now, velocity, forward
-    )
-    second, image = call(last_kernel, [VMEM] * 6, [field, field])(
-        partial, image, velocity, forward, got_on, got_off
-    )
-    return (image, second, first)
+        (pad, buffer(width_x), buffer(width_x), dma((2, blocks))),
+    )(now, prior, velocity, got)
+    parts, second_on, second_off = [], [], []
+    for (first, count), got_face in zip(chunks, got_off):
+        part, on_face, face = call(
+            functools.partial(close_kernel, first),
+            [VMEM] * 4,
+            [jax.ShapeDtypeStruct((depth, count, width_y), F32), plane(count), plane(count)],
+        )(partial, velocity, got_on, got_face)
+        second_off.append(swap(face, off_pairs))
+        second_on.append(swap(on_face, on_pairs))
+        parts.append(part)
+        part, partial = lax.optimization_barrier((part, partial))
+    partial, image, current = call(
+        functools.partial(second_kernel, starts),
+        [VMEM] * len(parts) + [HBM, VMEM, VMEM, SMEM],
+        [field, field, field],
+        (pad, buffer(width_x), dma((blocks,)), dma((len(parts),))),
+        [VMEM, VMEM, HBM],
+    )(*parts, now, velocity, forward, got)
+    done = ()
+    for i, (first, count) in enumerate(chunks):
+        done = call(
+            functools.partial(last_kernel, first, count),
+            [VMEM] * 6 + [HBM] * len(done),
+            [field, field],
+            (buffer(count), buffer(count), dma((2, count // BLOCK))),
+            [HBM, HBM],
+            input_output_aliases={6: 0, 7: 1} if done else {},
+        )(partial, image, velocity, forward, second_on[i], second_off[i], *done)
+    second, image = done
+    return (image, second, current)
 
 
 def solution(mesh):
     split = P(("groups", "slab"), None, None)
     return jax.shard_map(
-        on_device,
+        shard,
         mesh=mesh,
         in_specs=(
             split,

time: 67.8 us -> 67 us (0.988)
  blocking collectives: 0 us -> 17 us
  local copies, waits for them, and re-layouts: 13.7 us -> 3.25 us
  waiting for transfers between devices: 12.2 us -> 3.83 us
  starting transfers between devices: 12.2 us -> 13.8 us
    all_to_all x0 -> x1, blocking collectives: none -> 17 us  [shard(): got = lax.all_to_all(sent, 'slab', split_axis=0, concat_axis=0, tiled=True)]
    unnamed x30 -> x18, local copies, waits for them, and re-layouts: 13.7 us -> 3.25 us
    ppermute x4 -> x7, starting transfers between devices: 6.84 us -> 13.8 us  [swap(): return lax.ppermute(face, 'slab', pairs)]
    ppermute x4 -> x7, waiting for transfers between devices: 10.6 us -> 3.83 us  [swap(): return lax.ppermute(face, 'slab', pairs)]
    all_to_all x1 -> x0, starting transfers between devices: 5.39 us -> none  [on_device(): got = lax.all_to_all(sent, 'slab', split_axis=0, concat_axis=0, tiled=True)]
    all_to_all x1 -> x0, waiting for transfers between devices: 1.58 us -> none  [on_device(): got = lax.all_to_all(sent, 'slab', split_axis=0, concat_axis=0, tiled=True)]
    pallas_call x7 -> x9, Pallas kernels: 28.5 us -> 28.1 us  [the longest x1 8.69 us: shard(): call(own_kernel, [HBM, HBM, VMEM, SMEM], [field], (pad, buffer(width_x),...]
  transfers between devices with their start and end apart: 5 -> 7, of which waited for: 2 -> 2; matrix products, arithmetic and copies ran while one was open for 0% -> 0% of each run, Pallas kernels for 24% -> 33%
where the time goes in v2:
time: 67 us; the launch traced here: 66.8 us
  Pallas kernels  28.1 us (42%)
  blocking collectives  17 us (25%)
  starting transfers between devices  13.8 us (21%)
  waiting for transfers between devices  3.83 us (6%)
  local copies, waits for them, and re-layouts  3.25 us (5%)
  between operations  0.82 us (1%)
    all_to_all x1, blocking collectives, shard(): got = lax.all_to_all(sent, 'slab', split_axis=0, concat_axis=0, tiled=True)  17 us
    ppermute x7, starting transfers between devices, swap(): return lax.ppermute(face, 'slab', pairs)  13.8 us
    pallas_call x1, Pallas kernels, shard(): call(own_kernel, [HBM, HBM, VMEM, SMEM], [field], (pad, buffer(width_x),...  8.69 us
    pallas_call x1, Pallas kernels, shard(): call(functools.partial(second_kernel, starts), [VMEM] * len(parts) + [HBM...  8.49 us
    ppermute x7, waiting for transfers between devices, swap(): return lax.ppermute(face, 'slab', pairs)  3.83 us
    pallas_call x2, Pallas kernels, shard(): call(functools.partial(last_kernel, first, count), [VMEM] * 6 + [HBM] * l...  3.62 us
    unnamed x18, local copies, waits for them, and re-layouts  3.25 us
    pallas_call x2, Pallas kernels, shard(): call(functools.partial(close_kernel, first), [VMEM] * 4, [jax.ShapeDtypeS...  3.23 us
  transfers between devices with their start and end apart: 7, of which 2 were waited for; matrix products, arithmetic and copies ran while one was open for 0% of the time, Pallas kernels for 33%

profile of v2, /device:TPU:9, one launch (start us, length us, event | category | flops | bytes accessed | tf_op | source)
XLA Modules:
  0.0 66.8 jit_solution(17599021305335251386)
XLA Ops:
  0.6 0.0 copy-start
  0.6 0.0 copy-start.2
  0.7 1.7 %copy-done.2 = f32[4,320,320]{2,1,0:T(8,128)S(1)} copy-done((f32[4,320,320]{2,1,0:T(8,128)S(1)}, f32[4,320,320]{2,1,0:T(8,128)}, u32[]{:S(2)}) %copy-start.2) | copy-done | bytes 1638424
  2.3 0.0 copy-start.5
  2.3 0.0 copy-start.6
  2.3 0.0 copy-start.7
  2.3 0.0 copy-start.8
  2.3 1.2 %shard_map.103 = bf16[160,1280]{1,0:T(8,128)(2,1)S(1)} custom-call(f32[4,320,320]{2,1,0:T(8,128)S(1)} %copy-done.2), custom_call_target="tpu_custom_call" | custom-call | tf_op jit(solution)/shard_map/pallas_call | solution.py:401
  3.5 0.0 copy-done.5
  3.5 0.0 copy-done.6
  3.5 0.0 copy-done.7
  3.6 0.0 copy-done.8
  3.6 0.4 shard_map.104
  3.9 0.0 copy-start.3
  3.9 1.5 %copy-done.3 = f32[4,320,320]{2,1,0:T(8,128)S(1)} copy-done((f32[4,320,320]{2,1,0:T(8,128)S(1)}, f32[4,320,320]{2,1,0:T(8,128)}, u32[]{:S(2)}) %copy-start.3) | copy-done | bytes 1638424
  5.5 0.0 copy-start.4
  5.5 2.5 %shard_map.106 = (bf16[320,1280]{1,0:T(8,128)(2,1)S(1)}, bf16[160,1280]{1,0:T(8,128)(2,1)S(1)}) custom-call(f32[4,320,320]{2,1,0:T(8,128)S(1)} %copy-done.3), custom_call_target="tpu_custom_call" | custom-call | tf_op jit(solution)/shard_map/pallas_call | solution.py:416
  8.0 0.7 %collective-permute-start = (bf16[320,1280]{1,0:T(8,128)(2,1)S(1)}, bf16[320,1280]{1,0:T(8,128)(2,1)S(1)}, u32[]{:S(2)}, u32[]{:S(2)}) collective-permute-start(bf16[320,1280]{1,0:T(8,128)(2,1)S(1)} %get-tuple-element.23), channel_id=1, source_target_pairs={{0,1},{1,0},{2,3},{3,2},{4,5},{5,4},{6,7},{7,6},{8,9},{9,8},{10,11... | collective-permute-start | bytes 2457608 | tf_op jit(solution)/shard_map/ppermute | solution.py:398
  8.7 3.0 %collective-permute-start.1 = (bf16[160,1280]{1,0:T(8,128)(2,1)S(1)}, bf16[160,1280]{1,0:T(8,128)(2,1)S(1)}, u32[]{:S(2)}, u32[]{:S(2)}) collective-permute-start(bf16[160,1280]{1,0:T(8,128)(2,1)S(1)} %shard_map.103), channel_id=1, source_target_pairs={{1,2},{2,1},{3,4},{4,3},{5,6},{6,5},{7,8},{8,7},{9,10},{10,9},{11,... | collective-permute-start | bytes 1228808 | tf_op jit(solution)/shard_map/ppermute | solution.py:398
  11.8 2.5 %collective-permute-start.2 = (bf16[160,1280]{1,0:T(8,128)(2,1)S(1)}, bf16[160,1280]{1,0:T(8,128)(2,1)S(1)}, u32[]{:S(2)}, u32[]{:S(2)}) collective-permute-start(bf16[160,1280]{1,0:T(8,128)(2,1)S(1)} %get-tuple-element.26), channel_id=1, source_target_pairs={{1,2},{2,1},{3,4},{4,3},{5,6},{6,5},{7,8},{8,7},{9,10},{10,9},{11,... | collective-permute-start | bytes 1228808 | tf_op jit(solution)/shard_map/ppermute | solution.py:398
  14.3 17.0 %all_to_all.5.got.refs_5_ = f32[16,1,128]{2,1,0:T(1,128)S(1)} all-to-all(f32[16,1,128]{2,1,0:T(1,128)S(1)} %shard_map.104), channel_id=1, replica_groups=mesh['groups'=2,'slab'=16] {'slab'}, dimensions={0} | all-to-all | bytes 16384 | tf_op jit(solution)/shard_map/all_to_all | solution.py:414
  31.3 0.0 copy-done
  31.3 0.0 copy-done.4
  31.4 8.7 %shard_map.105.partial = f32[4,320,320]{2,1,0:T(8,128)S(1)} custom-call(f32[4,320,320]{2,1,0:T(8,128)S(1)} %copy-done.3, f32[4,320,320]{2,1,0:T(8,128)S(1)} %copy-done.4, f32[4,320,320]{2,1,0:T(8,128)S(1)} %copy-done, f32[16,1,128]{2,1,0:T(1,128)S(1)} %all_to_all.5.got.refs_5_), custom_call_target="tpu_custom_call" | custom-call | tf_op jit(solution)/shard_map/pallas_call | solution.py:424
  40.1 0.0 collective-permute-done.1.got_off
  40.1 0.0 collective-permute-done.got_on
  40.1 1.6 %shard_map.107 = (f32[4,160,320]{2,1,0:T(8,128)S(1)}, bf16[160,1280]{1,0:T(8,128)(2,1)S(1)}, bf16[160,1280]{1,0:T(8,128)(2,1)S(1)}) custom-call(f32[4,320,320]{2,1,0:T(8,128)S(1)} %shard_map.105.partial, f32[4,320,320]{2,1,0:T(8,128)S(1)} %copy-done, bf16[320,1280]{1,0:T(8,128)(2,1)S(1)} %collective-permute-done.got_on, ...), custom_call_target="tpu_custom_call" | custom-call | tf_op jit(solution)/shard_map/pallas_call | solution.py:432
  41.7 0.6 collective-permute-start.5
  42.3 0.0 copy-start.1
  42.3 2.7 %collective-permute-start.6 = (bf16[160,1280]{1,0:T(8,128)(2,1)S(1)}, bf16[160,1280]{1,0:T(8,128)(2,1)S(1)}, u32[]{:S(2)}, u32[]{:S(2)}) collective-permute-start(bf16[160,1280]{1,0:T(8,128)(2,1)S(1)} %get-tuple-element.33), channel_id=1, source_target_pairs={{1,2},{2,1},{3,4},{4,3},{5,6},{6,5},{7,8},{8,7},{9,10},{10,9},{11,... | collective-permute-start | bytes 1228808 | tf_op jit(solution)/shard_map/ppermute | solution.py:398
  45.1 0.0 collective-permute-done.2.got_off
  45.1 1.6 %shard_map.108 = (f32[4,160,320]{2,1,0:T(8,128)S(1)}, bf16[160,1280]{1,0:T(8,128)(2,1)S(1)}, bf16[160,1280]{1,0:T(8,128)(2,1)S(1)}) custom-call(f32[4,320,320]{2,1,0:T(8,128)S(1)} %shard_map.105.partial, f32[4,320,320]{2,1,0:T(8,128)S(1)} %copy-done, bf16[320,1280]{1,0:T(8,128)(2,1)S(1)} %collective-permute-done.got_on, ...), custom_call_target="tpu_custom_call" | custom-call | tf_op jit(solution)/shard_map/pallas_call | solution.py:432
  46.7 0.4 collective-permute-start.3
  47.1 3.8 %collective-permute-start.4 = (bf16[160,1280]{1,0:T(8,128)(2,1)S(1)}, bf16[160,1280]{1,0:T(8,128)(2,1)S(1)}, u32[]{:S(2)}, u32[]{:S(2)}) collective-permute-start(bf16[160,1280]{1,0:T(8,128)(2,1)S(1)} %get-tuple-element.31), channel_id=1, source_target_pairs={{1,2},{2,1},{3,4},{4,3},{5,6},{6,5},{7,8},{8,7},{9,10},{10,9},{11,... | collective-permute-start | bytes 1228808 | tf_op jit(solution)/shard_map/ppermute | solution.py:398
  50.8 0.0 copy-done.1
  50.8 8.5 %shard_map.109 = (f32[4,320,320]{2,1,0:T(8,128)S(1)}, f32[4,320,320]{2,1,0:T(8,128)S(1)}, f32[4,320,320]{2,1,0:T(8,128)}) custom-call(f32[4,160,320]{2,1,0:T(8,128)S(1)} %get-tuple-element.24.refs_0_, f32[4,160,320]{2,1,0:T(8,128)S(1)} %get-tuple-element.27.refs_1_, f32[4,320,320]{2,1,0:T(8,128)S(1)} %copy-done.3, f32[4,320,320]{2,1,0:T(8,128)S(1)} %copy-done, ...), custom_call_target="tpu_custom_call" | custom-call | tf_op jit(solution)/shard_map/pallas_call | solution.py:441
  59.3 0.0 collective-permute-done.5.got_on
  59.4 1.3 %collective-permute-done.6.got_off = bf16[160,1280]{1,0:T(8,128)(2,1)S(1)} collective-permute-done((bf16[160,1280]{1,0:T(8,128)(2,1)S(1)}, bf16[160,1280]{1,0:T(8,128)(2,1)S(1)}, u32[]{:S(2)}, u32[]{:S(2)}) %collective-permute-start.6) | collective-permute-done | bytes 409632 | tf_op jit(solution)/shard_map/ppermute | solution.py:398
  60.6 1.8 %shard_map.110 = (f32[4,320,320]{2,1,0:T(8,128)}, f32[4,320,320]{2,1,0:T(8,128)}) custom-call(f32[4,320,320]{2,1,0:T(8,128)S(1)} %get-tuple-element.28.partial, f32[4,320,320]{2,1,0:T(8,128)S(1)} %get-tuple-element.29.image_in, f32[4,320,320]{2,1,0:T(8,128)S(1)} %copy-done, f32[2,4,320,320]{3,2,1,0:T(8,128)S(1)} %copy-done.1, ...), custom_call_target="tpu_custom_call" | custom-call | tf_op jit(solution)/shard_map/pallas_call | solution.py:450
  62.4 0.0 collective-permute-done.3.got_on
  62.4 2.6 %collective-permute-done.4.got_off = bf16[160,1280]{1,0:T(8,128)(2,1)S(1)} collective-permute-done((bf16[160,1280]{1,0:T(8,128)(2,1)S(1)}, bf16[160,1280]{1,0:T(8,128)(2,1)S(1)}, u32[]{:S(2)}, u32[]{:S(2)}) %collective-permute-start.4) | collective-permute-done | bytes 409632 | tf_op jit(solution)/shard_map/ppermute | solution.py:398
  65.0 1.8 %shard_map.111 = (f32[4,320,320]{2,1,0:T(8,128)}, f32[4,320,320]{2,1,0:T(8,128)}) custom-call(f32[4,320,320]{2,1,0:T(8,128)S(1)} %get-tuple-element.28.partial, f32[4,320,320]{2,1,0:T(8,128)S(1)} %get-tuple-element.29.image_in, f32[4,320,320]{2,1,0:T(8,128)S(1)} %copy-done, ...), custom_call_target="tpu_custom_call", output_to_operand_aliasing={{0}: (6, {}), {1}: (7, {})} | custom-call | tf_op jit(solution)/shard_map/pallas_call | solution.py:450
Async XLA Ops:
  0.6 30.7 %copy-start = (f32[4,320,320]{2,1,0:T(8,128)S(1)}, f32[4,320,320]{2,1,0:T(8,128)}, u32[]{:S(2)}) copy-start(f32[4,320,320]{2,1,0:T(8,128)} %velocity.9) | copy-start | bytes 4915204
  0.6 1.7 %copy-start.2 = (f32[4,320,320]{2,1,0:T(8,128)S(1)}, f32[4,320,320]{2,1,0:T(8,128)}, u32[]{:S(2)}) copy-start(f32[4,320,320]{2,1,0:T(8,128)} %refs_2_.1) | copy-start | bytes 4915204
  2.3 1.2 %copy-start.5 = (bf16[64,2048]{1,0:T(8,128)(2,1)S(1)}, bf16[64,2048]{1,0:T(8,128)(2,1)}, u32[]{:S(2)}) copy-start(bf16[64,2048]{1,0:T(8,128)(2,1)} %traces) | copy-start | bytes 786436
  2.3 1.2 %copy-start.6 = (bf16[2,2048]{1,0:T(2,128)(2,1)S(1)}, bf16[2,2048]{1,0:T(2,128)(2,1)}, u32[]{:S(2)}) copy-start(bf16[2,2048]{1,0:T(2,128)(2,1)} %weights.1) | copy-start | bytes 24580
  2.3 1.2 %copy-start.7 = (s32[64,1]{0,1:T(1,128)S(1)}, s32[64,1]{0,1:T(1,128)}, u32[]{:S(2)}) copy-start(s32[64,1]{0,1:T(1,128)} %param.14) | copy-start | bytes 772
  2.3 1.2 %copy-start.8 = (s32[64]{0:T(128)S(1)}, s32[64]{0:T(128)}, u32[]{:S(2)}) copy-start(s32[64]{0:T(128)} %param.15) | copy-start | bytes 772
  3.9 1.6 %copy-start.3 = (f32[4,320,320]{2,1,0:T(8,128)S(1)}, f32[4,320,320]{2,1,0:T(8,128)}, u32[]{:S(2)}) copy-start(f32[4,320,320]{2,1,0:T(8,128)} %refs_2_.1) | copy-start | bytes 4915204
  5.5 25.9 %copy-start.4 = (f32[4,320,320]{2,1,0:T(8,128)S(1)}, f32[4,320,320]{2,1,0:T(8,128)}, u32[]{:S(2)}) copy-start(f32[4,320,320]{2,1,0:T(8,128)} %prior.1) | copy-start | bytes 4915204
  8.0 32.1 %collective-permute-start = (bf16[320,1280]{1,0:T(8,128)(2,1)S(1)}, bf16[320,1280]{1,0:T(8,128)(2,1)S(1)}, u32[]{:S(2)}, u32[]{:S(2)}) collective-permute-start(bf16[320,1280]{1,0:T(8,128)(2,1)S(1)} %get-tuple-element.23), channel_id=1, source_target_pairs={{0,1},{1,0},{2,3},{3,2},{4,5},{5,4},{6,7},{7,6},{8,9},{9,8},{10,11... | collective-permute-start | bytes 2457608 | tf_op jit(solution)/shard_map/ppermute | solution.py:398
  8.7 31.3 %collective-permute-start.1 = (bf16[160,1280]{1,0:T(8,128)(2,1)S(1)}, bf16[160,1280]{1,0:T(8,128)(2,1)S(1)}, u32[]{:S(2)}, u32[]{:S(2)}) collective-permute-start(bf16[160,1280]{1,0:T(8,128)(2,1)S(1)} %shard_map.103), channel_id=1, source_target_pairs={{1,2},{2,1},{3,4},{4,3},{5,6},{6,5},{7,8},{8,7},{9,10},{10,9},{11,... | collective-permute-start | bytes 1228808 | tf_op jit(solution)/shard_map/ppermute | solution.py:398
  11.8 33.3 %collective-permute-start.2 = (bf16[160,1280]{1,0:T(8,128)(2,1)S(1)}, bf16[160,1280]{1,0:T(8,128)(2,1)S(1)}, u32[]{:S(2)}, u32[]{:S(2)}) collective-permute-start(bf16[160,1280]{1,0:T(8,128)(2,1)S(1)} %get-tuple-element.26), channel_id=1, source_target_pairs={{1,2},{2,1},{3,4},{4,3},{5,6},{6,5},{7,8},{8,7},{9,10},{10,9},{11,... | collective-permute-start | bytes 1228808 | tf_op jit(solution)/shard_map/ppermute | solution.py:398
  41.7 17.7 %collective-permute-start.5 = (bf16[160,1280]{1,0:T(8,128)(2,1)S(1)}, bf16[160,1280]{1,0:T(8,128)(2,1)S(1)}, u32[]{:S(2)}, u32[]{:S(2)}) collective-permute-start(bf16[160,1280]{1,0:T(8,128)(2,1)S(1)} %get-tuple-element.32), channel_id=1, source_target_pairs={{0,1},{1,0},{2,3},{3,2},{4,5},{5,4},{6,7},{7,6},{8,9},{9,8},{10,11... | collective-permute-start | bytes 1228808 | tf_op jit(solution)/shard_map/ppermute | solution.py:398
  42.3 8.5 %copy-start.1 = (f32[2,4,320,320]{3,2,1,0:T(8,128)S(1)}, f32[2,4,320,320]{3,2,1,0:T(8,128)}, u32[]{:S(2)}) copy-start(f32[2,4,320,320]{3,2,1,0:T(8,128)} %forward.3) | copy-start | bytes 9830404
  42.3 18.3 %collective-permute-start.6 = (bf16[160,1280]{1,0:T(8,128)(2,1)S(1)}, bf16[160,1280]{1,0:T(8,128)(2,1)S(1)}, u32[]{:S(2)}, u32[]{:S(2)}) collective-permute-start(bf16[160,1280]{1,0:T(8,128)(2,1)S(1)} %get-tuple-element.33), channel_id=1, source_target_pairs={{1,2},{2,1},{3,4},{4,3},{5,6},{6,5},{7,8},{8,7},{9,10},{10,9},{11,... | collective-permute-start | bytes 1228808 | tf_op jit(solution)/shard_map/ppermute | solution.py:398
  46.7 15.7 %collective-permute-start.3 = (bf16[160,1280]{1,0:T(8,128)(2,1)S(1)}, bf16[160,1280]{1,0:T(8,128)(2,1)S(1)}, u32[]{:S(2)}, u32[]{:S(2)}) collective-permute-start(bf16[160,1280]{1,0:T(8,128)(2,1)S(1)} %get-tuple-element.30), channel_id=1, source_target_pairs={{0,1},{1,0},{2,3},{3,2},{4,5},{5,4},{6,7},{7,6},{8,9},{9,8},{10,11... | collective-permute-start | bytes 1228808 | tf_op jit(solution)/shard_map/ppermute | solution.py:398
  47.1 17.9 %collective-permute-start.4 = (bf16[160,1280]{1,0:T(8,128)(2,1)S(1)}, bf16[160,1280]{1,0:T(8,128)(2,1)S(1)}, u32[]{:S(2)}, u32[]{:S(2)}) collective-permute-start(bf16[160,1280]{1,0:T(8,128)(2,1)S(1)} %get-tuple-element.31), channel_id=1, source_target_pairs={{1,2},{2,1},{3,4},{4,3},{5,6},{6,5},{7,8},{8,7},{9,10},{10,9},{11,... | collective-permute-start | bytes 1228808 | tf_op jit(solution)/shard_map/ppermute | solution.py:398

commit v3 on v2

--- a/solution.py
+++ b/solution.py
@@ -14,6 +14,9 @@
 HALO = 4
 ROWS = 16
 BLOCK = 32
+EDGE = 8
+SUB = 8
+UNROLL = 4
 LANES = 128
 F32 = jnp.float32
 BF16 = jnp.bfloat16
@@ -23,7 +26,7 @@
 
 
 def params():
-    return pltpu.CompilerParams(vmem_limit_bytes=12 << 20)
+    return pltpu.CompilerParams(vmem_limit_bytes=16 << 20)
 
 
 def payload_lanes(width):
@@ -145,7 +148,7 @@
         row_loop(BLOCK, body)
 
 
-def route_kernel(slabs, width_y, traces, weights, target, cell, out):
+def route_kernel(slabs, lines, width_y, traces, weights, target, cell, out):
     rows = traces.shape[0]
     lane = lax.broadcasted_iota(jnp.int32, (rows, rows), 1)
     row = lax.broadcasted_iota(jnp.int32, (rows, rows), 0)
@@ -162,8 +165,10 @@
         for s in range(STEPS)
     ]
     cell_line = cell_col // width_y
-    columns.append(cell_line.astype(F32))
-    columns.append((cell_col - cell_line * width_y).astype(F32))
+    column = cell_col - cell_line * width_y
+    tile = column // LANES
+    columns.append((tile * lines + cell_line).astype(F32))
+    columns.append((column - tile * LANES).astype(F32))
     spot = lax.broadcasted_iota(jnp.int32, (rows, LANES), 1)
     spread = jnp.zeros((rows, LANES), F32)
     for j, column in enumerate(columns):
@@ -176,86 +181,120 @@
     out[...] = picked.reshape(out.shape)
 
 
-def clear(pad, width_x):
-    depth, _, lanes = pad.shape
-    for z in range(depth):
-        pad[z, 0:8, :] = jnp.zeros((8, lanes), F32)
-        pad[z, 8 + width_x : 16 + width_x, :] = jnp.zeros((8, lanes), F32)
-
-
-def fill(pad, first, source, start, count):
+def spread(tiles, source, first, start, count):
     depth, _, width_y = source.shape
-    lanes = pad.shape[2]
+    width_x = (tiles.shape[1] - 2 * EDGE) // depth
 
     def body(r):
         for z in range(depth):
-            value = source[z, pl.ds(r + start, ROWS), :]
-            value = jnp.pad(value, ((0, 0), (0, lanes - width_y)))
-            pad[z, pl.ds(r + (first + 8), ROWS), :] = value
+            into = pl.ds(r + (EDGE + z * width_x + first), ROWS)
+            for j in range(tiles.shape[0]):
+                lo, hi = j * LANES, min((j + 1) * LANES, width_y)
+                value = source[z, pl.ds(r + start, ROWS), lo:hi]
+                if hi - lo < LANES:
+                    value = jnp.pad(value, ((0, 0), (0, LANES - (hi - lo))))
+                tiles[j, into, :] = value
 
     row_loop(count, body)
 
 
-def own_laplace(pad, r):
-    depth = pad.shape[0]
-    span = ROWS + 16
-    blocks = [pad[z, pl.ds(r, span), :] for z in range(depth)]
-    centre = [block[8 : 8 + ROWS, :] for block in blocks]
-    lanes = pad.shape[2]
-    out = []
-    for z in range(depth):
-        total = 3.0 * W[0] * centre[z]
-        for k in range(1, HALO + 1):
-            pair = pltpu.roll(blocks[z], k, 0)[8 : 8 + ROWS, :]
-            pair = pair + pltpu.roll(blocks[z], span - k, 0)[8 : 8 + ROWS, :]
-            pair = pair + pltpu.roll(centre[z], k, 1) + pltpu.roll(centre[z], lanes - k, 1)
-            if z - k >= 0:
-                pair = pair + centre[z - k]
-            if z + k < depth:
-                pair = pair + centre[z + k]
-            total = total + W[k] * pair
-        out.append(total)
-    return centre, out
-
-
-def inject(step, got, velocity, grid):
-    _, width_x, width_y = grid.shape
-    lane = lax.broadcasted_iota(jnp.int32, (1, width_y), 1)
+def own_laplace(tiles, lap, depth, width_y):
+    count, _ = lap.shape
+    count = count // tiles.shape[0]
+    parts = SUB // depth
+    stride = count // SUB
+    number = tiles.shape[0]
+    shape = (SUB, LANES)
+    lane = lax.broadcasted_iota(jnp.int32, shape, 1)
+    sub = lax.broadcasted_iota(jnp.int32, shape, 0)
+    part = lax.rem(sub, parts)
+
+    def weight(k):
+        return W[k] if k <= HALO else 0.0
+
+    mixes = [jnp.where(sub >= d * parts, weight(d), weight(depth - d)) for d in range(1, depth)]
+
+    def rows_at(j, x):
+        return tiles[j, pl.ds(x + EDGE, SUB, stride=stride), :]
+
+    def one(x, low=None, high=None):
+        centre = [rows_at(j, x) for j in range(number)]
+        right = [[pltpu.roll(c, k, 1) for k in range(1, HALO + 1)] for c in centre]
+        left = [[pltpu.roll(c, LANES - k, 1) for k in range(1, HALO + 1)] for c in centre]
+        for j in range(number):
+            total = 3.0 * W[0] * centre[j]
+            for d in range(1, depth):
+                total = total + mixes[d - 1] * pltpu.roll(centre[j], d * parts, 0)
+            for k in range(1, HALO + 1):
+                before, after = rows_at(j, x - k), rows_at(j, x + k)
+                if low is not None and low < k:
+                    before = jnp.where(part == 0, 0.0, before)
+                if high is not None and high < k:
+                    after = jnp.where(part == parts - 1, 0.0, after)
+                side = right[j - 1][k - 1] if j else 0.0
+                pair = before + after + jnp.where(lane < k, side, right[j][k - 1])
+                if j + 1 < number:
+                    pair = pair + jnp.where(lane >= LANES - k, left[j + 1][k - 1], left[j][k - 1])
+                elif width_y % LANES > LANES - HALO or width_y % LANES == 0:
+                    pair = pair + jnp.where(lane >= LANES - k, 0.0, left[j][k - 1])
+                else:
+                    pair = pair + left[j][k - 1]
+                total = total + W[k] * pair
+            lap[pl.ds(x + j * count, SUB, stride=stride), :] = total
+
+    for x in range(HALO):
+        one(x, low=x)
+
+    def step(i, carry):
+        for u in range(UNROLL):
+            one(HALO + i * UNROLL + u)
+        return carry
+
+    steps = (stride - 2 * HALO) // UNROLL
+    lax.fori_loop(0, steps, step, 0)
+    for x in range(HALO + steps * UNROLL, stride):
+        one(x, high=stride - 1 - x)
+
+
+def inject(step, got, lap):
+    lane = lax.broadcasted_iota(jnp.int32, (1, LANES), 1)
 
     def body(i, carry):
         for slot in range(CAP):
             source = got[i, 0, step * CAP + slot]
-            line = got[i, 0, STEPS * CAP + slot].astype(jnp.int32)
-            column = got[i, 0, (STEPS + 1) * CAP + slot].astype(jnp.int32)
-            z = lax.div(line, jnp.int32(width_x))
-            row = pl.ds(line - z * width_x, 1)
-            extra = jnp.where(lane == column, velocity[z, row, :] * source, 0.0)
-            grid[z, row, :] = grid[z, row, :] + extra
+            row = pl.ds(got[i, 0, STEPS * CAP + slot].astype(jnp.int32), 1)
+            spot = got[i, 0, (STEPS + 1) * CAP + slot].astype(jnp.int32)
+            lap[row, :] = lap[row, :] + jnp.where(lane == spot, source, 0.0)
         return carry
 
     lax.fori_loop(0, got.shape[0], body, 0)
 
 
-def own_kernel(now, prior, velocity, got, out, pad, now_buf, prior_buf, sems):
+def tile_parts(width_y):
+    return [(lo, min(lo + LANES, width_y)) for lo in range(0, width_y, LANES)]
+
+
+def own_kernel(now, prior, velocity, got, out, tiles, lap, now_buf, prior_buf, sems):
     depth, width_x, width_y = now.shape
     now_copies = fetch(now, now_buf, sems.at[0], 0, width_x)
     prior_copies = fetch(prior, prior_buf, sems.at[1], 0, width_x)
-    clear(pad, width_x)
     for i, copy in enumerate(now_copies):
         copy.wait()
-        fill(pad, i * BLOCK, now_buf, i * BLOCK, BLOCK)
+        spread(tiles, now_buf, i * BLOCK, i * BLOCK, BLOCK)
+    own_laplace(tiles, lap, depth, width_y)
+    inject(0, got, lap)
     for copy in prior_copies:
         copy.wait()
 
     def body(r):
         rows = pl.ds(r, ROWS)
-        centre, lap = own_laplace(pad, r)
         for z in range(depth):
-            c, l = centre[z][:, :width_y], lap[z][:, :width_y]
-            out[z, rows, :] = 2.0 * c - prior_buf[z, rows, :] + velocity[z, rows, :] * l
+            for j, (lo, hi) in enumerate(tile_parts(width_y)):
+                change = lap[pl.ds(r + (j * depth + z) * width_x, ROWS), :][:, : hi - lo]
+                value = 2.0 * now_buf[z, rows, lo:hi] - prior_buf[z, rows, lo:hi]
+                out[z, rows, lo:hi] = value + velocity[z, rows, lo:hi] * change
 
     row_loop(width_x, body)
-    inject(0, got, velocity, out)
 
 
 def halo_sum(got_on, rows_on, got_off, rows_off, width_y, depth):
@@ -293,7 +332,7 @@
 
 def second_kernel(starts, *refs):
     parts, refs = refs[: len(starts)], refs[len(starts) :]
-    now, velocity, forward, got, out, image, current, pad, now_buf, sems, out_sems = refs
+    now, velocity, forward, got, out, image, current, tiles, lap, now_buf, sems, out_sems = refs
     depth, width_x, width_y = now.shape
     copies = fetch(now, now_buf, sems, 0, width_x)
     writes = []
@@ -303,31 +342,30 @@
         )
         write.start()
         writes.append(write)
-    clear(pad, width_x)
     for first, part in zip(starts, parts):
-        fill(pad, first, part, 0, part.shape[1])
+        spread(tiles, part, first, 0, part.shape[1])
+    own_laplace(tiles, lap, depth, width_y)
+    inject(1, got, lap)
     for copy in copies:
         copy.wait()
 
-    def body(r):
-        rows = pl.ds(r, ROWS)
-        centre, lap = own_laplace(pad, r)
-        for z in range(depth):
-            c, l = centre[z][:, :width_y], lap[z][:, :width_y]
-            out[z, rows, :] = 2.0 * c - now_buf[z, rows, :] + velocity[z, rows, :] * l
-
-    row_loop(width_x, body)
-    inject(1, got, velocity, out)
-
-    def body_image(r):
-        rows = pl.ds(r, ROWS)
-        for z in range(depth):
-            image[z, rows, :] = (
-                forward[0, z, rows, :] * pad[z, pl.ds(r + 8, ROWS), :][:, :width_y]
-                + forward[1, z, rows, :] * out[z, rows, :]
-            )
-
-    row_loop(width_x, body_image)
+    for first, part in zip(starts, parts):
+
+        def body(r):
+            rows = pl.ds(r, ROWS)
+            whole = pl.ds(r + first, ROWS)
+            for z in range(depth):
+                for j, (lo, hi) in enumerate(tile_parts(width_y)):
+                    change = lap[pl.ds(r + ((j * depth + z) * width_x + first), ROWS), :]
+                    here = part[z, rows, lo:hi]
+                    value = 2.0 * here - now_buf[z, whole, lo:hi]
+                    value = value + velocity[z, whole, lo:hi] * change[:, : hi - lo]
+                    out[z, whole, lo:hi] = value
+                    image[z, whole, lo:hi] = (
+                        forward[0, z, whole, lo:hi] * here + forward[1, z, whole, lo:hi] * value
+                    )
+
+        row_loop(part.shape[1], body)
     for write in writes:
         write.wait()
 
@@ -362,17 +400,20 @@
 
 
 def shard(now, prior, velocity, forward, traces, weights, target, cell):
+    now = pltpu.with_memory_space_constraint(now, pltpu.HBM)
+    prior = pltpu.with_memory_space_constraint(prior, pltpu.HBM)
     slabs = lax.axis_size("slab")
     depth, width_x, width_y = now.shape
     rows = traces.shape[0]
-    lanes = -(-(width_y + HALO) // LANES) * LANES
     face_lanes = payload_lanes(width_y)
     half = width_x // (2 * BLOCK) * BLOCK
     chunks = ((0, half), (half, width_x - half))
     starts = tuple(first for first, _ in chunks)
     blocks = width_x // BLOCK
     field = jax.ShapeDtypeStruct(now.shape, F32)
-    pad = pltpu.VMEM((depth, width_x + 16, lanes), F32)
+    number = -(-width_y // LANES)
+    tiles = pltpu.VMEM((number, depth * width_x + 2 * EDGE, LANES), F32)
+    lap = pltpu.VMEM((number * depth * width_x, LANES), F32)
     dma = pltpu.SemaphoreType.DMA
     on_pairs = [(k, k ^ 1) for k in range(slabs) if k ^ 1 < slabs]
     off_pairs = [(i + 1, j + 1) for i, j in on_pairs if i + 1 < slabs and j + 1 < slabs]
@@ -407,7 +448,7 @@
     got_off.append(swap(face, off_pairs))
     face, traces = lax.optimization_barrier((face, traces))
     (sent,) = call(
-        functools.partial(route_kernel, slabs, width_y),
+        functools.partial(route_kernel, slabs, depth * width_x, width_y),
         [VMEM] * 4,
         [jax.ShapeDtypeStruct((slabs, 1, LANES), F32)],
     )(traces, weights, target.reshape(1, rows), cell.reshape(1, rows))
@@ -425,7 +466,7 @@
         own_kernel,
         [HBM, HBM, VMEM, SMEM],
         [field],
-        (pad, buffer(width_x), buffer(width_x), dma((2, blocks))),
+        (tiles, lap, buffer(width_x), buffer(width_x), dma((2, blocks))),
     )(now, prior, velocity, got)
     parts, second_on, second_off = [], [], []
     for (first, count), got_face in zip(chunks, got_off):
@@ -442,7 +483,7 @@
         functools.partial(second_kernel, starts),
         [VMEM] * len(parts) + [HBM, VMEM, VMEM, SMEM],
         [field, field, field],
-        (pad, buffer(width_x), dma((blocks,)), dma((len(parts),))),
+        (tiles, lap, buffer(width_x), dma((blocks,)), dma((len(parts),))),
         [VMEM, VMEM, HBM],
     )(*parts, now, velocity, forward, got)
     done = ()

time: 67 us -> 70.5 us (1.052); the launches traced: 66.8 us -> 69.5 us
  Pallas kernels: 28.1 us -> 37.8 us
  waiting for transfers between devices: 3.83 us -> 0.02 us
  local copies, waits for them, and re-layouts: 3.25 us -> 0.02 us
    pallas_call x2, Pallas kernels: 9.05 us -> 13.8 us  [the longest x1 13.5 us: shard(): call(own_kernel, [HBM, HBM, VMEM, SMEM], [field], (tiles, lap, buffer(wid...]
    pallas_call x1, Pallas kernels: 8.49 us -> 12.3 us  [shard(): call(functools.partial(second_kernel, starts), [VMEM] * len(parts) + [HBM...]
    ppermute x7, waiting for transfers between devices: 3.83 us -> 0.02 us  [swap(): return lax.ppermute(face, 'slab', pairs)]
    unnamed x18 -> x12, local copies, waits for them, and re-layouts: 3.25 us -> 0.02 us
    pallas_call x1, Pallas kernels: 1.18 us -> 1.93 us  [shard(): call(functools.partial(pack_kernel, 0, False), [HBM], [plane(half)], (buf...]
  transfers between devices with their start and end apart: 7 -> 7, of which waited for: 2 -> 0; matrix products, arithmetic and copies ran while one was open for 0% -> 0% of each run, Pallas kernels for 33% -> 44%
where the time goes in v3:
time: 70.5 us; the launch traced here: 69.5 us
  Pallas kernels  37.8 us (54%)
  blocking collectives  17 us (24%)
  starting transfers between devices  13.8 us (20%)
  between operations  0.84 us (1%)
    all_to_all x1, blocking collectives, shard(): got = lax.all_to_all(sent, 'slab', split_axis=0, concat_axis=0, tiled=True)  17 us
    ppermute x7, starting transfers between devices, swap(): return lax.ppermute(face, 'slab', pairs)  13.8 us
    pallas_call x1, Pallas kernels, shard(): call(own_kernel, [HBM, HBM, VMEM, SMEM], [field], (tiles, lap, buffer(wid...  13.5 us
    pallas_call x1, Pallas kernels, shard(): call(functools.partial(second_kernel, starts), [VMEM] * len(parts) + [HBM...  12.3 us
    pallas_call x2, Pallas kernels, shard(): call(functools.partial(last_kernel, first, count), [VMEM] * 6 + [HBM] * l...  3.64 us
    pallas_call x2, Pallas kernels, shard(): call(functools.partial(close_kernel, first), [VMEM] * 4, [jax.ShapeDtypeS...  3.23 us
    pallas_call x1, Pallas kernels, shard(): call(functools.partial(pack_kernel, half, True), [HBM], [plane(width_x),...  2.81 us
    pallas_call x1, Pallas kernels, shard(): call(functools.partial(pack_kernel, 0, False), [HBM], [plane(half)], (buf...  1.93 us
  transfers between devices with their start and end apart: 7, of which 0 were waited for; matrix products, arithmetic and copies ran while one was open for 0% of the time, Pallas kernels for 44%

profile of v3, /device:TPU:9, one launch (start us, length us, event | category | flops | bytes accessed | tf_op | source)
XLA Modules:
  0.0 69.5 jit_solution(12615559225671357116)
XLA Ops:
  0.6 0.0 copy-start.2
  0.6 0.0 copy-start.5
  0.7 0.0 copy-start.4
  0.7 0.0 copy-start.3
  0.7 0.0 copy-start
  0.7 1.9 %shard_map.103 = bf16[160,1280]{1,0:T(8,128)(2,1)S(1)} custom-call(f32[4,320,320]{2,1,0:T(8,128)} %refs_2_.1), custom_call_target="tpu_custom_call" | custom-call | tf_op jit(solution)/shard_map/pallas_call | solution.py:442
  2.6 0.0 copy-done.2
  2.6 0.0 copy-done.5
  2.6 0.0 copy-done.4
  2.6 0.0 copy-done.3
  2.7 0.4 shard_map.104
  3.0 2.8 %shard_map.106 = (bf16[320,1280]{1,0:T(8,128)(2,1)S(1)}, bf16[160,1280]{1,0:T(8,128)(2,1)S(1)}) custom-call(f32[4,320,320]{2,1,0:T(8,128)} %refs_2_.1), custom_call_target="tpu_custom_call" | custom-call | tf_op jit(solution)/shard_map/pallas_call | solution.py:457
  5.8 0.7 %collective-permute-start = (bf16[320,1280]{1,0:T(8,128)(2,1)S(1)}, bf16[320,1280]{1,0:T(8,128)(2,1)S(1)}, u32[]{:S(2)}, u32[]{:S(2)}) collective-permute-start(bf16[320,1280]{1,0:T(8,128)(2,1)S(1)} %get-tuple-element.23), channel_id=1, source_target_pairs={{0,1},{1,0},{2,3},{3,2},{4,5},{5,4},{6,7},{7,6},{8,9},{9,8},{10,11... | collective-permute-start | bytes 2457608 | tf_op jit(solution)/shard_map/ppermute | solution.py:439
  6.6 3.0 %collective-permute-start.1 = (bf16[160,1280]{1,0:T(8,128)(2,1)S(1)}, bf16[160,1280]{1,0:T(8,128)(2,1)S(1)}, u32[]{:S(2)}, u32[]{:S(2)}) collective-permute-start(bf16[160,1280]{1,0:T(8,128)(2,1)S(1)} %shard_map.103), channel_id=1, source_target_pairs={{1,2},{2,1},{3,4},{4,3},{5,6},{6,5},{7,8},{8,7},{9,10},{10,9},{11,... | collective-permute-start | bytes 1228808 | tf_op jit(solution)/shard_map/ppermute | solution.py:439
  9.6 2.5 %collective-permute-start.2 = (bf16[160,1280]{1,0:T(8,128)(2,1)S(1)}, bf16[160,1280]{1,0:T(8,128)(2,1)S(1)}, u32[]{:S(2)}, u32[]{:S(2)}) collective-permute-start(bf16[160,1280]{1,0:T(8,128)(2,1)S(1)} %get-tuple-element.26), channel_id=1, source_target_pairs={{1,2},{2,1},{3,4},{4,3},{5,6},{6,5},{7,8},{8,7},{9,10},{10,9},{11,... | collective-permute-start | bytes 1228808 | tf_op jit(solution)/shard_map/ppermute | solution.py:439
  12.2 17.0 %all_to_all.5.got.refs_5_ = f32[16,1,128]{2,1,0:T(1,128)S(1)} all-to-all(f32[16,1,128]{2,1,0:T(1,128)S(1)} %shard_map.104), channel_id=1, replica_groups=mesh['groups'=2,'slab'=16] {'slab'}, dimensions={0} | all-to-all | bytes 16384 | tf_op jit(solution)/shard_map/all_to_all | solution.py:455
  29.2 0.0 copy-done
  29.2 13.5 %shard_map.105.partial = f32[4,320,320]{2,1,0:T(8,128)S(1)} custom-call(f32[4,320,320]{2,1,0:T(8,128)} %refs_2_.1, f32[4,320,320]{2,1,0:T(8,128)} %prior.1, f32[4,320,320]{2,1,0:T(8,128)S(1)} %copy-done, f32[16,1,128]{2,1,0:T(1,128)S(1)} %all_to_all.5.got.refs_5_), custom_call_target="tpu_custom_call" | custom-call | tf_op jit(solution)/shard_map/pallas_call | solution.py:465
  42.7 0.0 collective-permute-done.1.got_off
  42.7 0.0 collective-permute-done.got_on
  42.7 1.6 %shard_map.107 = (f32[4,160,320]{2,1,0:T(8,128)S(1)}, bf16[160,1280]{1,0:T(8,128)(2,1)S(1)}, bf16[160,1280]{1,0:T(8,128)(2,1)S(1)}) custom-call(f32[4,320,320]{2,1,0:T(8,128)S(1)} %shard_map.105.partial, f32[4,320,320]{2,1,0:T(8,128)S(1)} %copy-done, bf16[320,1280]{1,0:T(8,128)(2,1)S(1)} %collective-permute-done.got_on, ...), custom_call_target="tpu_custom_call" | custom-call | tf_op jit(solution)/shard_map/pallas_call | solution.py:473
  44.3 0.6 collective-permute-start.5
  44.9 0.0 copy-start.1
  44.9 2.7 %collective-permute-start.6 = (bf16[160,1280]{1,0:T(8,128)(2,1)S(1)}, bf16[160,1280]{1,0:T(8,128)(2,1)S(1)}, u32[]{:S(2)}, u32[]{:S(2)}) collective-permute-start(bf16[160,1280]{1,0:T(8,128)(2,1)S(1)} %get-tuple-element.33), channel_id=1, source_target_pairs={{1,2},{2,1},{3,4},{4,3},{5,6},{6,5},{7,8},{8,7},{9,10},{10,9},{11,... | collective-permute-start | bytes 1228808 | tf_op jit(solution)/shard_map/ppermute | solution.py:439
  47.7 0.0 collective-permute-done.2.got_off
  47.7 1.6 %shard_map.108 = (f32[4,160,320]{2,1,0:T(8,128)S(1)}, bf16[160,1280]{1,0:T(8,128)(2,1)S(1)}, bf16[160,1280]{1,0:T(8,128)(2,1)S(1)}) custom-call(f32[4,320,320]{2,1,0:T(8,128)S(1)} %shard_map.105.partial, f32[4,320,320]{2,1,0:T(8,128)S(1)} %copy-done, bf16[320,1280]{1,0:T(8,128)(2,1)S(1)} %collective-permute-done.got_on, ...), custom_call_target="tpu_custom_call" | custom-call | tf_op jit(solution)/shard_map/pallas_call | solution.py:473
  49.3 0.4 collective-permute-start.3
  49.7 3.8 %collective-permute-start.4 = (bf16[160,1280]{1,0:T(8,128)(2,1)S(1)}, bf16[160,1280]{1,0:T(8,128)(2,1)S(1)}, u32[]{:S(2)}, u32[]{:S(2)}) collective-permute-start(bf16[160,1280]{1,0:T(8,128)(2,1)S(1)} %get-tuple-element.31), channel_id=1, source_target_pairs={{1,2},{2,1},{3,4},{4,3},{5,6},{6,5},{7,8},{8,7},{9,10},{10,9},{11,... | collective-permute-start | bytes 1228808 | tf_op jit(solution)/shard_map/ppermute | solution.py:439
  53.5 0.0 copy-done.1
  53.5 12.3 %shard_map.109 = (f32[4,320,320]{2,1,0:T(8,128)S(1)}, f32[4,320,320]{2,1,0:T(8,128)S(1)}, f32[4,320,320]{2,1,0:T(8,128)}) custom-call(f32[4,160,320]{2,1,0:T(8,128)S(1)} %get-tuple-element.24.refs_0_, f32[4,160,320]{2,1,0:T(8,128)S(1)} %get-tuple-element.27.refs_1_, f32[4,320,320]{2,1,0:T(8,128)} %refs_2_.1, f32[4,320,320]{2,1,0:T(8,128)S(1)} %copy-done, ...), custom_call_target="tpu_custom_call" | custom-call | tf_op jit(solution)/shard_map/pallas_call | solution.py:482
  65.8 0.0 collective-permute-done.5.got_on
  65.8 0.0 collective-permute-done.6.got_off
  65.8 1.8 %shard_map.110 = (f32[4,320,320]{2,1,0:T(8,128)}, f32[4,320,320]{2,1,0:T(8,128)}) custom-call(f32[4,320,320]{2,1,0:T(8,128)S(1)} %get-tuple-element.28.partial, f32[4,320,320]{2,1,0:T(8,128)S(1)} %get-tuple-element.29.image_in, f32[4,320,320]{2,1,0:T(8,128)S(1)} %copy-done, f32[2,4,320,320]{3,2,1,0:T(8,128)S(1)} %copy-done.1, ...), custom_call_target="tpu_custom_call" | custom-call | tf_op jit(solution)/shard_map/pallas_call | solution.py:491
  67.6 0.0 collective-permute-done.3.got_on
  67.7 0.0 collective-permute-done.4.got_off
  67.7 1.8 %shard_map.111 = (f32[4,320,320]{2,1,0:T(8,128)}, f32[4,320,320]{2,1,0:T(8,128)}) custom-call(f32[4,320,320]{2,1,0:T(8,128)S(1)} %get-tuple-element.28.partial, f32[4,320,320]{2,1,0:T(8,128)S(1)} %get-tuple-element.29.image_in, f32[4,320,320]{2,1,0:T(8,128)S(1)} %copy-done, ...), custom_call_target="tpu_custom_call", output_to_operand_aliasing={{0}: (6, {}), {1}: (7, {})} | custom-call | tf_op jit(solution)/shard_map/pallas_call | solution.py:491
Async XLA Ops:
  0.6 2.0 %copy-start.2 = (bf16[64,2048]{1,0:T(8,128)(2,1)S(1)}, bf16[64,2048]{1,0:T(8,128)(2,1)}, u32[]{:S(2)}) copy-start(bf16[64,2048]{1,0:T(8,128)(2,1)} %traces) | copy-start | bytes 786436
  0.6 2.0 %copy-start.5 = (s32[64]{0:T(128)S(1)}, s32[64]{0:T(128)}, u32[]{:S(2)}) copy-start(s32[64]{0:T(128)} %param.15) | copy-start | bytes 772
  0.7 2.0 %copy-start.4 = (s32[64,1]{0,1:T(1,128)S(1)}, s32[64,1]{0,1:T(1,128)}, u32[]{:S(2)}) copy-start(s32[64,1]{0,1:T(1,128)} %param.14) | copy-start | bytes 772
  0.7 2.0 %copy-start.3 = (bf16[2,2048]{1,0:T(2,128)(2,1)S(1)}, bf16[2,2048]{1,0:T(2,128)(2,1)}, u32[]{:S(2)}) copy-start(bf16[2,2048]{1,0:T(2,128)(2,1)} %weights.1) | copy-start | bytes 24580
  0.7 28.5 %copy-start = (f32[4,320,320]{2,1,0:T(8,128)S(1)}, f32[4,320,320]{2,1,0:T(8,128)}, u32[]{:S(2)}) copy-start(f32[4,320,320]{2,1,0:T(8,128)} %velocity.9) | copy-start | bytes 4915204
  5.8 36.8 %collective-permute-start = (bf16[320,1280]{1,0:T(8,128)(2,1)S(1)}, bf16[320,1280]{1,0:T(8,128)(2,1)S(1)}, u32[]{:S(2)}, u32[]{:S(2)}) collective-permute-start(bf16[320,1280]{1,0:T(8,128)(2,1)S(1)} %get-tuple-element.23), channel_id=1, source_target_pairs={{0,1},{1,0},{2,3},{3,2},{4,5},{5,4},{6,7},{7,6},{8,9},{9,8},{10,11... | collective-permute-start | bytes 2457608 | tf_op jit(solution)/shard_map/ppermute | solution.py:439
  6.6 36.1 %collective-permute-start.1 = (bf16[160,1280]{1,0:T(8,128)(2,1)S(1)}, bf16[160,1280]{1,0:T(8,128)(2,1)S(1)}, u32[]{:S(2)}, u32[]{:S(2)}) collective-permute-start(bf16[160,1280]{1,0:T(8,128)(2,1)S(1)} %shard_map.103), channel_id=1, source_target_pairs={{1,2},{2,1},{3,4},{4,3},{5,6},{6,5},{7,8},{8,7},{9,10},{10,9},{11,... | collective-permute-start | bytes 1228808 | tf_op jit(solution)/shard_map/ppermute | solution.py:439
  9.6 38.0 %collective-permute-start.2 = (bf16[160,1280]{1,0:T(8,128)(2,1)S(1)}, bf16[160,1280]{1,0:T(8,128)(2,1)S(1)}, u32[]{:S(2)}, u32[]{:S(2)}) collective-permute-start(bf16[160,1280]{1,0:T(8,128)(2,1)S(1)} %get-tuple-element.26), channel_id=1, source_target_pairs={{1,2},{2,1},{3,4},{4,3},{5,6},{6,5},{7,8},{8,7},{9,10},{10,9},{11,... | collective-permute-start | bytes 1228808 | tf_op jit(solution)/shard_map/ppermute | solution.py:439
  44.3 21.5 %collective-permute-start.5 = (bf16[160,1280]{1,0:T(8,128)(2,1)S(1)}, bf16[160,1280]{1,0:T(8,128)(2,1)S(1)}, u32[]{:S(2)}, u32[]{:S(2)}) collective-permute-start(bf16[160,1280]{1,0:T(8,128)(2,1)S(1)} %get-tuple-element.32), channel_id=1, source_target_pairs={{0,1},{1,0},{2,3},{3,2},{4,5},{5,4},{6,7},{7,6},{8,9},{9,8},{10,11... | collective-permute-start | bytes 1228808 | tf_op jit(solution)/shard_map/ppermute | solution.py:439
  44.9 8.5 %copy-start.1 = (f32[2,4,320,320]{3,2,1,0:T(8,128)S(1)}, f32[2,4,320,320]{3,2,1,0:T(8,128)}, u32[]{:S(2)}) copy-start(f32[2,4,320,320]{3,2,1,0:T(8,128)} %forward.3) | copy-start | bytes 9830404
  44.9 20.9 %collective-permute-start.6 = (bf16[160,1280]{1,0:T(8,128)(2,1)S(1)}, bf16[160,1280]{1,0:T(8,128)(2,1)S(1)}, u32[]{:S(2)}, u32[]{:S(2)}) collective-permute-start(bf16[160,1280]{1,0:T(8,128)(2,1)S(1)} %get-tuple-element.33), channel_id=1, source_target_pairs={{1,2},{2,1},{3,4},{4,3},{5,6},{6,5},{7,8},{8,7},{9,10},{10,9},{11,... | collective-permute-start | bytes 1228808 | tf_op jit(solution)/shard_map/ppermute | solution.py:439
  49.3 18.3 %collective-permute-start.3 = (bf16[160,1280]{1,0:T(8,128)(2,1)S(1)}, bf16[160,1280]{1,0:T(8,128)(2,1)S(1)}, u32[]{:S(2)}, u32[]{:S(2)}) collective-permute-start(bf16[160,1280]{1,0:T(8,128)(2,1)S(1)} %get-tuple-element.30), channel_id=1, source_target_pairs={{0,1},{1,0},{2,3},{3,2},{4,5},{5,4},{6,7},{7,6},{8,9},{9,8},{10,11... | collective-permute-start | bytes 1228808 | tf_op jit(solution)/shard_map/ppermute | solution.py:439
  49.7 18.0 %collective-permute-start.4 = (bf16[160,1280]{1,0:T(8,128)(2,1)S(1)}, bf16[160,1280]{1,0:T(8,128)(2,1)S(1)}, u32[]{:S(2)}, u32[]{:S(2)}) collective-permute-start(bf16[160,1280]{1,0:T(8,128)(2,1)S(1)} %get-tuple-element.31), channel_id=1, source_target_pairs={{1,2},{2,1},{3,4},{4,3},{5,6},{6,5},{7,8},{8,7},{9,10},{10,9},{11,... | collective-permute-start | bytes 1228808 | tf_op jit(solution)/shard_map/ppermute | solution.py:439

commit v4 on v3

--- a/solution.py
+++ b/solution.py
@@ -14,9 +14,7 @@
 HALO = 4
 ROWS = 16
 BLOCK = 32
-EDGE = 8
 SUB = 8
-UNROLL = 4
 LANES = 128
 F32 = jnp.float32
 BF16 = jnp.bfloat16
@@ -181,79 +179,75 @@
     out[...] = picked.reshape(out.shape)
 
 
+def tile_parts(width_y):
+    return [(lo, min(lo + LANES, width_y)) for lo in range(0, width_y, LANES)]
+
+
+def tile_rows(z, row, j, width_x, number):
+    return pl.ds((z * (width_x + SUB) + SUB + row) * number + j, SUB, stride=number)
+
+
+def clear(tiles, depth, width_x, number):
+    for z in range(depth + 1):
+        first = z * (width_x + SUB) * number
+        tiles[first : first + SUB * number, :] = jnp.zeros((SUB * number, LANES), F32)
+
+
 def spread(tiles, source, first, start, count):
     depth, _, width_y = source.shape
-    width_x = (tiles.shape[1] - 2 * EDGE) // depth
+    parts = tile_parts(width_y)
+    number = len(parts)
+    width_x = (tiles.shape[0] // number - SUB) // depth - SUB
 
     def body(r):
         for z in range(depth):
-            into = pl.ds(r + (EDGE + z * width_x + first), ROWS)
-            for j in range(tiles.shape[0]):
-                lo, hi = j * LANES, min((j + 1) * LANES, width_y)
-                value = source[z, pl.ds(r + start, ROWS), lo:hi]
-                if hi - lo < LANES:
-                    value = jnp.pad(value, ((0, 0), (0, LANES - (hi - lo))))
-                tiles[j, into, :] = value
+            for j, (lo, hi) in enumerate(parts):
+                for u in range(0, ROWS, SUB):
+                    value = source[z, pl.ds(r + (start + u), SUB), lo:hi]
+                    if hi - lo < LANES:
+                        value = jnp.pad(value, ((0, 0), (0, LANES - (hi - lo))))
+                    tiles[tile_rows(z, r + (first + u), j, width_x, number), :] = value
 
     row_loop(count, body)
 
 
 def own_laplace(tiles, lap, depth, width_y):
-    count, _ = lap.shape
-    count = count // tiles.shape[0]
-    parts = SUB // depth
-    stride = count // SUB
-    number = tiles.shape[0]
-    shape = (SUB, LANES)
-    lane = lax.broadcasted_iota(jnp.int32, shape, 1)
-    sub = lax.broadcasted_iota(jnp.int32, shape, 0)
-    part = lax.rem(sub, parts)
-
-    def weight(k):
-        return W[k] if k <= HALO else 0.0
-
-    mixes = [jnp.where(sub >= d * parts, weight(d), weight(depth - d)) for d in range(1, depth)]
-
-    def rows_at(j, x):
-        return tiles[j, pl.ds(x + EDGE, SUB, stride=stride), :]
-
-    def one(x, low=None, high=None):
-        centre = [rows_at(j, x) for j in range(number)]
-        right = [[pltpu.roll(c, k, 1) for k in range(1, HALO + 1)] for c in centre]
-        left = [[pltpu.roll(c, LANES - k, 1) for k in range(1, HALO + 1)] for c in centre]
-        for j in range(number):
-            total = 3.0 * W[0] * centre[j]
-            for d in range(1, depth):
-                total = total + mixes[d - 1] * pltpu.roll(centre[j], d * parts, 0)
+    number = -(-width_y // LANES)
+    width_x = lap.shape[0] // (number * depth)
+    lane = lax.broadcasted_iota(jnp.int32, (SUB, LANES), 1)
+    wraps = width_y % LANES == 0 or width_y % LANES > LANES - HALO
+
+    def step(i, carry):
+        r = i * SUB
+
+        def at(z, j, shift=0):
+            return tiles[tile_rows(z, r + shift, j, width_x, number), :]
+
+        centre = [[at(z, j) for j in range(number)] for z in range(depth)]
+        for z in range(depth):
+            total = [3.0 * W[0] * centre[z][j] for j in range(number)]
             for k in range(1, HALO + 1):
-                before, after = rows_at(j, x - k), rows_at(j, x + k)
-                if low is not None and low < k:
-                    before = jnp.where(part == 0, 0.0, before)
-                if high is not None and high < k:
-                    after = jnp.where(part == parts - 1, 0.0, after)
-                side = right[j - 1][k - 1] if j else 0.0
-                pair = before + after + jnp.where(lane < k, side, right[j][k - 1])
-                if j + 1 < number:
-                    pair = pair + jnp.where(lane >= LANES - k, left[j + 1][k - 1], left[j][k - 1])
-                elif width_y % LANES > LANES - HALO or width_y % LANES == 0:
-                    pair = pair + jnp.where(lane >= LANES - k, 0.0, left[j][k - 1])
-                else:
-                    pair = pair + left[j][k - 1]
-                total = total + W[k] * pair
-            lap[pl.ds(x + j * count, SUB, stride=stride), :] = total
-
-    for x in range(HALO):
-        one(x, low=x)
-
-    def step(i, carry):
-        for u in range(UNROLL):
-            one(HALO + i * UNROLL + u)
+                right = [pltpu.roll(c, k, 1) for c in centre[z]]
+                left = [pltpu.roll(c, LANES - k, 1) for c in centre[z]]
+                for j in range(number):
+                    pair = at(z, j, -k) + at(z, j, k)
+                    pair = pair + jnp.where(lane < k, right[j - 1] if j else 0.0, right[j])
+                    if j + 1 < number or wraps:
+                        side = left[j + 1] if j + 1 < number else 0.0
+                        pair = pair + jnp.where(lane >= LANES - k, side, left[j])
+                    else:
+                        pair = pair + left[j]
+                    if z - k >= 0:
+                        pair = pair + centre[z - k][j]
+                    if z + k < depth:
+                        pair = pair + centre[z + k][j]
+                    total[j] = total[j] + W[k] * pair
+            for j in range(number):
+                place = pl.multiple_of(r + (j * depth + z) * width_x, SUB)
+                lap[pl.ds(place, SUB), :] = total[j]
         return carry
 
-    steps = (stride - 2 * HALO) // UNROLL
-    lax.fori_loop(0, steps, step, 0)
-    for x in range(HALO + steps * UNROLL, stride):
-        one(x, high=stride - 1 - x)
+    lax.fori_loop(0, width_x // SUB, step, 0)
 
 
 def inject(step, got, lap):
@@ -270,14 +264,11 @@
     lax.fori_loop(0, got.shape[0], body, 0)
 
 
-def tile_parts(width_y):
-    return [(lo, min(lo + LANES, width_y)) for lo in range(0, width_y, LANES)]
-
-
 def own_kernel(now, prior, velocity, got, out, tiles, lap, now_buf, prior_buf, sems):
     depth, width_x, width_y = now.shape
     now_copies = fetch(now, now_buf, sems.at[0], 0, width_x)
     prior_copies = fetch(prior, prior_buf, sems.at[1], 0, width_x)
+    clear(tiles, depth, width_x, len(tile_parts(width_y)))
     for i, copy in enumerate(now_copies):
         copy.wait()
         spread(tiles, now_buf, i * BLOCK, i * BLOCK, BLOCK)
@@ -342,6 +333,7 @@
         )
         write.start()
         writes.append(write)
+    clear(tiles, depth, width_x, len(tile_parts(width_y)))
     for first, part in zip(starts, parts):
         spread(tiles, part, first, 0, part.shape[1])
     own_laplace(tiles, lap, depth, width_y)
@@ -412,7 +404,7 @@
     blocks = width_x // BLOCK
     field = jax.ShapeDtypeStruct(now.shape, F32)
     number = -(-width_y // LANES)
-    tiles = pltpu.VMEM((number, depth * width_x + 2 * EDGE, LANES), F32)
+    tiles = pltpu.VMEM((number * (depth * (width_x + SUB) + SUB), LANES), F32)
     lap = pltpu.VMEM((number * depth * width_x, LANES), F32)
     dma = pltpu.SemaphoreType.DMA
     on_pairs = [(k, k ^ 1) for k in range(slabs) if k ^ 1 < slabs]

time: 70.5 us -> 66.4 us (0.942); the launches traced: 69.5 us -> 66.2 us
  Pallas kernels: 37.8 us -> 31.4 us
  waiting for transfers between devices: 0.02 us -> 3.1 us
    pallas_call x1, Pallas kernels: 13.5 us -> 10.3 us  [shard(): call(own_kernel, [HBM, HBM, VMEM, SMEM], [field], (tiles, lap, buffer(wid...]
    pallas_call x1, Pallas kernels: 12.3 us -> 9.22 us  [shard(): call(functools.partial(second_kernel, starts), [VMEM] * len(parts) + [HBM...]
    ppermute x7, waiting for transfers between devices: 0.02 us -> 3.1 us  [swap(): return lax.ppermute(face, 'slab', pairs)]
  transfers between devices with their start and end apart: 7 -> 7, of which waited for: 0 -> 2; matrix products, arithmetic and copies ran while one was open for 0% -> 0% of each run, Pallas kernels for 44% -> 37%
where the time goes in v4:
time: 66.4 us; the launch traced here: 66.2 us
  Pallas kernels  31.4 us (47%)
  blocking collectives  17 us (26%)
  starting transfers between devices  13.8 us (21%)
  waiting for transfers between devices  3.1 us (5%)
  between operations  0.83 us (1%)
    all_to_all x1, blocking collectives, shard(): got = lax.all_to_all(sent, 'slab', split_axis=0, concat_axis=0, tiled=True)  17 us
    ppermute x7, starting transfers between devices, swap(): return lax.ppermute(face, 'slab', pairs)  13.8 us
    pallas_call x1, Pallas kernels, shard(): call(own_kernel, [HBM, HBM, VMEM, SMEM], [field], (tiles, lap, buffer(wid...  10.3 us
    pallas_call x1, Pallas kernels, shard(): call(functools.partial(second_kernel, starts), [VMEM] * len(parts) + [HBM...  9.22 us
    pallas_call x2, Pallas kernels, shard(): call(functools.partial(last_kernel, first, count), [VMEM] * 6 + [HBM] * l...  3.62 us
    pallas_call x2, Pallas kernels, shard(): call(functools.partial(close_kernel, first), [VMEM] * 4, [jax.ShapeDtypeS...  3.23 us
    ppermute x7, waiting for transfers between devices, swap(): return lax.ppermute(face, 'slab', pairs)  3.1 us
    pallas_call x1, Pallas kernels, shard(): call(functools.partial(pack_kernel, half, True), [HBM], [plane(width_x),...  2.81 us
  transfers between devices with their start and end apart: 7, of which 2 were waited for; matrix products, arithmetic and copies ran while one was open for 0% of the time, Pallas kernels for 37%

profile of v4, /device:TPU:9, one launch (start us, length us, event | category | flops | bytes accessed | tf_op | source)
XLA Modules:
  0.0 66.2 jit_solution(14448384299013928284)
XLA Ops:
  0.6 0.0 copy-start.2
  0.6 0.0 copy-start.5
  0.7 0.0 copy-start.4
  0.7 0.0 copy-start.3
  0.7 0.0 copy-start
  0.7 1.9 %shard_map.103 = bf16[160,1280]{1,0:T(8,128)(2,1)S(1)} custom-call(f32[4,320,320]{2,1,0:T(8,128)} %refs_2_.1), custom_call_target="tpu_custom_call" | custom-call | tf_op jit(solution)/shard_map/pallas_call | solution.py:434
  2.6 0.0 copy-done.2
  2.6 0.0 copy-done.5
  2.6 0.0 copy-done.4
  2.6 0.0 copy-done.3
  2.7 0.4 shard_map.104
  3.0 2.8 %shard_map.106 = (bf16[320,1280]{1,0:T(8,128)(2,1)S(1)}, bf16[160,1280]{1,0:T(8,128)(2,1)S(1)}) custom-call(f32[4,320,320]{2,1,0:T(8,128)} %refs_2_.1), custom_call_target="tpu_custom_call" | custom-call | tf_op jit(solution)/shard_map/pallas_call | solution.py:449
  5.8 0.7 %collective-permute-start = (bf16[320,1280]{1,0:T(8,128)(2,1)S(1)}, bf16[320,1280]{1,0:T(8,128)(2,1)S(1)}, u32[]{:S(2)}, u32[]{:S(2)}) collective-permute-start(bf16[320,1280]{1,0:T(8,128)(2,1)S(1)} %get-tuple-element.23), channel_id=1, source_target_pairs={{0,1},{1,0},{2,3},{3,2},{4,5},{5,4},{6,7},{7,6},{8,9},{9,8},{10,11... | collective-permute-start | bytes 2457608 | tf_op jit(solution)/shard_map/ppermute | solution.py:431
  6.6 3.0 %collective-permute-start.1 = (bf16[160,1280]{1,0:T(8,128)(2,1)S(1)}, bf16[160,1280]{1,0:T(8,128)(2,1)S(1)}, u32[]{:S(2)}, u32[]{:S(2)}) collective-permute-start(bf16[160,1280]{1,0:T(8,128)(2,1)S(1)} %shard_map.103), channel_id=1, source_target_pairs={{1,2},{2,1},{3,4},{4,3},{5,6},{6,5},{7,8},{8,7},{9,10},{10,9},{11,... | collective-permute-start | bytes 1228808 | tf_op jit(solution)/shard_map/ppermute | solution.py:431
  9.6 2.5 %collective-permute-start.2 = (bf16[160,1280]{1,0:T(8,128)(2,1)S(1)}, bf16[160,1280]{1,0:T(8,128)(2,1)S(1)}, u32[]{:S(2)}, u32[]{:S(2)}) collective-permute-start(bf16[160,1280]{1,0:T(8,128)(2,1)S(1)} %get-tuple-element.26), channel_id=1, source_target_pairs={{1,2},{2,1},{3,4},{4,3},{5,6},{6,5},{7,8},{8,7},{9,10},{10,9},{11,... | collective-permute-start | bytes 1228808 | tf_op jit(solution)/shard_map/ppermute | solution.py:431
  12.2 17.0 %all_to_all.5.got.refs_5_ = f32[16,1,128]{2,1,0:T(1,128)S(1)} all-to-all(f32[16,1,128]{2,1,0:T(1,128)S(1)} %shard_map.104), channel_id=1, replica_groups=mesh['groups'=2,'slab'=16] {'slab'}, dimensions={0} | all-to-all | bytes 16384 | tf_op jit(solution)/shard_map/all_to_all | solution.py:447
  29.2 0.0 copy-done
  29.2 10.3 %shard_map.105.partial = f32[4,320,320]{2,1,0:T(8,128)S(1)} custom-call(f32[4,320,320]{2,1,0:T(8,128)} %refs_2_.1, f32[4,320,320]{2,1,0:T(8,128)} %prior.1, f32[4,320,320]{2,1,0:T(8,128)S(1)} %copy-done, f32[16,1,128]{2,1,0:T(1,128)S(1)} %all_to_all.5.got.refs_5_), custom_call_target="tpu_custom_call" | custom-call | tf_op jit(solution)/shard_map/pallas_call | solution.py:457
  39.5 0.0 collective-permute-done.1.got_off
  39.5 0.0 collective-permute-done.got_on
  39.5 1.6 %shard_map.107 = (f32[4,160,320]{2,1,0:T(8,128)S(1)}, bf16[160,1280]{1,0:T(8,128)(2,1)S(1)}, bf16[160,1280]{1,0:T(8,128)(2,1)S(1)}) custom-call(f32[4,320,320]{2,1,0:T(8,128)S(1)} %shard_map.105.partial, f32[4,320,320]{2,1,0:T(8,128)S(1)} %copy-done, bf16[320,1280]{1,0:T(8,128)(2,1)S(1)} %collective-permute-done.got_on, ...), custom_call_target="tpu_custom_call" | custom-call | tf_op jit(solution)/shard_map/pallas_call | solution.py:465
  41.1 0.6 collective-permute-start.5
  41.7 0.0 copy-start.1
  41.7 2.7 %collective-permute-start.6 = (bf16[160,1280]{1,0:T(8,128)(2,1)S(1)}, bf16[160,1280]{1,0:T(8,128)(2,1)S(1)}, u32[]{:S(2)}, u32[]{:S(2)}) collective-permute-start(bf16[160,1280]{1,0:T(8,128)(2,1)S(1)} %get-tuple-element.33), channel_id=1, source_target_pairs={{1,2},{2,1},{3,4},{4,3},{5,6},{6,5},{7,8},{8,7},{9,10},{10,9},{11,... | collective-permute-start | bytes 1228808 | tf_op jit(solution)/shard_map/ppermute | solution.py:431
  44.5 0.0 collective-permute-done.2.got_off
  44.5 1.6 %shard_map.108 = (f32[4,160,320]{2,1,0:T(8,128)S(1)}, bf16[160,1280]{1,0:T(8,128)(2,1)S(1)}, bf16[160,1280]{1,0:T(8,128)(2,1)S(1)}) custom-call(f32[4,320,320]{2,1,0:T(8,128)S(1)} %shard_map.105.partial, f32[4,320,320]{2,1,0:T(8,128)S(1)} %copy-done, bf16[320,1280]{1,0:T(8,128)(2,1)S(1)} %collective-permute-done.got_on, ...), custom_call_target="tpu_custom_call" | custom-call | tf_op jit(solution)/shard_map/pallas_call | solution.py:465
  46.1 0.4 collective-permute-start.3
  46.5 3.8 %collective-permute-start.4 = (bf16[160,1280]{1,0:T(8,128)(2,1)S(1)}, bf16[160,1280]{1,0:T(8,128)(2,1)S(1)}, u32[]{:S(2)}, u32[]{:S(2)}) collective-permute-start(bf16[160,1280]{1,0:T(8,128)(2,1)S(1)} %get-tuple-element.31), channel_id=1, source_target_pairs={{1,2},{2,1},{3,4},{4,3},{5,6},{6,5},{7,8},{8,7},{9,10},{10,9},{11,... | collective-permute-start | bytes 1228808 | tf_op jit(solution)/shard_map/ppermute | solution.py:431
  50.2 0.0 copy-done.1
  50.2 9.2 %shard_map.109 = (f32[4,320,320]{2,1,0:T(8,128)S(1)}, f32[4,320,320]{2,1,0:T(8,128)S(1)}, f32[4,320,320]{2,1,0:T(8,128)}) custom-call(f32[4,160,320]{2,1,0:T(8,128)S(1)} %get-tuple-element.24.refs_0_, f32[4,160,320]{2,1,0:T(8,128)S(1)} %get-tuple-element.27.refs_1_, f32[4,320,320]{2,1,0:T(8,128)} %refs_2_.1, f32[4,320,320]{2,1,0:T(8,128)S(1)} %copy-done, ...), custom_call_target="tpu_custom_call" | custom-call | tf_op jit(solution)/shard_map/pallas_call | solution.py:474
  59.5 0.0 collective-permute-done.5.got_on
  59.5 0.5 collective-permute-done.6.got_off
  60.0 1.8 %shard_map.110 = (f32[4,320,320]{2,1,0:T(8,128)}, f32[4,320,320]{2,1,0:T(8,128)}) custom-call(f32[4,320,320]{2,1,0:T(8,128)S(1)} %get-tuple-element.28.partial, f32[4,320,320]{2,1,0:T(8,128)S(1)} %get-tuple-element.29.image_in, f32[4,320,320]{2,1,0:T(8,128)S(1)} %copy-done, f32[2,4,320,320]{3,2,1,0:T(8,128)S(1)} %copy-done.1, ...), custom_call_target="tpu_custom_call" | custom-call | tf_op jit(solution)/shard_map/pallas_call | solution.py:483
  61.8 0.0 collective-permute-done.3.got_on
  61.9 2.6 %collective-permute-done.4.got_off = bf16[160,1280]{1,0:T(8,128)(2,1)S(1)} collective-permute-done((bf16[160,1280]{1,0:T(8,128)(2,1)S(1)}, bf16[160,1280]{1,0:T(8,128)(2,1)S(1)}, u32[]{:S(2)}, u32[]{:S(2)}) %collective-permute-start.4) | collective-permute-done | bytes 409632 | tf_op jit(solution)/shard_map/ppermute | solution.py:431
  64.4 1.8 %shard_map.111 = (f32[4,320,320]{2,1,0:T(8,128)}, f32[4,320,320]{2,1,0:T(8,128)}) custom-call(f32[4,320,320]{2,1,0:T(8,128)S(1)} %get-tuple-element.28.partial, f32[4,320,320]{2,1,0:T(8,128)S(1)} %get-tuple-element.29.image_in, f32[4,320,320]{2,1,0:T(8,128)S(1)} %copy-done, ...), custom_call_target="tpu_custom_call", output_to_operand_aliasing={{0}: (6, {}), {1}: (7, {})} | custom-call | tf_op jit(solution)/shard_map/pallas_call | solution.py:483
Async XLA Ops:
  0.6 2.0 %copy-start.2 = (bf16[64,2048]{1,0:T(8,128)(2,1)S(1)}, bf16[64,2048]{1,0:T(8,128)(2,1)}, u32[]{:S(2)}) copy-start(bf16[64,2048]{1,0:T(8,128)(2,1)} %traces) | copy-start | bytes 786436
  0.6 2.0 %copy-start.5 = (s32[64]{0:T(128)S(1)}, s32[64]{0:T(128)}, u32[]{:S(2)}) copy-start(s32[64]{0:T(128)} %param.15) | copy-start | bytes 772
  0.7 2.0 %copy-start.4 = (s32[64,1]{0,1:T(1,128)S(1)}, s32[64,1]{0,1:T(1,128)}, u32[]{:S(2)}) copy-start(s32[64,1]{0,1:T(1,128)} %param.14) | copy-start | bytes 772
  0.7 2.0 %copy-start.3 = (bf16[2,2048]{1,0:T(2,128)(2,1)S(1)}, bf16[2,2048]{1,0:T(2,128)(2,1)}, u32[]{:S(2)}) copy-start(bf16[2,2048]{1,0:T(2,128)(2,1)} %weights.1) | copy-start | bytes 24580
  0.7 28.5 %copy-start = (f32[4,320,320]{2,1,0:T(8,128)S(1)}, f32[4,320,320]{2,1,0:T(8,128)}, u32[]{:S(2)}) copy-start(f32[4,320,320]{2,1,0:T(8,128)} %velocity.9) | copy-start | bytes 4915204
  5.8 33.6 %collective-permute-start = (bf16[320,1280]{1,0:T(8,128)(2,1)S(1)}, bf16[320,1280]{1,0:T(8,128)(2,1)S(1)}, u32[]{:S(2)}, u32[]{:S(2)}) collective-permute-start(bf16[320,1280]{1,0:T(8,128)(2,1)S(1)} %get-tuple-element.23), channel_id=1, source_target_pairs={{0,1},{1,0},{2,3},{3,2},{4,5},{5,4},{6,7},{7,6},{8,9},{9,8},{10,11... | collective-permute-start | bytes 2457608 | tf_op jit(solution)/shard_map/ppermute | solution.py:431
  6.6 32.9 %collective-permute-start.1 = (bf16[160,1280]{1,0:T(8,128)(2,1)S(1)}, bf16[160,1280]{1,0:T(8,128)(2,1)S(1)}, u32[]{:S(2)}, u32[]{:S(2)}) collective-permute-start(bf16[160,1280]{1,0:T(8,128)(2,1)S(1)} %shard_map.103), channel_id=1, source_target_pairs={{1,2},{2,1},{3,4},{4,3},{5,6},{6,5},{7,8},{8,7},{9,10},{10,9},{11,... | collective-permute-start | bytes 1228808 | tf_op jit(solution)/shard_map/ppermute | solution.py:431
  9.6 34.8 %collective-permute-start.2 = (bf16[160,1280]{1,0:T(8,128)(2,1)S(1)}, bf16[160,1280]{1,0:T(8,128)(2,1)S(1)}, u32[]{:S(2)}, u32[]{:S(2)}) collective-permute-start(bf16[160,1280]{1,0:T(8,128)(2,1)S(1)} %get-tuple-element.26), channel_id=1, source_target_pairs={{1,2},{2,1},{3,4},{4,3},{5,6},{6,5},{7,8},{8,7},{9,10},{10,9},{11,... | collective-permute-start | bytes 1228808 | tf_op jit(solution)/shard_map/ppermute | solution.py:431
  41.1 18.4 %collective-permute-start.5 = (bf16[160,1280]{1,0:T(8,128)(2,1)S(1)}, bf16[160,1280]{1,0:T(8,128)(2,1)S(1)}, u32[]{:S(2)}, u32[]{:S(2)}) collective-permute-start(bf16[160,1280]{1,0:T(8,128)(2,1)S(1)} %get-tuple-element.32), channel_id=1, source_target_pairs={{0,1},{1,0},{2,3},{3,2},{4,5},{5,4},{6,7},{7,6},{8,9},{9,8},{10,11... | collective-permute-start | bytes 1228808 | tf_op jit(solution)/shard_map/ppermute | solution.py:431
  41.7 8.5 %copy-start.1 = (f32[2,4,320,320]{3,2,1,0:T(8,128)S(1)}, f32[2,4,320,320]{3,2,1,0:T(8,128)}, u32[]{:S(2)}) copy-start(f32[2,4,320,320]{3,2,1,0:T(8,128)} %forward.3) | copy-start | bytes 9830404
  41.7 18.3 %collective-permute-start.6 = (bf16[160,1280]{1,0:T(8,128)(2,1)S(1)}, bf16[160,1280]{1,0:T(8,128)(2,1)S(1)}, u32[]{:S(2)}, u32[]{:S(2)}) collective-permute-start(bf16[160,1280]{1,0:T(8,128)(2,1)S(1)} %get-tuple-element.33), channel_id=1, source_target_pairs={{1,2},{2,1},{3,4},{4,3},{5,6},{6,5},{7,8},{8,7},{9,10},{10,9},{11,... | collective-permute-start | bytes 1228808 | tf_op jit(solution)/shard_map/ppermute | solution.py:431
  46.1 15.7 %collective-permute-start.3 = (bf16[160,1280]{1,0:T(8,128)(2,1)S(1)}, bf16[160,1280]{1,0:T(8,128)(2,1)S(1)}, u32[]{:S(2)}, u32[]{:S(2)}) collective-permute-start(bf16[160,1280]{1,0:T(8,128)(2,1)S(1)} %get-tuple-element.30), channel_id=1, source_target_pairs={{0,1},{1,0},{2,3},{3,2},{4,5},{5,4},{6,7},{7,6},{8,9},{9,8},{10,11... | collective-permute-start | bytes 1228808 | tf_op jit(solution)/shard_map/ppermute | solution.py:431
  46.5 17.9 %collective-permute-start.4 = (bf16[160,1280]{1,0:T(8,128)(2,1)S(1)}, bf16[160,1280]{1,0:T(8,128)(2,1)S(1)}, u32[]{:S(2)}, u32[]{:S(2)}) collective-permute-start(bf16[160,1280]{1,0:T(8,128)(2,1)S(1)} %get-tuple-element.31), channel_id=1, source_target_pairs={{1,2},{2,1},{3,4},{4,3},{5,6},{6,5},{7,8},{8,7},{9,10},{10,9},{11,... | collective-permute-start | bytes 1228808 | tf_op jit(solution)/shard_map/ppermute | solution.py:431

commit v5 on v4

v5 whole, which is shorter than its diff:
```python
import functools

import jax
import jax.numpy as jnp
from jax import lax
from jax.experimental import pallas as pl
from jax.experimental.pallas import tpu as pltpu
from jax.sharding import PartitionSpec as P


CAP = 4
STEPS = 2
W = (-205.0 / 72.0, 8.0 / 5.0, -1.0 / 5.0, 8.0 / 315.0, -1.0 / 560.0)
HALO = 4
ROWS = 16
BLOCK = 32
SUB = 8
UNROLL = 4
SHARE = (3, 2)
LANES = 128
F32 = jnp.float32
BF16 = jnp.bfloat16
VMEM = pl.BlockSpec(memory_space=pltpu.VMEM)
SMEM = pl.BlockSpec(memory_space=pltpu.SMEM)
HBM = pl.BlockSpec(memory_space=pltpu.HBM)


def params():
    return pltpu.CompilerParams(vmem_limit_bytes=16 << 20)


def payload_lanes(width):
    full = width // LANES * LANES
    rest = width - full
    if rest == 0:
        return HALO * full
    return HALO * full + (2 * LANES if rest * 2 <= LANES else HALO * LANES)


def depth_at(j, depth):
    odd = lax.rem(lax.axis_index("slab"), 2)
    return j + (1 - odd) * (depth - 1 - 2 * j)


def encode(u):
    t1 = u[0].astype(BF16).astype(F32)
    e1 = u[0] - t1
    t2 = (u[1] + (W[2] / W[3]) * e1).astype(BF16).astype(F32)
    t3 = u[2].astype(BF16).astype(F32)
    t0 = W[1] * e1 + W[2] * (u[1] - t2) + W[3] * (u[2] - t3) + W[4] * u[3]
    return (t0, t1, t2, t3)


def decode(t):
    t0, t1, t2, t3 = t
    return (
        t0 + W[1] * t1 + W[2] * t2 + W[3] * t3,
        W[2] * t1 + W[3] * t2 + W[4] * t3,
        W[3] * t1 + W[4] * t2,
        W[4] * t1,
    )


def put(ref, rows, t):
    width = t[0].shape[1]
    full = width // LANES * LANES
    rest = width - full
    for k in range(HALO):
        ref[rows, k * full : (k + 1) * full] = t[k][:, :full].astype(BF16)
    if rest == 0:
        return
    base = HALO * full
    if rest * 2 <= LANES:
        half = LANES // 2
        for k in range(0, HALO, 2):
            a = jnp.pad(t[k][:, full:], ((0, 0), (0, half - rest)))
            b = jnp.pad(t[k + 1][:, full:], ((0, 0), (0, half - rest)))
            ref[rows, base : base + LANES] = jnp.concatenate([a, b], axis=1).astype(BF16)
            base += LANES
    else:
        for k in range(HALO):
            tail = jnp.pad(t[k][:, full:], ((0, 0), (0, LANES - rest)))
            ref[rows, base : base + LANES] = tail.astype(BF16)
            base += LANES


def take(ref, rows, width):
    full = width // LANES * LANES
    rest = width - full
    main = [ref[rows, k * full : (k + 1) * full].astype(F32) for k in range(HALO)]
    if rest == 0:
        return main
    base = HALO * full
    tails = []
    if rest * 2 <= LANES:
        half = LANES // 2
        for _ in range(0, HALO, 2):
            both = ref[rows, base : base + LANES].astype(F32)
            tails.append(both[:, :rest])
            tails.append(pltpu.roll(both, half, 1)[:, :rest])
            base += LANES
    else:
        for _ in range(HALO):
            tails.append(ref[rows, base : base + LANES].astype(F32)[:, :rest])
            base += LANES
    return [jnp.concatenate([m, t], axis=1) for m, t in zip(main, tails)]


def row_loop(count, body):
    def step(i, carry):
        body(pl.multiple_of(i * ROWS, ROWS))
        return carry

    lax.fori_loop(0, count // ROWS, step, 0)


def row_span(width_x):
    return 1 << (width_x - 1).bit_length()


def blocks_of(first, count):
    return [(i, min(BLOCK, first + count - i)) for i in range(first, first + count, BLOCK)]


def fetch(source, buf, sems, first, count):
    copies = []
    for n, (row, size) in enumerate(blocks_of(first, count)):
        rows = pl.ds(row, size)
        copies.append(
            pltpu.make_async_copy(source.at[:, rows], buf.at[:, pl.ds(row - first, size)], sems.at[n])
        )
        copies[-1].start()
    return copies


def pack_kernel(first, with_on, now, *refs):
    refs = list(refs)
    on_ref = refs.pop(0) if with_on else None
    off_ref, buf, sems = refs
    depth = now.shape[0]
    base = 0 if with_on else first
    copies = fetch(now, buf, sems, base, buf.shape[1])

    for i, copy in enumerate(copies):
        copy.wait()

        def body(r):
            r = r + i * BLOCK
            rows = pl.ds(r, ROWS)
            u = [buf[depth_at(j, depth), rows, :] for j in range(depth)]
            if base + i * BLOCK >= first and base + i * BLOCK < first + off_ref.shape[0]:
                put(off_ref, pl.ds(r + base - first, ROWS), encode(u[::-1][:HALO]))
            if with_on:
                put(on_ref, rows, encode(u[:HALO]))

        row_loop(BLOCK, body)


def route_kernel(slabs, field, traces, weights, target, cell, out):
    depth, width_x, width_y = field
    rows = traces.shape[0]
    lane = lax.broadcasted_iota(jnp.int32, (rows, rows), 1)
    row = lax.broadcasted_iota(jnp.int32, (rows, rows), 0)
    eye = lane == row
    target_row = jnp.broadcast_to(target[...], (rows, rows))
    cell_row = jnp.broadcast_to(cell[...], (rows, rows))
    target_col = jnp.sum(jnp.where(eye, target_row, 0), axis=1, keepdims=True)
    cell_col = jnp.sum(jnp.where(eye, cell_row, 0), axis=1, keepdims=True)
    same = (target_row == target_col) & (lane < row)
    rank = jnp.sum(jnp.where(same, 1, 0), axis=1, keepdims=True)
    values = traces[...].astype(F32)
    columns = [
        jnp.sum(values * weights[s : s + 1, :].astype(F32), axis=1, keepdims=True)
        for s in range(STEPS)
    ]
    line = cell_col // width_y
    layer = line // width_x
    column = cell_col - line * width_y
    plane = (column // LANES) * depth + layer
    code = (plane * row_span(width_x) + line - layer * width_x) * LANES + column % LANES
    columns.append(code.astype(F32))
    spot = lax.broadcasted_iota(jnp.int32, (rows, LANES), 1)
    spread = jnp.zeros((rows, LANES), F32)
    for j, column in enumerate(columns):
        spread = jnp.where(spot == j * CAP + rank, column, spread)
    taker = lax.broadcasted_iota(jnp.int32, (slabs, rows), 0)
    chosen = (taker == jnp.broadcast_to(target[...], (slabs, rows))).astype(F32)
    picked = jnp.dot(
        chosen, spread, precision=lax.Precision.HIGHEST, preferred_element_type=F32
    )
    out[...] = picked.reshape(out.shape)


def tile_parts(width_y):
    return [(lo, min(lo + LANES, width_y)) for lo in range(0, width_y, LANES)]


def join(pieces, width_y):
    last = width_y - (len(pieces) - 1) * LANES
    return jnp.concatenate([*pieces[:-1], pieces[-1][:, :last]], axis=1)


def tile_rows(z, row, j, count, number):
    return pl.ds((z * (count + 2 * SUB) + SUB + row) * number + j, SUB, stride=number)


def spread(tiles, count, source, start, row, size):
    depth, _, width_y = source.shape
    parts = tile_parts(width_y)

    def body(i, carry):
        r = i * SUB
        for z in range(depth):
            for j, (lo, hi) in enumerate(parts):
                value = source[z, pl.ds(pl.multiple_of(r + start, SUB), SUB), lo:hi]
                if hi - lo < LANES:
                    value = jnp.pad(value, ((0, 0), (0, LANES - (hi - lo))))
                tiles[tile_rows(z, r + row, j, count, len(parts)), :] = value
        return carry

    lax.fori_loop(0, size // SUB, body, 0)


def clear(tiles, count, depth, number, row):
    for z in range(depth):
        for j in range(number):
            tiles[tile_rows(z, row, j, count, number), :] = jnp.zeros((SUB, LANES), F32)


def own_laplace(tiles, lap, depth, count, width_y):
    number = len(tile_parts(width_y))
    lane = lax.broadcasted_iota(jnp.int32, (SUB, LANES), 1)
    wraps = width_y % LANES == 0 or width_y % LANES > LANES - HALO
    groups = count // SUB
    unroll = max(u for u in range(1, UNROLL + 1) if groups % u == 0)

    def one(r):
        def at(z, j, shift=0):
            return tiles[tile_rows(z, r + shift, j, count, number), :]

        centre = [[at(z, j) for j in range(number)] for z in range(depth)]
        for z in range(depth):
            total = [3.0 * W[0] * centre[z][j] for j in range(number)]
            for k in range(1, HALO + 1):
                right = [pltpu.roll(c, k, 1) for c in centre[z]]
                left = [pltpu.roll(c, LANES - k, 1) for c in centre[z]]
                for j in range(number):
                    pair = at(z, j, -k) + at(z, j, k)
                    pair = pair + jnp.where(lane < k, right[j - 1] if j else 0.0, right[j])
                    if j + 1 < number or wraps:
                        side = left[j + 1] if j + 1 < number else 0.0
                        pair = pair + jnp.where(lane >= LANES - k, side, left[j])
                    else:
                        pair = pair + left[j]
                    if z - k >= 0:
                        pair = pair + centre[z - k][j]
                    if z + k < depth:
                        pair = pair + centre[z + k][j]
                    total[j] = total[j] + W[k] * pair
            for j in range(number):
                place = pl.multiple_of(r + (j * depth + z) * count, SUB)
                lap[pl.ds(place, SUB), :] = total[j]

    def step(i, carry):
        for u in range(unroll):
            one((i * unroll + u) * SUB)
        return carry

    lax.fori_loop(0, groups // unroll, step, 0)


def inject(step, got, lap, planes, first, count, width_x):
    lane = lax.broadcasted_iota(jnp.int32, (1, LANES), 1)
    span = row_span(width_x)
    shift = LANES.bit_length() - 1

    def body(i, carry):
        for slot in range(CAP):
            source = got[i, 0, step * CAP + slot]
            code = got[i, 0, STEPS * CAP + slot].astype(jnp.int32)
            line = lax.shift_right_logical(code, jnp.int32(shift))
            row = (line & (span - 1)) - first
            plane = lax.shift_right_logical(line, jnp.int32(span.bit_length() - 1))
            inside = (row >= 0) & (row < count)
            place = pl.ds(jnp.where(inside, plane * count + row, planes * count), 1)
            lap[place, :] = lap[place, :] + jnp.where(lane == (code & (LANES - 1)), source, 0.0)
        return carry

    lax.fori_loop(0, got.shape[0], body, 0)


def lap_rows(lap, z, r, depth, count, width_y):
    pieces = []
    for j in range(len(tile_parts(width_y))):
        place = pl.multiple_of((j * depth + z) * count + r, ROWS)
        pieces.append(lap[pl.ds(place, ROWS), :])
    return join(pieces, width_y)


def halo_sum(got_on, rows_on, got_off, rows_off, width_y, depth):
    near = decode(take(got_on, rows_on, width_y))
    far = decode(take(got_off, rows_off, width_y))
    out = []
    for j in range(depth):
        terms = [near[j]] if j < HALO else []
        if depth - 1 - j < HALO:
            terms.append(far[depth - 1 - j])
        out.append(functools.reduce(lambda a, b: a + b, terms) if terms else None)
    return out


def first_kernel(
    first, now, prior, velocity, got, got_on, got_off, part, on_ref, off_ref,
    tiles, lap, now_buf, prior_buf, speed_buf, sems
):
    depth, width_x, width_y = now.shape
    count = part.shape[1]
    number = len(tile_parts(width_y))
    low, high = max(first - SUB, 0), min(first + count + SUB, width_x)
    now_copies = fetch(now, now_buf, sems.at[0], low, high - low)
    prior_copies = fetch(prior, prior_buf, sems.at[1], first, count)
    speed_copies = fetch(velocity, speed_buf, sems.at[2], first, count)
    if low == first:
        clear(tiles, count, depth, number, -SUB)
    if high == first + count:
        clear(tiles, count, depth, number, count)
    for copy, (row, size) in zip(now_copies, blocks_of(low, high - low)):
        copy.wait()
        spread(tiles, count, now_buf, row - low, row - first, size)
    own_laplace(tiles, lap, depth, count, width_y)
    inject(0, got, lap, number * depth, first, count, width_x)
    for copy in prior_copies + speed_copies:
        copy.wait()

    def body(r):
        rows = pl.ds(r, ROWS)
        here = pl.ds(pl.multiple_of(r + (first - low), SUB), ROWS)
        halo = halo_sum(got_on, pl.ds(r + first, ROWS), got_off, rows, width_y, depth)
        u = []
        for j in range(depth):
            z = depth_at(j, depth)
            change = lap_rows(lap, z, r, depth, count, width_y)
            if halo[j] is not None:
                change = change + halo[j]
            value = 2.0 * now_buf[z, here, :] - prior_buf[z, rows, :]
            value = value + speed_buf[z, rows, :] * change
            part[z, rows, :] = value
            u.append(value)
        put(off_ref, rows, encode(u[::-1][:HALO]))
        put(on_ref, rows, encode(u[:HALO]))

    row_loop(count, body)


def second_local(first, starts, parts, now, velocity, forward, got, tiles, lap, bufs, sems):
    now_buf, speed_buf, *forward_bufs = bufs
    depth, width_x, width_y = now.shape
    count = now_buf.shape[1]
    number = len(tile_parts(width_y))
    low, high = max(first - SUB, 0), min(first + count + SUB, width_x)
    copies = fetch(now, now_buf, sems.at[0], first, count)
    copies += fetch(velocity, speed_buf, sems.at[1], first, count)
    for s in range(STEPS):
        copies += fetch(forward.at[s], forward_bufs[s], sems.at[2 + s], first, count)
    if low == first:
        clear(tiles, count, depth, number, -SUB)
    if high == first + count:
        clear(tiles, count, depth, number, count)
    for start, part in zip(starts, parts):
        row, end = max(low, start), min(high, start + part.shape[1])
        spread(tiles, count, part, row - start, row - first, end - row)
    own_laplace(tiles, lap, depth, count, width_y)
    inject(1, got, lap, number * depth, first, count, width_x)
    for copy in copies:
        copy.wait()
    return parts[starts.index(first)]


def send_rows(pairs, first, row, sems, n):
    writes = []
    for k, (buf, target) in enumerate(pairs):
        write = pltpu.make_async_copy(
            buf.at[:, pl.ds(row, BLOCK)], target.at[:, pl.ds(first + row, BLOCK)], sems.at[k, n]
        )
        write.start()
        writes.append(write)
    return writes


def second_kernel(first, starts, *refs):
    parts, refs = refs[: len(starts)], refs[len(starts) :]
    now, velocity, forward, got, got_on, got_off, out, image, current, tiles, lap = refs[:11]
    *bufs, out_buf, image_buf, sems, out_sems, part_sems = refs[11:]
    depth, _, width_y = now.shape
    count = out_buf.shape[1]
    writes = []
    for i, (start, part) in enumerate(zip(starts, parts)):
        write = pltpu.make_async_copy(
            part, current.at[:, pl.ds(start, part.shape[1])], part_sems.at[i]
        )
        write.start()
        writes.append(write)
    here = second_local(first, starts, parts, now, velocity, forward, got, tiles, lap, bufs, sems)
    now_buf, speed_buf, early, late = bufs
    for n, i in enumerate(range(0, count, BLOCK)):

        def body(r):
            r = r + i
            rows = pl.ds(r, ROWS)
            halo = halo_sum(got_on, rows, got_off, rows, width_y, depth)
            for j in range(depth):
                z = depth_at(j, depth)
                change = lap_rows(lap, z, r, depth, count, width_y)
                if halo[j] is not None:
                    change = change + halo[j]
                mine = here[z, rows, :]
                value = 2.0 * mine - now_buf[z, rows, :] + speed_buf[z, rows, :] * change
                out_buf[z, rows, :] = value
                image_buf[z, rows, :] = early[z, rows, :] * mine + late[z, rows, :] * value

        row_loop(BLOCK, body)
        writes += send_rows(((out_buf, out), (image_buf, image)), first, i, out_sems, n)
    for write in writes:
        write.wait()


def partial_kernel(first, starts, *refs):
    parts, refs = refs[: len(starts)], refs[len(starts) :]
    now, velocity, forward, got, out, image, speed, late, tiles, lap, now_buf, early, sems = refs
    depth, _, width_y = now.shape
    count = now_buf.shape[1]
    bufs = (now_buf, speed, early, late)
    here = second_local(first, starts, parts, now, velocity, forward, got, tiles, lap, bufs, sems)

    def body(r):
        rows = pl.ds(r, ROWS)
        for z in range(depth):
            change = lap_rows(lap, z, r, depth, count, width_y)
            mine = here[z, rows, :]
            value = 2.0 * mine - now_buf[z, rows, :] + speed[z, rows, :] * change
            out[z, rows, :] = value
            image[z, rows, :] = early[z, rows, :] * mine + late[z, rows, :] * value

    row_loop(count, body)


def last_kernel(first, partial, image_in, speed, late, got_on, got_off, *refs):
    out, image, out_buf, image_buf, sems = refs[-5:]
    depth, count, width_y = out_buf.shape
    writes = []
    for n, i in enumerate(range(0, count, BLOCK)):

        def body(r):
            rows = pl.ds(r + i, ROWS)
            halo = halo_sum(got_on, rows, got_off, rows, width_y, depth)
            for j in range(depth):
                z = depth_at(j, depth)
                extra = speed[z, rows, :] * halo[j] if halo[j] is not None else 0.0
                out_buf[z, rows, :] = partial[z, rows, :] + extra
                image_buf[z, rows, :] = image_in[z, rows, :] + late[z, rows, :] * extra

        row_loop(BLOCK, body)
        writes += send_rows(((out_buf, out), (image_buf, image)), first, i, sems, n)
    for write in writes:
        write.wait()


def shard(now, prior, velocity, forward, traces, weights, target, cell):
    now, prior, velocity, forward = (
        pltpu.with_memory_space_constraint(x, pltpu.HBM) for x in (now, prior, velocity, forward)
    )
    slabs = lax.axis_size("slab")
    depth, width_x, width_y = now.shape
    rows = traces.shape[0]
    face_lanes = payload_lanes(width_y)
    split = width_x * SHARE[0] // (sum(SHARE) * BLOCK) * BLOCK
    chunks = ((0, split), (split, width_x - split))
    starts = tuple(first for first, _ in chunks)
    field = jax.ShapeDtypeStruct(now.shape, F32)
    number = len(tile_parts(width_y))
    dma = pltpu.SemaphoreType.DMA
    on_pairs = [(k, k ^ 1) for k in range(slabs) if k ^ 1 < slabs]
    off_pairs = [(i + 1, j + 1) for i, j in on_pairs if i + 1 < slabs and j + 1 < slabs]

    def plane(count):
        return jax.ShapeDtypeStruct((count, face_lanes), BF16)

    def rows_of(count):
        return jax.ShapeDtypeStruct((depth, count, width_y), F32)

    def buffer(count):
        return pltpu.VMEM((depth, count, width_y), F32)

    def stencil(count):
        tiles = pltpu.VMEM((number * depth * (count + 2 * SUB), LANES), F32)
        lap = pltpu.VMEM((number * depth * count + SUB, LANES), F32)
        return (tiles, lap)

    def blocks(count):
        return -(-count // BLOCK)

    def call(kernel, ins, outs, scratch=(), out_spec=None, **kw):
        return pl.pallas_call(
            kernel,
            in_specs=ins,
            out_specs=out_spec or [VMEM] * len(outs),
            out_shape=outs,
            scratch_shapes=scratch,
            compiler_params=params(),
            **kw,
        )

    def swap(face, pairs):
        return lax.ppermute(face, "slab", pairs)

    got_off = []
    (face,) = call(
        functools.partial(pack_kernel, 0, False),
        [HBM],
        [plane(split)],
        (buffer(split), dma((blocks(split),))),
    )(now)
    got_off.append(swap(face, off_pairs))
    face, traces = lax.optimization_barrier((face, traces))
    (sent,) = call(
        functools.partial(route_kernel, slabs, now.shape),
        [VMEM] * 4,
        [jax.ShapeDtypeStruct((slabs, 1, LANES), F32)],
    )(traces, weights, target.reshape(1, rows), cell.reshape(1, rows))
    got = lax.all_to_all(sent, "slab", split_axis=0, concat_axis=0, tiled=True)
    sent, later = lax.optimization_barrier((sent, now))
    on_face, face = call(
        functools.partial(pack_kernel, split, True),
        [HBM],
        [plane(width_x), plane(width_x - split)],
        (buffer(width_x), dma((blocks(width_x),))),
    )(later)
    got_off.append(swap(face, off_pairs))
    got_on = swap(on_face, on_pairs)
    parts, second_on, second_off = [], [], []
    for (first, count), got_face in zip(chunks, got_off):
        part, on_face, face = call(
            functools.partial(first_kernel, first),
            [HBM] * 3 + [SMEM, VMEM, VMEM],
            [rows_of(count), plane(count), plane(count)],
            (
                *stencil(count),
                buffer(count + 2 * SUB),
                buffer(count),
                buffer(count),
                dma((3, blocks(count + 2 * SUB))),
            ),
        )(now, prior, velocity, got, got_on, got_face)
        second_off.append(swap(face, off_pairs))
        second_on.append(swap(on_face, on_pairs))
        parts.append(part)
        part, prior = lax.optimization_barrier((part, prior))
    (first, count), (last, size) = chunks
    second, image, current = call(
        functools.partial(second_kernel, first, starts),
        [VMEM] * len(parts) + [HBM] * 3 + [SMEM, VMEM, VMEM],
        [field, field, field],
        (
            *stencil(count),
            *[buffer(count)] * 6,
            dma((2 + STEPS, blocks(count))),
            dma((2, blocks(count))),
            dma((len(parts),)),
        ),
        [HBM] * 3,
    )(*parts, now, velocity, forward, got, second_on[0], second_off[0])
    partial, image_part, speed, late = call(
        functools.partial(partial_kernel, last, starts),
        [VMEM] * len(parts) + [HBM] * 3 + [SMEM],
        [rows_of(size)] * 4,
        (*stencil(size), buffer(size), buffer(size), dma((2 + STEPS, blocks(size)))),
    )(*parts, now, velocity, forward, got)
    second, image = call(
        functools.partial(last_kernel, last),
        [VMEM] * 6 + [HBM] * 2,
        [field, field],
        (buffer(size), buffer(size), dma((2, blocks(size)))),
        [HBM] * 2,
        input_output_aliases={6: 0, 7: 1},
    )(partial, image_part, speed, late, second_on[1], second_off[1], second, image)
    return (image, second, current)


def solution(mesh):
    split = P(("groups", "slab"), None, None)
    return jax.shard_map(
        shard,
        mesh=mesh,
        in_specs=(
            split,
            split,
            split,
            P(None, ("groups", "slab"), None, None),
            P(("groups", "slab"), None),
            P(),
            P(("groups", "slab"), None),
            P(("groups", "slab")),
        ),
        out_specs=(split, split, split),
        check_vma=False,
    )
```

time: 66.4 us -> 64.8 us (0.976)
  Pallas kernels: 31.4 us -> 30.2 us
    pallas_call x9 -> x8, Pallas kernels: 31.4 us -> 30.2 us  [the longest x2 13.2 us: shard(): call(functools.partial(first_kernel, first), [HBM] * 3 + [SMEM, VMEM, VME...]
  transfers between devices with their start and end apart: 7 -> 7, of which waited for: 2 -> 1; matrix products, arithmetic and copies ran while one was open for 0% -> 0% of each run, Pallas kernels for 37% -> 36%
where the time goes in v5:
time: 64.8 us; the launch traced here: 64.5 us
  Pallas kernels  30.2 us (47%)
  blocking collectives  17 us (26%)
  starting transfers between devices  13.6 us (21%)
  waiting for transfers between devices  2.78 us (4%)
  between operations  0.81 us (1%)
    all_to_all x1, blocking collectives, shard(): got = lax.all_to_all(sent, 'slab', split_axis=0, concat_axis=0, tiled=True)  17 us
    ppermute x7, starting transfers between devices, swap(): return lax.ppermute(face, 'slab', pairs)  13.6 us
    pallas_call x2, Pallas kernels, shard(): call(functools.partial(first_kernel, first), [HBM] * 3 + [SMEM, VMEM, VME...  13.2 us
    pallas_call x1, Pallas kernels, shard(): call(functools.partial(second_kernel, first, starts), [VMEM] * len(parts)...  6.56 us
    pallas_call x1, Pallas kernels, shard(): call(functools.partial(partial_kernel, last, starts), [VMEM] * len(parts)...  3.74 us
    ppermute x7, waiting for transfers between devices, swap(): return lax.ppermute(face, 'slab', pairs)  2.78 us
    pallas_call x1, Pallas kernels, shard(): call(functools.partial(pack_kernel, split, True), [HBM], [plane(width_x),...  2.78 us
    pallas_call x1, Pallas kernels, shard(): call(functools.partial(pack_kernel, 0, False), [HBM], [plane(split)], (bu...  1.99 us
  transfers between devices with their start and end apart: 7, of which 1 were waited for; matrix products, arithmetic and copies ran while one was open for 0% of the time, Pallas kernels for 36%

profile of v5, /device:TPU:9, one launch (start us, length us, event | category | flops | bytes accessed | tf_op | source)
XLA Modules:
  0.0 64.5 jit_solution(3758114309716015606)
XLA Ops:
  0.6 0.0 copy-start
  0.6 0.0 copy-start.3
  0.7 0.0 copy-start.2
  0.7 0.0 copy-start.1
  0.7 2.0 %shard_map.103 = bf16[192,1280]{1,0:T(8,128)(2,1)S(1)} custom-call(f32[4,320,320]{2,1,0:T(8,128)} %refs_2_.3), custom_call_target="tpu_custom_call" | custom-call | tf_op jit(solution)/shard_map/pallas_call | solution.py:517
  2.7 0.0 copy-done
  2.7 0.0 copy-done.3
  2.7 0.0 copy-done.2
  2.7 0.0 copy-done.1
  2.7 0.4 shard_map.104
  3.1 2.8 %shard_map.105 = (bf16[320,1280]{1,0:T(8,128)(2,1)S(1)}, bf16[128,1280]{1,0:T(8,128)(2,1)S(1)}) custom-call(f32[4,320,320]{2,1,0:T(8,128)} %refs_2_.3), custom_call_target="tpu_custom_call" | custom-call | tf_op jit(solution)/shard_map/pallas_call | solution.py:532
  5.9 0.7 %collective-permute-start = (bf16[320,1280]{1,0:T(8,128)(2,1)S(1)}, bf16[320,1280]{1,0:T(8,128)(2,1)S(1)}, u32[]{:S(2)}, u32[]{:S(2)}) collective-permute-start(bf16[320,1280]{1,0:T(8,128)(2,1)S(1)} %get-tuple-element.25), channel_id=1, source_target_pairs={{0,1},{1,0},{2,3},{3,2},{4,5},{5,4},{6,7},{7,6},{8,9},{9,8},{10,11... | collective-permute-start | bytes 2457608 | tf_op jit(solution)/shard_map/ppermute | solution.py:514
  6.6 3.0 %collective-permute-start.1 = (bf16[192,1280]{1,0:T(8,128)(2,1)S(1)}, bf16[192,1280]{1,0:T(8,128)(2,1)S(1)}, u32[]{:S(2)}, u32[]{:S(2)}) collective-permute-start(bf16[192,1280]{1,0:T(8,128)(2,1)S(1)} %shard_map.103), channel_id=1, source_target_pairs={{1,2},{2,1},{3,4},{4,3},{5,6},{6,5},{7,8},{8,7},{9,10},{10,9},{11,... | collective-permute-start | bytes 1474568 | tf_op jit(solution)/shard_map/ppermute | solution.py:514
  9.7 2.5 %collective-permute-start.2 = (bf16[128,1280]{1,0:T(8,128)(2,1)S(1)}, bf16[128,1280]{1,0:T(8,128)(2,1)S(1)}, u32[]{:S(2)}, u32[]{:S(2)}) collective-permute-start(bf16[128,1280]{1,0:T(8,128)(2,1)S(1)} %get-tuple-element.28), channel_id=1, source_target_pairs={{1,2},{2,1},{3,4},{4,3},{5,6},{6,5},{7,8},{8,7},{9,10},{10,9},{11,... | collective-permute-start | bytes 983048 | tf_op jit(solution)/shard_map/ppermute | solution.py:514
  12.2 17.0 %all_to_all.5.got.refs_5_ = f32[16,1,128]{2,1,0:T(1,128)S(1)} all-to-all(f32[16,1,128]{2,1,0:T(1,128)S(1)} %shard_map.104), channel_id=1, replica_groups=mesh['groups'=2,'slab'=16] {'slab'}, dimensions={0} | all-to-all | bytes 16384 | tf_op jit(solution)/shard_map/all_to_all | solution.py:530
  29.2 0.0 collective-permute-done.1.got_off
  29.2 0.0 collective-permute-done.got_on
  29.2 7.5 %shard_map.106 = (f32[4,192,320]{2,1,0:T(8,128)S(1)}, bf16[192,1280]{1,0:T(8,128)(2,1)S(1)}, bf16[192,1280]{1,0:T(8,128)(2,1)S(1)}) custom-call(f32[4,320,320]{2,1,0:T(8,128)} %refs_2_.3, f32[4,320,320]{2,1,0:T(8,128)} %prior.2, f32[4,320,320]{2,1,0:T(8,128)} %refs_3_.3, f32[16,1,128]{2,1,0:T(1,128)S(1)} %all_to_all.5.got.refs_5_, ...), custom_call_target="tpu_custom_call" | custom-call | tf_op jit(solution)/shard_map/pallas_call | solution.py:542
  36.7 0.7 %collective-permute-start.5 = (bf16[192,1280]{1,0:T(8,128)(2,1)S(1)}, bf16[192,1280]{1,0:T(8,128)(2,1)S(1)}, u32[]{:S(2)}, u32[]{:S(2)}) collective-permute-start(bf16[192,1280]{1,0:T(8,128)(2,1)S(1)} %get-tuple-element.36), channel_id=1, source_target_pairs={{0,1},{1,0},{2,3},{3,2},{4,5},{5,4},{6,7},{7,6},{8,9},{9,8},{10,11... | collective-permute-start | bytes 1474568 | tf_op jit(solution)/shard_map/ppermute | solution.py:514
  37.4 2.5 %collective-permute-start.6 = (bf16[192,1280]{1,0:T(8,128)(2,1)S(1)}, bf16[192,1280]{1,0:T(8,128)(2,1)S(1)}, u32[]{:S(2)}, u32[]{:S(2)}) collective-permute-start(bf16[192,1280]{1,0:T(8,128)(2,1)S(1)} %get-tuple-element.37), channel_id=1, source_target_pairs={{1,2},{2,1},{3,4},{4,3},{5,6},{6,5},{7,8},{8,7},{9,10},{10,9},{11,... | collective-permute-start | bytes 1474568 | tf_op jit(solution)/shard_map/ppermute | solution.py:514
  39.8 0.0 collective-permute-done.2.got_off
  39.8 5.7 %shard_map.107 = (f32[4,128,320]{2,1,0:T(8,128)S(1)}, bf16[128,1280]{1,0:T(8,128)(2,1)S(1)}, bf16[128,1280]{1,0:T(8,128)(2,1)S(1)}) custom-call(f32[4,320,320]{2,1,0:T(8,128)} %refs_2_.3, f32[4,320,320]{2,1,0:T(8,128)} %prior.2, f32[4,320,320]{2,1,0:T(8,128)} %refs_3_.3, f32[16,1,128]{2,1,0:T(1,128)S(1)} %all_to_all.5.got.refs_5_, ...), custom_call_target="tpu_custom_call" | custom-call | tf_op jit(solution)/shard_map/pallas_call | solution.py:542
  45.6 0.4 collective-permute-start.3
  46.0 3.7 %collective-permute-start.4 = (bf16[128,1280]{1,0:T(8,128)(2,1)S(1)}, bf16[128,1280]{1,0:T(8,128)(2,1)S(1)}, u32[]{:S(2)}, u32[]{:S(2)}) collective-permute-start(bf16[128,1280]{1,0:T(8,128)(2,1)S(1)} %get-tuple-element.35), channel_id=1, source_target_pairs={{1,2},{2,1},{3,4},{4,3},{5,6},{6,5},{7,8},{8,7},{9,10},{10,9},{11,... | collective-permute-start | bytes 983048 | tf_op jit(solution)/shard_map/ppermute | solution.py:514
  49.8 3.7 %shard_map.108 = (f32[4,128,320]{2,1,0:T(8,128)S(1)}, f32[4,128,320]{2,1,0:T(8,128)S(1)}, f32[4,128,320]{2,1,0:T(8,128)S(1)}, f32[4,128,320]{2,1,0:T(8,128)S(1)}) custom-call(f32[4,192,320]{2,1,0:T(8,128)S(1)} %get-tuple-element.26.refs_0_, f32[4,128,320]{2,1,0:T(8,128)S(1)} %get-tuple-element.29.refs_1_, f32[4,320,320]{2,1,0:T(8,128)} %refs_2_.3, ...), custom_call_target="tpu_custom_call" | custom-call | tf_op jit(solution)/shard_map/pallas_call | solution.py:572
  53.5 0.0 collective-permute-done.5.refs_6_
  53.5 2.8 %collective-permute-done.6.refs_7_ = bf16[192,1280]{1,0:T(8,128)(2,1)S(1)} collective-permute-done((bf16[192,1280]{1,0:T(8,128)(2,1)S(1)}, bf16[192,1280]{1,0:T(8,128)(2,1)S(1)}, u32[]{:S(2)}, u32[]{:S(2)}) %collective-permute-start.6) | collective-permute-done | bytes 491552 | tf_op jit(solution)/shard_map/ppermute | solution.py:514
  56.3 6.6 %shard_map.109 = (f32[4,320,320]{2,1,0:T(8,128)}, f32[4,320,320]{2,1,0:T(8,128)}, f32[4,320,320]{2,1,0:T(8,128)}) custom-call(f32[4,192,320]{2,1,0:T(8,128)S(1)} %get-tuple-element.26.refs_0_, f32[4,128,320]{2,1,0:T(8,128)S(1)} %get-tuple-element.29.refs_1_, f32[4,320,320]{2,1,0:T(8,128)} %refs_2_.3, f32[4,320,320]{2,1,0:T(8,128)} %refs_3_.3, ...), custom_call_target="tpu_custom_call" | custom-call | tf_op jit(solution)/shard_map/pallas_call | solution.py:559
  62.8 0.0 collective-permute-done.3.got_on
  62.8 0.0 collective-permute-done.4.got_off
  62.9 1.6 %shard_map.110 = (f32[4,320,320]{2,1,0:T(8,128)}, f32[4,320,320]{2,1,0:T(8,128)}) custom-call(f32[4,128,320]{2,1,0:T(8,128)S(1)} %get-tuple-element.30.partial, f32[4,128,320]{2,1,0:T(8,128)S(1)} %get-tuple-element.31.image_in, f32[4,128,320]{2,1,0:T(8,128)S(1)} %get-tuple-element.32.speed, ...), custom_call_target="tpu_custom_call", output_to_operand_aliasing={{0}: (6, {}), {1}: (7, {})} | custom-call | tf_op jit(solution)/shard_map/pallas_call | solution.py:578
Async XLA Ops:
  0.6 2.0 %copy-start = (bf16[64,2048]{1,0:T(8,128)(2,1)S(1)}, bf16[64,2048]{1,0:T(8,128)(2,1)}, u32[]{:S(2)}) copy-start(bf16[64,2048]{1,0:T(8,128)(2,1)} %traces) | copy-start | bytes 786436
  0.6 2.0 %copy-start.3 = (s32[64]{0:T(128)S(1)}, s32[64]{0:T(128)}, u32[]{:S(2)}) copy-start(s32[64]{0:T(128)} %param.15) | copy-start | bytes 772
  0.7 2.0 %copy-start.2 = (s32[64,1]{0,1:T(1,128)S(1)}, s32[64,1]{0,1:T(1,128)}, u32[]{:S(2)}) copy-start(s32[64,1]{0,1:T(1,128)} %param.14) | copy-start | bytes 772
  0.7 2.0 %copy-start.1 = (bf16[2,2048]{1,0:T(2,128)(2,1)S(1)}, bf16[2,2048]{1,0:T(2,128)(2,1)}, u32[]{:S(2)}) copy-start(bf16[2,2048]{1,0:T(2,128)(2,1)} %weights.1) | copy-start | bytes 24580
  5.9 23.3 %collective-permute-start = (bf16[320,1280]{1,0:T(8,128)(2,1)S(1)}, bf16[320,1280]{1,0:T(8,128)(2,1)S(1)}, u32[]{:S(2)}, u32[]{:S(2)}) collective-permute-start(bf16[320,1280]{1,0:T(8,128)(2,1)S(1)} %get-tuple-element.25), channel_id=1, source_target_pairs={{0,1},{1,0},{2,3},{3,2},{4,5},{5,4},{6,7},{7,6},{8,9},{9,8},{10,11... | collective-permute-start | bytes 2457608 | tf_op jit(solution)/shard_map/ppermute | solution.py:514
  6.6 22.6 %collective-permute-start.1 = (bf16[192,1280]{1,0:T(8,128)(2,1)S(1)}, bf16[192,1280]{1,0:T(8,128)(2,1)S(1)}, u32[]{:S(2)}, u32[]{:S(2)}) collective-permute-start(bf16[192,1280]{1,0:T(8,128)(2,1)S(1)} %shard_map.103), channel_id=1, source_target_pairs={{1,2},{2,1},{3,4},{4,3},{5,6},{6,5},{7,8},{8,7},{9,10},{10,9},{11,... | collective-permute-start | bytes 1474568 | tf_op jit(solution)/shard_map/ppermute | solution.py:514
  9.7 30.2 %collective-permute-start.2 = (bf16[128,1280]{1,0:T(8,128)(2,1)S(1)}, bf16[128,1280]{1,0:T(8,128)(2,1)S(1)}, u32[]{:S(2)}, u32[]{:S(2)}) collective-permute-start(bf16[128,1280]{1,0:T(8,128)(2,1)S(1)} %get-tuple-element.28), channel_id=1, source_target_pairs={{1,2},{2,1},{3,4},{4,3},{5,6},{6,5},{7,8},{8,7},{9,10},{10,9},{11,... | collective-permute-start | bytes 983048 | tf_op jit(solution)/shard_map/ppermute | solution.py:514
  36.7 16.8 %collective-permute-start.5 = (bf16[192,1280]{1,0:T(8,128)(2,1)S(1)}, bf16[192,1280]{1,0:T(8,128)(2,1)S(1)}, u32[]{:S(2)}, u32[]{:S(2)}) collective-permute-start(bf16[192,1280]{1,0:T(8,128)(2,1)S(1)} %get-tuple-element.36), channel_id=1, source_target_pairs={{0,1},{1,0},{2,3},{3,2},{4,5},{5,4},{6,7},{7,6},{8,9},{9,8},{10,11... | collective-permute-start | bytes 1474568 | tf_op jit(solution)/shard_map/ppermute | solution.py:514
  37.4 18.9 %collective-permute-start.6 = (bf16[192,1280]{1,0:T(8,128)(2,1)S(1)}, bf16[192,1280]{1,0:T(8,128)(2,1)S(1)}, u32[]{:S(2)}, u32[]{:S(2)}) collective-permute-start(bf16[192,1280]{1,0:T(8,128)(2,1)S(1)} %get-tuple-element.37), channel_id=1, source_target_pairs={{1,2},{2,1},{3,4},{4,3},{5,6},{6,5},{7,8},{8,7},{9,10},{10,9},{11,... | collective-permute-start | bytes 1474568 | tf_op jit(solution)/shard_map/ppermute | solution.py:514
  45.6 17.3 %collective-permute-start.3 = (bf16[128,1280]{1,0:T(8,128)(2,1)S(1)}, bf16[128,1280]{1,0:T(8,128)(2,1)S(1)}, u32[]{:S(2)}, u32[]{:S(2)}) collective-permute-start(bf16[128,1280]{1,0:T(8,128)(2,1)S(1)} %get-tuple-element.34), channel_id=1, source_target_pairs={{0,1},{1,0},{2,3},{3,2},{4,5},{5,4},{6,7},{7,6},{8,9},{9,8},{10,11... | collective-permute-start | bytes 983048 | tf_op jit(solution)/shard_map/ppermute | solution.py:514
  46.0 16.8 %collective-permute-start.4 = (bf16[128,1280]{1,0:T(8,128)(2,1)S(1)}, bf16[128,1280]{1,0:T(8,128)(2,1)S(1)}, u32[]{:S(2)}, u32[]{:S(2)}) collective-permute-start(bf16[128,1280]{1,0:T(8,128)(2,1)S(1)} %get-tuple-element.35), channel_id=1, source_target_pairs={{1,2},{2,1},{3,4},{4,3},{5,6},{6,5},{7,8},{8,7},{9,10},{10,9},{11,... | collective-permute-start | bytes 983048 | tf_op jit(solution)/shard_map/ppermute | solution.py:514

commit v6 on v5

--- a/solution.py
+++ b/solution.py
@@ -15,7 +15,6 @@
 ROWS = 16
 BLOCK = 32
 SUB = 8
-UNROLL = 4
 SHARE = (3, 2)
 LANES = 128
 F32 = jnp.float32
@@ -133,27 +132,35 @@
     return copies
 
 
-def pack_kernel(first, with_on, now, *refs):
-    refs = list(refs)
-    on_ref = refs.pop(0) if with_on else None
-    off_ref, buf, sems = refs
+def pack_kernel(first, now, off_ref, buf, sems):
     depth = now.shape[0]
-    base = 0 if with_on else first
-    copies = fetch(now, buf, sems, base, buf.shape[1])
-
-    for i, copy in enumerate(copies):
+    count = off_ref.shape[0]
+    copies = fetch(now, buf, sems, first, count)
+    for copy, (row, size) in zip(copies, blocks_of(0, count)):
         copy.wait()
 
         def body(r):
-            r = r + i * BLOCK
-            rows = pl.ds(r, ROWS)
+            rows = pl.ds(r + row, ROWS)
             u = [buf[depth_at(j, depth), rows, :] for j in range(depth)]
-            if base + i * BLOCK >= first and base + i * BLOCK < first + off_ref.shape[0]:
-                put(off_ref, pl.ds(r + base - first, ROWS), encode(u[::-1][:HALO]))
-            if with_on:
-                put(on_ref, rows, encode(u[:HALO]))
-
-        row_loop(BLOCK, body)
+            put(off_ref, rows, encode(u[::-1][:HALO]))
+
+        row_loop(size, body)
+
+
+def pack_all_kernel(first, now, on_ref, off_ref, field, sems):
+    depth, width_x, _ = now.shape
+    copies = fetch(now, field, sems, 0, width_x)
+    for copy, (row, size) in zip(copies, blocks_of(0, width_x)):
+        copy.wait()
+
+        def body(r):
+            rows = pl.ds(r + row, ROWS)
+            u = [field[depth_at(j, depth), rows, :] for j in range(depth)]
+            if row >= first:
+                put(off_ref, pl.ds(r + (row - first), ROWS), encode(u[::-1][:HALO]))
+            put(on_ref, rows, encode(u[:HALO]))
+
+        row_loop(size, body)
 
 
 def route_kernel(slabs, field, traces, weights, target, cell, out):
@@ -227,12 +234,10 @@
             tiles[tile_rows(z, row, j, count, number), :] = jnp.zeros((SUB, LANES), F32)
 
 
-def own_laplace(tiles, lap, depth, count, width_y):
+def add_laplace(tiles, lap, depth, count, width_y, first):
     number = len(tile_parts(width_y))
     lane = lax.broadcasted_iota(jnp.int32, (SUB, LANES), 1)
     wraps = width_y % LANES == 0 or width_y % LANES > LANES - HALO
-    groups = count // SUB
-    unroll = max(u for u in range(1, UNROLL + 1) if groups % u == 0)
 
     def one(r):
         def at(z, j, shift=0):
@@ -240,7 +245,10 @@
 
         centre = [[at(z, j) for j in range(number)] for z in range(depth)]
         for z in range(depth):
-            total = [3.0 * W[0] * centre[z][j] for j in range(number)]
+            places = [
+                pl.ds(pl.multiple_of(r + (j * depth + z) * count, SUB), SUB) for j in range(number)
+            ]
+            total = [lap[places[j], :] + 3.0 * W[0] * centre[z][j] for j in range(number)]
             for k in range(1, HALO + 1):
                 right = [pltpu.roll(c, k, 1) for c in centre[z]]
                 left = [pltpu.roll(c, LANES - k, 1) for c in centre[z]]
@@ -258,15 +266,34 @@
                         pair = pair + centre[z + k][j]
                     total[j] = total[j] + W[k] * pair
             for j in range(number):
-                place = pl.multiple_of(r + (j * depth + z) * count, SUB)
-                lap[pl.ds(place, SUB), :] = total[j]
+                lap[places[j], :] = total[j]
+
+    for u in range(0, ROWS, SUB):
+        one(first + u)
+
+
+def stream(count, stencil, finish):
+    stencil(0)
 
     def step(i, carry):
-        for u in range(unroll):
-            one((i * unroll + u) * SUB)
+        r = pl.multiple_of(i * ROWS, ROWS)
+        finish(r)
+        stencil(r + ROWS)
         return carry
 
-    lax.fori_loop(0, groups // unroll, step, 0)
+    lax.fori_loop(0, count // ROWS - 1, step, 0)
+    finish(count - ROWS)
+
+
+def blank(lap):
+    def body(i, carry):
+        lap[pl.ds(pl.multiple_of(i * 8 * SUB, SUB), 8 * SUB), :] = jnp.zeros((8 * SUB, LANES), F32)
+        return carry
+
+    whole = lap.shape[0] // (8 * SUB)
+    lax.fori_loop(0, whole, body, 0)
+    rest = lap.shape[0] - whole * 8 * SUB
+    lap[whole * 8 * SUB :, :] = jnp.zeros((rest, LANES), F32)
 
 
 def inject(step, got, lap, planes, first, count, width_x):
@@ -309,90 +336,81 @@
     return out
 
 
-def first_kernel(
-    first, now, prior, velocity, got, got_on, got_off, part, on_ref, off_ref,
-    tiles, lap, now_buf, prior_buf, speed_buf, sems
-):
-    depth, width_x, width_y = now.shape
-    count = part.shape[1]
+def prepare(step, first, count, sources, got, tiles, lap):
+    depth, _, width_y = sources[0][1].shape
+    width_x = sum(source.shape[1] for _, source in sources)
     number = len(tile_parts(width_y))
     low, high = max(first - SUB, 0), min(first + count + SUB, width_x)
-    now_copies = fetch(now, now_buf, sems.at[0], low, high - low)
-    prior_copies = fetch(prior, prior_buf, sems.at[1], first, count)
-    speed_copies = fetch(velocity, speed_buf, sems.at[2], first, count)
+    blank(lap)
     if low == first:
         clear(tiles, count, depth, number, -SUB)
     if high == first + count:
         clear(tiles, count, depth, number, count)
-    for copy, (row, size) in zip(now_copies, blocks_of(low, high - low)):
+    for start, source in sources:
+        row, end = max(low, start), min(high, start + source.shape[1])
+        spread(tiles, count, source, row - start, row - first, end - row)
+    inject(step, got, lap, number * depth, first, count, width_x)
+
+
+def first_kernel(
+    first, now, prior, velocity, got, got_on, got_off, part, on_ref, off_ref,
+    tiles, lap, prior_buf, speed_buf, sems
+):
+    depth, count, width_y = part.shape
+    copies = fetch(prior, prior_buf, sems.at[0], first, count)
+    copies += fetch(velocity, speed_buf, sems.at[1], first, count)
+    prepare(0, first, count, ((0, now),), got, tiles, lap)
+    for copy in copies:
         copy.wait()
-        spread(tiles, count, now_buf, row - low, row - first, size)
-    own_laplace(tiles, lap, depth, count, width_y)
-    inject(0, got, lap, number * depth, first, count, width_x)
-    for copy in prior_copies + speed_copies:
-        copy.wait()
-
-    def body(r):
+
+    def finish(r):
         rows = pl.ds(r, ROWS)
-        here = pl.ds(pl.multiple_of(r + (first - low), SUB), ROWS)
-        halo = halo_sum(got_on, pl.ds(r + first, ROWS), got_off, rows, width_y, depth)
+        whole = pl.ds(r + first, ROWS)
+        halo = halo_sum(got_on, whole, got_off, rows, width_y, depth)
         u = []
         for j in range(depth):
             z = depth_at(j, depth)
             change = lap_rows(lap, z, r, depth, count, width_y)
             if halo[j] is not None:
                 change = change + halo[j]
-            value = 2.0 * now_buf[z, here, :] - prior_buf[z, rows, :]
+            value = 2.0 * now[z, whole, :] - prior_buf[z, rows, :]
             value = value + speed_buf[z, rows, :] * change
             part[z, rows, :] = value
             u.append(value)
         put(off_ref, rows, encode(u[::-1][:HALO]))
         put(on_ref, rows, encode(u[:HALO]))
 
-    row_loop(count, body)
-
-
-def second_local(first, starts, parts, now, velocity, forward, got, tiles, lap, bufs, sems):
-    now_buf, speed_buf, *forward_bufs = bufs
-    depth, width_x, width_y = now.shape
-    count = now_buf.shape[1]
-    number = len(tile_parts(width_y))
-    low, high = max(first - SUB, 0), min(first + count + SUB, width_x)
-    copies = fetch(now, now_buf, sems.at[0], first, count)
-    copies += fetch(velocity, speed_buf, sems.at[1], first, count)
-    for s in range(STEPS):
-        copies += fetch(forward.at[s], forward_bufs[s], sems.at[2 + s], first, count)
-    if low == first:
-        clear(tiles, count, depth, number, -SUB)
-    if high == first + count:
-        clear(tiles, count, depth, number, count)
-    for start, part in zip(starts, parts):
-        row, end = max(low, start), min(high, start + part.shape[1])
-        spread(tiles, count, part, row - start, row - first, end - row)
-    own_laplace(tiles, lap, depth, count, width_y)
-    inject(1, got, lap, number * depth, first, count, width_x)
-    for copy in copies:
-        copy.wait()
-    return parts[starts.index(first)]
-
-
-def send_rows(pairs, first, row, sems, n):
-    writes = []
-    for k, (buf, target) in enumerate(pairs):
-        write = pltpu.make_async_copy(
-            buf.at[:, pl.ds(row, BLOCK)], target.at[:, pl.ds(first + row, BLOCK)], sems.at[k, n]
+    stream(count, lambda r: add_laplace(tiles, lap, depth, count, width_y, r), finish)
+
+
+def second_fetch(first, velocity, forward, speed_buf, early, late, sems):
+    count = speed_buf.shape[1]
+    copies = fetch(velocity, speed_buf, sems.at[0], first, count)
+    copies += fetch(forward.at[0], early, sems.at[1], first, count)
+    return copies + fetch(forward.at[1], late, sems.at[2], first, count)
+
+
+def send_rows(pairs, first, r, sems):
+    return [
+        pltpu.make_async_copy(
+            buf.at[:, pl.ds(r, ROWS)], target.at[:, pl.ds(r + first, ROWS)], sems.at[k, r // ROWS]
         )
-        write.start()
-        writes.append(write)
-    return writes
+        for k, (buf, target) in enumerate(pairs)
+    ]
+
+
+def await_rows(pairs, first, count, sems):
+    for r in range(0, count, ROWS):
+        for write in send_rows(pairs, first, r, sems):
+            write.wait()
 
 
 def second_kernel(first, starts, *refs):
     parts, refs = refs[: len(starts)], refs[len(starts) :]
     now, velocity, forward, got, got_on, got_off, out, image, current, tiles, lap = refs[:11]
-    *bufs, out_buf, image_buf, sems, out_sems, part_sems = refs[11:]
-    depth, _, width_y = now.shape
-    count = out_buf.shape[1]
+    speed, early, late, out_buf, image_buf, sems, out_sems, part_sems = refs[11:]
+    depth, count, width_y = out_buf.shape
+    copies = second_fetch(first, velocity, forward, speed, early, late, sems)
     writes = []
     for i, (start, part) in enumerate(zip(starts, parts)):
         write = pltpu.make_async_copy(
@@ -400,69 +418,73 @@
         )
         write.start()
         writes.append(write)
-    here = second_local(first, starts, parts, now, velocity, forward, got, tiles, lap, bufs, sems)
-    now_buf, speed_buf, early, late = bufs
-    for n, i in enumerate(range(0, count, BLOCK)):
-
-        def body(r):
-            r = r + i
-            rows = pl.ds(r, ROWS)
-            halo = halo_sum(got_on, rows, got_off, rows, width_y, depth)
-            for j in range(depth):
-                z = depth_at(j, depth)
-                change = lap_rows(lap, z, r, depth, count, width_y)
-                if halo[j] is not None:
-                    change = change + halo[j]
-                mine = here[z, rows, :]
-                value = 2.0 * mine - now_buf[z, rows, :] + speed_buf[z, rows, :] * change
-                out_buf[z, rows, :] = value
-                image_buf[z, rows, :] = early[z, rows, :] * mine + late[z, rows, :] * value
-
-        row_loop(BLOCK, body)
-        writes += send_rows(((out_buf, out), (image_buf, image)), first, i, out_sems, n)
+    prepare(1, first, count, tuple(zip(starts, parts)), got, tiles, lap)
+    for copy in copies:
+        copy.wait()
+    here = parts[starts.index(first)]
+    pairs = ((out_buf, out), (image_buf, image))
+
+    def finish(r):
+        rows = pl.ds(r, ROWS)
+        halo = halo_sum(got_on, rows, got_off, rows, width_y, depth)
+        for j in range(depth):
+            z = depth_at(j, depth)
+            change = lap_rows(lap, z, r, depth, count, width_y)
+            if halo[j] is not None:
+                change = change + halo[j]
+            mine = here[z, rows, :]
+            value = 2.0 * mine - now[z, pl.ds(r + first, ROWS), :] + speed[z, rows, :] * change
+            out_buf[z, rows, :] = value
+            image_buf[z, rows, :] = early[z, rows, :] * mine + late[z, rows, :] * value
+        for write in send_rows(pairs, first, r, out_sems):
+            write.start()
+
+    stream(count, lambda r: add_laplace(tiles, lap, depth, count, width_y, r), finish)
+    await_rows(pairs, first, count, out_sems)
     for write in writes:
         write.wait()
 
 
 def partial_kernel(first, starts, *refs):
     parts, refs = refs[: len(starts)], refs[len(starts) :]
-    now, velocity, forward, got, out, image, speed, late, tiles, lap, now_buf, early, sems = refs
-    depth, _, width_y = now.shape
-    count = now_buf.shape[1]
-    bufs = (now_buf, speed, early, late)
-    here = second_local(first, starts, parts, now, velocity, forward, got, tiles, lap, bufs, sems)
-
-    def body(r):
+    now, velocity, forward, got, out, image, speed, late, tiles, lap, early, sems = refs
+    depth, count, width_y = out.shape
+    copies = second_fetch(first, velocity, forward, speed, early, late, sems)
+    prepare(1, first, count, tuple(zip(starts, parts)), got, tiles, lap)
+    for copy in copies:
+        copy.wait()
+    here = parts[starts.index(first)]
+
+    def finish(r):
         rows = pl.ds(r, ROWS)
         for z in range(depth):
             change = lap_rows(lap, z, r, depth, count, width_y)
             mine = here[z, rows, :]
-            value = 2.0 * mine - now_buf[z, rows, :] + speed[z, rows, :] * change
+            value = 2.0 * mine - now[z, pl.ds(r + first, ROWS), :] + speed[z, rows, :] * change
             out[z, rows, :] = value
             image[z, rows, :] = early[z, rows, :] * mine + late[z, rows, :] * value
 
-    row_loop(count, body)
+    stream(count, lambda r: add_laplace(tiles, lap, depth, count, width_y, r), finish)
 
 
 def last_kernel(first, partial, image_in, speed, late, got_on, got_off, *refs):
     out, image, out_buf, image_buf, sems = refs[-5:]
     depth, count, width_y = out_buf.shape
-    writes = []
-    for n, i in enumerate(range(0, count, BLOCK)):
-
-        def body(r):
-            rows = pl.ds(r + i, ROWS)
-            halo = halo_sum(got_on, rows, got_off, rows, width_y, depth)
-            for j in range(depth):
-                z = depth_at(j, depth)
-                extra = speed[z, rows, :] * halo[j] if halo[j] is not None else 0.0
-                out_buf[z, rows, :] = partial[z, rows, :] + extra
-                image_buf[z, rows, :] = image_in[z, rows, :] + late[z, rows, :] * extra
-
-        row_loop(BLOCK, body)
-        writes += send_rows(((out_buf, out), (image_buf, image)), first, i, sems, n)
-    for write in writes:
-        write.wait()
+    pairs = ((out_buf, out), (image_buf, image))
+
+    def body(r):
+        rows = pl.ds(r, ROWS)
+        halo = halo_sum(got_on, rows, got_off, rows, width_y, depth)
+        for j in range(depth):
+            z = depth_at(j, depth)
+            extra = speed[z, rows, :] * halo[j] if halo[j] is not None else 0.0
+            out_buf[z, rows, :] = partial[z, rows, :] + extra
+            image_buf[z, rows, :] = image_in[z, rows, :] + late[z, rows, :] * extra
+        for write in send_rows(pairs, first, r, sems):
+            write.start()
+
+    row_loop(count, body)
+    await_rows(pairs, first, count, sems)
 
 
 def shard(now, prior, velocity, forward, traces, weights, target, cell):
@@ -515,7 +537,7 @@
 
     got_off = []
     (face,) = call(
-        functools.partial(pack_kernel, 0, False),
+        functools.partial(pack_kernel, 0),
         [HBM],
         [plane(split)],
         (buffer(split), dma((blocks(split),))),
@@ -529,11 +551,11 @@
     )(traces, weights, target.reshape(1, rows), cell.reshape(1, rows))
     got = lax.all_to_all(sent, "slab", split_axis=0, concat_axis=0, tiled=True)
     sent, later = lax.optimization_barrier((sent, now))
-    on_face, face = call(
-        functools.partial(pack_kernel, split, True),
+    on_face, face, now = call(
+        functools.partial(pack_all_kernel, split),
         [HBM],
-        [plane(width_x), plane(width_x - split)],
-        (buffer(width_x), dma((blocks(width_x),))),
+        [plane(width_x), plane(width_x - split), field],
+        (dma((blocks(width_x),)),),
     )(later)
     got_off.append(swap(face, off_pairs))
     got_on = swap(on_face, on_pairs)
@@ -541,15 +563,9 @@
     for (first, count), got_face in zip(chunks, got_off):
         part, on_face, face = call(
             functools.partial(first_kernel, first),
-            [HBM] * 3 + [SMEM, VMEM, VMEM],
+            [VMEM, HBM, HBM, SMEM, VMEM, VMEM],
             [rows_of(count), plane(count), plane(count)],
-            (
-                *stencil(count),
-                buffer(count + 2 * SUB),
-                buffer(count),
-                buffer(count),
-                dma((3, blocks(count + 2 * SUB))),
-            ),
+            (*stencil(count), buffer(count), buffer(count), dma((2, blocks(count)))),
         )(now, prior, velocity, got, got_on, got_face)
         second_off.append(swap(face, off_pairs))
         second_on.append(swap(on_face, on_pairs))
@@ -558,28 +574,28 @@
     (first, count), (last, size) = chunks
     second, image, current = call(
         functools.partial(second_kernel, first, starts),
-        [VMEM] * len(parts) + [HBM] * 3 + [SMEM, VMEM, VMEM],
+        [VMEM] * (len(parts) + 1) + [HBM] * 2 + [SMEM, VMEM, VMEM],
         [field, field, field],
         (
             *stencil(count),
-            *[buffer(count)] * 6,
-            dma((2 + STEPS, blocks(count))),
-            dma((2, blocks(count))),
+            *[buffer(count)] * 5,
+            dma((3, blocks(count))),
+            dma((2, count // ROWS)),
             dma((len(parts),)),
         ),
         [HBM] * 3,
     )(*parts, now, velocity, forward, got, second_on[0], second_off[0])
     partial, image_part, speed, late = call(
         functools.partial(partial_kernel, last, starts),
-        [VMEM] * len(parts) + [HBM] * 3 + [SMEM],
+        [VMEM] * (len(parts) + 1) + [HBM] * 2 + [SMEM],
         [rows_of(size)] * 4,
-        (*stencil(size), buffer(size), buffer(size), dma((2 + STEPS, blocks(size)))),
+        (*stencil(size), buffer(size), dma((3, blocks(size)))),
     )(*parts, now, velocity, forward, got)
     second, image = call(
         functools.partial(last_kernel, last),
         [VMEM] * 6 + [HBM] * 2,
         [field, field],
-        (buffer(size), buffer(size), dma((2, blocks(size)))),
+        (buffer(size), buffer(size), dma((2, size // ROWS))),
         [HBM] * 2,
         input_output_aliases={6: 0, 7: 1},
     )(partial, image_part, speed, late, second_on[1], second_off[1], second, image)

time: 64.8 us -> 65.1 us (level)
  transfers between devices with their start and end apart: 7 -> 7, of which waited for: 1 -> 1; matrix products, arithmetic and copies ran while one was open for 0% -> 0% of each run, Pallas kernels for 36% -> 37%
where the time goes in v6:
time: 65.1 us; the launch traced here: 64.8 us
  Pallas kernels  30.6 us (47%)
  blocking collectives  17 us (26%)
  starting transfers between devices  13.6 us (21%)
  waiting for transfers between devices  2.74 us (4%)
  between operations  0.81 us (1%)
    all_to_all x1, blocking collectives, shard(): got = lax.all_to_all(sent, 'slab', split_axis=0, concat_axis=0, tiled=True)  17 us
    ppermute x7, starting transfers between devices, swap(): return lax.ppermute(face, 'slab', pairs)  13.6 us
    pallas_call x2, Pallas kernels, shard(): call(functools.partial(first_kernel, first), [VMEM, HBM, HBM, SMEM, VMEM,...  11 us
    pallas_call x1, Pallas kernels, shard(): call(functools.partial(second_kernel, first, starts), [VMEM] * (len(parts...  8.1 us
    pallas_call x1, Pallas kernels, shard(): call(functools.partial(partial_kernel, last, starts), [VMEM] * (len(parts...  4.73 us
    pallas_call x1, Pallas kernels, shard(): call(functools.partial(pack_all_kernel, split), [HBM], [plane(width_x), p...  2.78 us
    ppermute x7, waiting for transfers between devices, swap(): return lax.ppermute(face, 'slab', pairs)  2.74 us
    pallas_call x1, Pallas kernels, shard(): call(functools.partial(pack_kernel, 0), [HBM], [plane(split)], (buffer(sp...  1.99 us
  transfers between devices with their start and end apart: 7, of which 1 were waited for; matrix products, arithmetic and copies ran while one was open for 0% of the time, Pallas kernels for 37%

profile of v6, /device:TPU:9, one launch (start us, length us, event | category | flops | bytes accessed | tf_op | source)
XLA Modules:
  0.0 64.8 jit_solution(12473877478226880906)
XLA Ops:
  0.6 0.0 copy-start
  0.6 0.0 copy-start.2
  0.7 0.0 copy-start.3
  0.7 0.0 copy-start.1
  0.7 2.0 %shard_map.103 = bf16[192,1280]{1,0:T(8,128)(2,1)S(1)} custom-call(f32[4,320,320]{2,1,0:T(8,128)} %now.2), custom_call_target="tpu_custom_call" | custom-call | tf_op jit(solution)/shard_map/pallas_call | solution.py:539
  2.7 0.0 copy-done
  2.7 0.0 copy-done.2
  2.7 0.0 copy-done.3
  2.7 0.0 copy-done.1
  2.7 0.4 shard_map.104
  3.1 2.8 %shard_map.105 = (bf16[320,1280]{1,0:T(8,128)(2,1)S(1)}, bf16[128,1280]{1,0:T(8,128)(2,1)S(1)}, f32[4,320,320]{2,1,0:T(8,128)S(1)}) custom-call(f32[4,320,320]{2,1,0:T(8,128)} %now.2), custom_call_target="tpu_custom_call" | custom-call | tf_op jit(solution)/shard_map/pallas_call | solution.py:554
  5.9 0.7 %collective-permute-start = (bf16[320,1280]{1,0:T(8,128)(2,1)S(1)}, bf16[320,1280]{1,0:T(8,128)(2,1)S(1)}, u32[]{:S(2)}, u32[]{:S(2)}) collective-permute-start(bf16[320,1280]{1,0:T(8,128)(2,1)S(1)} %get-tuple-element.27), channel_id=1, source_target_pairs={{0,1},{1,0},{2,3},{3,2},{4,5},{5,4},{6,7},{7,6},{8,9},{9,8},{10,11... | collective-permute-start | bytes 2457608 | tf_op jit(solution)/shard_map/ppermute | solution.py:536
  6.6 3.0 %collective-permute-start.1 = (bf16[192,1280]{1,0:T(8,128)(2,1)S(1)}, bf16[192,1280]{1,0:T(8,128)(2,1)S(1)}, u32[]{:S(2)}, u32[]{:S(2)}) collective-permute-start(bf16[192,1280]{1,0:T(8,128)(2,1)S(1)} %shard_map.103), channel_id=1, source_target_pairs={{1,2},{2,1},{3,4},{4,3},{5,6},{6,5},{7,8},{8,7},{9,10},{10,9},{11,... | collective-permute-start | bytes 1474568 | tf_op jit(solution)/shard_map/ppermute | solution.py:536
  9.7 2.5 %collective-permute-start.2 = (bf16[128,1280]{1,0:T(8,128)(2,1)S(1)}, bf16[128,1280]{1,0:T(8,128)(2,1)S(1)}, u32[]{:S(2)}, u32[]{:S(2)}) collective-permute-start(bf16[128,1280]{1,0:T(8,128)(2,1)S(1)} %get-tuple-element.30), channel_id=1, source_target_pairs={{1,2},{2,1},{3,4},{4,3},{5,6},{6,5},{7,8},{8,7},{9,10},{10,9},{11,... | collective-permute-start | bytes 983048 | tf_op jit(solution)/shard_map/ppermute | solution.py:536
  12.2 17.0 %all_to_all.5.got.refs_5_ = f32[16,1,128]{2,1,0:T(1,128)S(1)} all-to-all(f32[16,1,128]{2,1,0:T(1,128)S(1)} %shard_map.104), channel_id=1, replica_groups=mesh['groups'=2,'slab'=16] {'slab'}, dimensions={0} | all-to-all | bytes 16384 | tf_op jit(solution)/shard_map/all_to_all | solution.py:552
  29.2 0.0 collective-permute-done.1.got_off
  29.2 0.0 collective-permute-done.got_on
  29.2 6.2 %shard_map.106 = (f32[4,192,320]{2,1,0:T(8,128)S(1)}, bf16[192,1280]{1,0:T(8,128)(2,1)S(1)}, bf16[192,1280]{1,0:T(8,128)(2,1)S(1)}) custom-call(f32[4,320,320]{2,1,0:T(8,128)S(1)} %get-tuple-element.26.now.refs_2_, f32[4,320,320]{2,1,0:T(8,128)} %prior.2, f32[4,320,320]{2,1,0:T(8,128)} %refs_3_.3, f32[16,1,128]{2,1,0:T(1,128)S(1)} %all_to_all.5.got.refs_5_, ...), custom_call_target="tpu_custom_call" | custom-call | tf_op jit(solution)/shard_map/pallas_call | solution.py:564
  35.4 0.7 %collective-permute-start.5 = (bf16[192,1280]{1,0:T(8,128)(2,1)S(1)}, bf16[192,1280]{1,0:T(8,128)(2,1)S(1)}, u32[]{:S(2)}, u32[]{:S(2)}) collective-permute-start(bf16[192,1280]{1,0:T(8,128)(2,1)S(1)} %get-tuple-element.38), channel_id=1, source_target_pairs={{0,1},{1,0},{2,3},{3,2},{4,5},{5,4},{6,7},{7,6},{8,9},{9,8},{10,11... | collective-permute-start | bytes 1474568 | tf_op jit(solution)/shard_map/ppermute | solution.py:536
  36.1 2.5 %collective-permute-start.6 = (bf16[192,1280]{1,0:T(8,128)(2,1)S(1)}, bf16[192,1280]{1,0:T(8,128)(2,1)S(1)}, u32[]{:S(2)}, u32[]{:S(2)}) collective-permute-start(bf16[192,1280]{1,0:T(8,128)(2,1)S(1)} %get-tuple-element.39), channel_id=1, source_target_pairs={{1,2},{2,1},{3,4},{4,3},{5,6},{6,5},{7,8},{8,7},{9,10},{10,9},{11,... | collective-permute-start | bytes 1474568 | tf_op jit(solution)/shard_map/ppermute | solution.py:536
  38.6 0.0 collective-permute-done.2.got_off
  38.6 4.8 %shard_map.107 = (f32[4,128,320]{2,1,0:T(8,128)S(1)}, bf16[128,1280]{1,0:T(8,128)(2,1)S(1)}, bf16[128,1280]{1,0:T(8,128)(2,1)S(1)}) custom-call(f32[4,320,320]{2,1,0:T(8,128)S(1)} %get-tuple-element.26.now.refs_2_, f32[4,320,320]{2,1,0:T(8,128)} %prior.2, f32[4,320,320]{2,1,0:T(8,128)} %refs_3_.3, f32[16,1,128]{2,1,0:T(1,128)S(1)} %all_to_all.5.got.refs_5_, ...), custom_call_target="tpu_custom_call" | custom-call | tf_op jit(solution)/shard_map/pallas_call | solution.py:564
  43.4 0.4 collective-permute-start.3
  43.8 3.7 %collective-permute-start.4 = (bf16[128,1280]{1,0:T(8,128)(2,1)S(1)}, bf16[128,1280]{1,0:T(8,128)(2,1)S(1)}, u32[]{:S(2)}, u32[]{:S(2)}) collective-permute-start(bf16[128,1280]{1,0:T(8,128)(2,1)S(1)} %get-tuple-element.37), channel_id=1, source_target_pairs={{1,2},{2,1},{3,4},{4,3},{5,6},{6,5},{7,8},{8,7},{9,10},{10,9},{11,... | collective-permute-start | bytes 983048 | tf_op jit(solution)/shard_map/ppermute | solution.py:536
  47.6 4.7 %shard_map.108 = (f32[4,128,320]{2,1,0:T(8,128)S(1)}, f32[4,128,320]{2,1,0:T(8,128)S(1)}, f32[4,128,320]{2,1,0:T(8,128)S(1)}, f32[4,128,320]{2,1,0:T(8,128)S(1)}) custom-call(f32[4,192,320]{2,1,0:T(8,128)S(1)} %get-tuple-element.28.refs_0_, f32[4,128,320]{2,1,0:T(8,128)S(1)} %get-tuple-element.31.refs_1_, f32[4,320,320]{2,1,0:T(8,128)S(1)} %get-tuple-element.26.now.refs_2_, ...), custom_call_target="tpu_custom_call" | custom-call | tf_op jit(solution)/shard_map/pallas_call | solution.py:588
  52.3 0.0 collective-permute-done.5.refs_6_
  52.3 2.7 %collective-permute-done.6.refs_7_ = bf16[192,1280]{1,0:T(8,128)(2,1)S(1)} collective-permute-done((bf16[192,1280]{1,0:T(8,128)(2,1)S(1)}, bf16[192,1280]{1,0:T(8,128)(2,1)S(1)}, u32[]{:S(2)}, u32[]{:S(2)}) %collective-permute-start.6) | collective-permute-done | bytes 491552 | tf_op jit(solution)/shard_map/ppermute | solution.py:536
  55.0 8.1 %shard_map.109 = (f32[4,320,320]{2,1,0:T(8,128)}, f32[4,320,320]{2,1,0:T(8,128)}, f32[4,320,320]{2,1,0:T(8,128)}) custom-call(f32[4,192,320]{2,1,0:T(8,128)S(1)} %get-tuple-element.28.refs_0_, f32[4,128,320]{2,1,0:T(8,128)S(1)} %get-tuple-element.31.refs_1_, f32[4,320,320]{2,1,0:T(8,128)S(1)} %get-tuple-element.26.now.refs_2_, f32[4,320,320]{2,1,0:T(8,128)} %refs_3_.3, ...), custom_call_target="tpu_custom_call" | custom-call | tf_op jit(solution)/shard_map/pallas_call | solution.py:575
  63.1 0.0 collective-permute-done.3.got_on
  63.1 0.0 collective-permute-done.4.got_off
  63.2 1.6 %shard_map.110 = (f32[4,320,320]{2,1,0:T(8,128)}, f32[4,320,320]{2,1,0:T(8,128)}) custom-call(f32[4,128,320]{2,1,0:T(8,128)S(1)} %get-tuple-element.32.partial, f32[4,128,320]{2,1,0:T(8,128)S(1)} %get-tuple-element.33.image_in, f32[4,128,320]{2,1,0:T(8,128)S(1)} %get-tuple-element.34.speed, ...), custom_call_target="tpu_custom_call", output_to_operand_aliasing={{0}: (6, {}), {1}: (7, {})} | custom-call | tf_op jit(solution)/shard_map/pallas_call | solution.py:594
Async XLA Ops:
  0.6 2.0 %copy-start = (bf16[64,2048]{1,0:T(8,128)(2,1)S(1)}, bf16[64,2048]{1,0:T(8,128)(2,1)}, u32[]{:S(2)}) copy-start(bf16[64,2048]{1,0:T(8,128)(2,1)} %traces) | copy-start | bytes 786436
  0.6 2.0 %copy-start.2 = (s32[64,1]{0,1:T(1,128)S(1)}, s32[64,1]{0,1:T(1,128)}, u32[]{:S(2)}) copy-start(s32[64,1]{0,1:T(1,128)} %param.14) | copy-start | bytes 772
  0.7 2.0 %copy-start.3 = (s32[64]{0:T(128)S(1)}, s32[64]{0:T(128)}, u32[]{:S(2)}) copy-start(s32[64]{0:T(128)} %param.15) | copy-start | bytes 772
  0.7 2.0 %copy-start.1 = (bf16[2,2048]{1,0:T(2,128)(2,1)S(1)}, bf16[2,2048]{1,0:T(2,128)(2,1)}, u32[]{:S(2)}) copy-start(bf16[2,2048]{1,0:T(2,128)(2,1)} %weights.1) | copy-start | bytes 24580
  5.9 23.3 %collective-permute-start = (bf16[320,1280]{1,0:T(8,128)(2,1)S(1)}, bf16[320,1280]{1,0:T(8,128)(2,1)S(1)}, u32[]{:S(2)}, u32[]{:S(2)}) collective-permute-start(bf16[320,1280]{1,0:T(8,128)(2,1)S(1)} %get-tuple-element.27), channel_id=1, source_target_pairs={{0,1},{1,0},{2,3},{3,2},{4,5},{5,4},{6,7},{7,6},{8,9},{9,8},{10,11... | collective-permute-start | bytes 2457608 | tf_op jit(solution)/shard_map/ppermute | solution.py:536
  6.6 22.6 %collective-permute-start.1 = (bf16[192,1280]{1,0:T(8,128)(2,1)S(1)}, bf16[192,1280]{1,0:T(8,128)(2,1)S(1)}, u32[]{:S(2)}, u32[]{:S(2)}) collective-permute-start(bf16[192,1280]{1,0:T(8,128)(2,1)S(1)} %shard_map.103), channel_id=1, source_target_pairs={{1,2},{2,1},{3,4},{4,3},{5,6},{6,5},{7,8},{8,7},{9,10},{10,9},{11,... | collective-permute-start | bytes 1474568 | tf_op jit(solution)/shard_map/ppermute | solution.py:536
  9.7 28.9 %collective-permute-start.2 = (bf16[128,1280]{1,0:T(8,128)(2,1)S(1)}, bf16[128,1280]{1,0:T(8,128)(2,1)S(1)}, u32[]{:S(2)}, u32[]{:S(2)}) collective-permute-start(bf16[128,1280]{1,0:T(8,128)(2,1)S(1)} %get-tuple-element.30), channel_id=1, source_target_pairs={{1,2},{2,1},{3,4},{4,3},{5,6},{6,5},{7,8},{8,7},{9,10},{10,9},{11,... | collective-permute-start | bytes 983048 | tf_op jit(solution)/shard_map/ppermute | solution.py:536
  35.4 16.8 %collective-permute-start.5 = (bf16[192,1280]{1,0:T(8,128)(2,1)S(1)}, bf16[192,1280]{1,0:T(8,128)(2,1)S(1)}, u32[]{:S(2)}, u32[]{:S(2)}) collective-permute-start(bf16[192,1280]{1,0:T(8,128)(2,1)S(1)} %get-tuple-element.38), channel_id=1, source_target_pairs={{0,1},{1,0},{2,3},{3,2},{4,5},{5,4},{6,7},{7,6},{8,9},{9,8},{10,11... | collective-permute-start | bytes 1474568 | tf_op jit(solution)/shard_map/ppermute | solution.py:536
  36.1 18.9 %collective-permute-start.6 = (bf16[192,1280]{1,0:T(8,128)(2,1)S(1)}, bf16[192,1280]{1,0:T(8,128)(2,1)S(1)}, u32[]{:S(2)}, u32[]{:S(2)}) collective-permute-start(bf16[192,1280]{1,0:T(8,128)(2,1)S(1)} %get-tuple-element.39), channel_id=1, source_target_pairs={{1,2},{2,1},{3,4},{4,3},{5,6},{6,5},{7,8},{8,7},{9,10},{10,9},{11,... | collective-permute-start | bytes 1474568 | tf_op jit(solution)/shard_map/ppermute | solution.py:536
  43.4 19.8 %collective-permute-start.3 = (bf16[128,1280]{1,0:T(8,128)(2,1)S(1)}, bf16[128,1280]{1,0:T(8,128)(2,1)S(1)}, u32[]{:S(2)}, u32[]{:S(2)}) collective-permute-start(bf16[128,1280]{1,0:T(8,128)(2,1)S(1)} %get-tuple-element.36), channel_id=1, source_target_pairs={{0,1},{1,0},{2,3},{3,2},{4,5},{5,4},{6,7},{7,6},{8,9},{9,8},{10,11... | collective-permute-start | bytes 983048 | tf_op jit(solution)/shard_map/ppermute | solution.py:536
  43.8 19.3 %collective-permute-start.4 = (bf16[128,1280]{1,0:T(8,128)(2,1)S(1)}, bf16[128,1280]{1,0:T(8,128)(2,1)S(1)}, u32[]{:S(2)}, u32[]{:S(2)}) collective-permute-start(bf16[128,1280]{1,0:T(8,128)(2,1)S(1)} %get-tuple-element.37), channel_id=1, source_target_pairs={{1,2},{2,1},{3,4},{4,3},{5,6},{6,5},{7,8},{8,7},{9,10},{10,9},{11,... | collective-permute-start | bytes 983048 | tf_op jit(solution)/shard_map/ppermute | solution.py:536

commit v7 on v5

--- a/solution.py
+++ b/solution.py
@@ -133,27 +133,46 @@
     return copies
 
 
-def pack_kernel(first, with_on, now, *refs):
-    refs = list(refs)
-    on_ref = refs.pop(0) if with_on else None
-    off_ref, buf, sems = refs
+def pack_kernel(first, now, off_ref, buf, sems):
     depth = now.shape[0]
-    base = 0 if with_on else first
-    copies = fetch(now, buf, sems, base, buf.shape[1])
-
-    for i, copy in enumerate(copies):
+    count = off_ref.shape[0]
+    copies = fetch(now, buf, sems, first, count)
+    for copy, (row, size) in zip(copies, blocks_of(0, count)):
         copy.wait()
 
         def body(r):
-            r = r + i * BLOCK
-            rows = pl.ds(r, ROWS)
+            rows = pl.ds(r + row, ROWS)
             u = [buf[depth_at(j, depth), rows, :] for j in range(depth)]
-            if base + i * BLOCK >= first and base + i * BLOCK < first + off_ref.shape[0]:
-                put(off_ref, pl.ds(r + base - first, ROWS), encode(u[::-1][:HALO]))
-            if with_on:
+            put(off_ref, rows, encode(u[::-1][:HALO]))
+
+        row_loop(size, body)
+
+
+def pack_both_kernel(first, now, on_ref, off_ref, buf, sems):
+    depth, width_x, _ = now.shape
+    copies = fetch(now, buf, sems, 0, width_x)
+    for copy, (row, size) in zip(copies, blocks_of(0, width_x)):
+        copy.wait()
+
+        def body(r):
+            rows = pl.ds(r + row, ROWS)
+            u = [buf[depth_at(j, depth), rows, :] for j in range(depth)]
+            if row >= first:
+                put(off_ref, pl.ds(r + (row - first), ROWS), encode(u[::-1][:HALO]))
+            else:
                 put(on_ref, rows, encode(u[:HALO]))
 
-        row_loop(BLOCK, body)
+        row_loop(size, body)
+
+
+def pack_on_kernel(field, on_ref):
+    depth = field.shape[0]
+
+    def body(r):
+        u = [field[depth_at(j, depth), pl.ds(r + SUB, ROWS), :] for j in range(depth)]
+        put(on_ref, pl.ds(r, ROWS), encode(u[:HALO]))
+
+    row_loop(on_ref.shape[0], body)
 
 
 def route_kernel(slabs, field, traces, weights, target, cell, out):
@@ -192,7 +211,7 @@
 
 
 def tile_parts(width_y):
-    return [(lo, min(lo + LANES, width_y)) for lo in range(0, width_y, LANES)]
+    return [(lo, min(lo + LANES, width_y)) for lo in range(0, width_y + HALO, LANES)]
 
 
 def join(pieces, width_y):
@@ -212,9 +231,12 @@
         r = i * SUB
         for z in range(depth):
             for j, (lo, hi) in enumerate(parts):
-                value = source[z, pl.ds(pl.multiple_of(r + start, SUB), SUB), lo:hi]
-                if hi - lo < LANES:
-                    value = jnp.pad(value, ((0, 0), (0, LANES - (hi - lo))))
+                if hi > lo:
+                    value = source[z, pl.ds(pl.multiple_of(r + start, SUB), SUB), lo:hi]
+                    if hi - lo < LANES:
+                        value = jnp.pad(value, ((0, 0), (0, LANES - (hi - lo))))
+                else:
+                    value = jnp.zeros((SUB, LANES), F32)
                 tiles[tile_rows(z, r + row, j, count, len(parts)), :] = value
         return carry
 
@@ -227,12 +249,21 @@
             tiles[tile_rows(z, row, j, count, number), :] = jnp.zeros((SUB, LANES), F32)
 
 
-def own_laplace(tiles, lap, depth, count, width_y):
+def add_laplace(tiles, lap, depth, count, width_y):
     number = len(tile_parts(width_y))
     lane = lax.broadcasted_iota(jnp.int32, (SUB, LANES), 1)
-    wraps = width_y % LANES == 0 or width_y % LANES > LANES - HALO
     groups = count // SUB
     unroll = max(u for u in range(1, UNROLL + 1) if groups % u == 0)
+    middle = 3.0 * W[0] - 2.0 * W[4]
+
+    def both(values, k):
+        right = [pltpu.roll(v, k, 1) for v in values]
+        left = [pltpu.roll(v, LANES - k, 1) for v in values]
+        return [
+            jnp.where(lane < k, right[j - 1], right[j])
+            + jnp.where(lane >= LANES - k, left[(j + 1) % number], left[j])
+            for j in range(number)
+        ]
 
     def one(r):
         def at(z, j, shift=0):
@@ -240,26 +271,25 @@
 
         centre = [[at(z, j) for j in range(number)] for z in range(depth)]
         for z in range(depth):
-            total = [3.0 * W[0] * centre[z][j] for j in range(number)]
-            for k in range(1, HALO + 1):
-                right = [pltpu.roll(c, k, 1) for c in centre[z]]
-                left = [pltpu.roll(c, LANES - k, 1) for c in centre[z]]
-                for j in range(number):
+            places = [
+                pl.ds(pl.multiple_of(r + (j * depth + z) * count, SUB), SUB) for j in range(number)
+            ]
+            once, twice = both(centre[z], 1), both(centre[z], 2)
+            inner = [
+                W[2] * centre[z][j] + W[3] * once[j] + W[4] * twice[j] for j in range(number)
+            ]
+            outer = both(inner, 2)
+            for j in range(number):
+                total = lap[places[j], :] + middle * centre[z][j]
+                total = total + (W[1] - W[3]) * once[j] + outer[j]
+                for k in range(1, HALO + 1):
                     pair = at(z, j, -k) + at(z, j, k)
-                    pair = pair + jnp.where(lane < k, right[j - 1] if j else 0.0, right[j])
-                    if j + 1 < number or wraps:
-                        side = left[j + 1] if j + 1 < number else 0.0
-                        pair = pair + jnp.where(lane >= LANES - k, side, left[j])
-                    else:
-                        pair = pair + left[j]
                     if z - k >= 0:
                         pair = pair + centre[z - k][j]
                     if z + k < depth:
                         pair = pair + centre[z + k][j]
-                    total[j] = total[j] + W[k] * pair
-            for j in range(number):
-                place = pl.multiple_of(r + (j * depth + z) * count, SUB)
-                lap[pl.ds(place, SUB), :] = total[j]
+                    total = total + W[k] * pair
+                lap[places[j], :] = total
 
     def step(i, carry):
         for u in range(unroll):
@@ -267,6 +297,17 @@
         return carry
 
     lax.fori_loop(0, groups // unroll, step, 0)
+
+
+def blank(lap):
+    def body(i, carry):
+        lap[pl.ds(pl.multiple_of(i * 8 * SUB, SUB), 8 * SUB), :] = jnp.zeros((8 * SUB, LANES), F32)
+        return carry
+
+    whole = lap.shape[0] // (8 * SUB)
+    lax.fori_loop(0, whole, body, 0)
+    rest = lap.shape[0] - whole * 8 * SUB
+    lap[whole * 8 * SUB :, :] = jnp.zeros((rest, LANES), F32)
 
 
 def inject(step, got, lap, planes, first, count, width_x):
@@ -291,7 +332,7 @@
 
 def lap_rows(lap, z, r, depth, count, width_y):
     pieces = []
-    for j in range(len(tile_parts(width_y))):
+    for j in range(-(-width_y // LANES)):
         place = pl.multiple_of((j * depth + z) * count + r, ROWS)
         pieces.append(lap[pl.ds(place, ROWS), :])
     return join(pieces, width_y)
@@ -309,40 +350,49 @@
     return out
 
 
-def first_kernel(
-    first, now, prior, velocity, got, got_on, got_off, part, on_ref, off_ref,
-    tiles, lap, now_buf, prior_buf, speed_buf, sems
-):
-    depth, width_x, width_y = now.shape
-    count = part.shape[1]
+def prepare(step, first, count, width_x, depth, width_y, got, tiles, lap):
     number = len(tile_parts(width_y))
+    blank(lap)
+    if first == 0:
+        clear(tiles, count, depth, number, -SUB)
+    if first + count == width_x:
+        clear(tiles, count, depth, number, count)
+    inject(step, got, lap, number * depth, first, count, width_x)
+
+
+def first_kernel(first, width_x, more, now, prior, velocity, got, got_on, got_off, *refs):
+    part, on_ref, off_ref = refs[:3]
+    following = refs[3] if more else None
+    tiles, lap, now_buf, prior_buf, speed_buf, sems = refs[-6:]
+    depth, count, width_y = part.shape
     low, high = max(first - SUB, 0), min(first + count + SUB, width_x)
-    now_copies = fetch(now, now_buf, sems.at[0], low, high - low)
-    prior_copies = fetch(prior, prior_buf, sems.at[1], first, count)
-    speed_copies = fetch(velocity, speed_buf, sems.at[2], first, count)
-    if low == first:
-        clear(tiles, count, depth, number, -SUB)
-    if high == first + count:
-        clear(tiles, count, depth, number, count)
+    now_copies = fetch(now, now_buf, sems.at[0], low, high - low) if more else []
+    copies = fetch(prior, prior_buf, sems.at[1], first, count)
+    copies += fetch(velocity, speed_buf, sems.at[2], first, count)
+    if more:
+        copies += fetch(now, following, sems.at[3], width_x - more, more)
+    prepare(0, first, count, width_x, depth, width_y, got, tiles, lap)
     for copy, (row, size) in zip(now_copies, blocks_of(low, high - low)):
         copy.wait()
         spread(tiles, count, now_buf, row - low, row - first, size)
-    own_laplace(tiles, lap, depth, count, width_y)
-    inject(0, got, lap, number * depth, first, count, width_x)
-    for copy in prior_copies + speed_copies:
+    held = now_buf if more else now
+    if not more:
+        spread(tiles, count, now, 0, low - first, high - low)
+    add_laplace(tiles, lap, depth, count, width_y)
+    for copy in copies:
         copy.wait()
 
     def body(r):
         rows = pl.ds(r, ROWS)
         here = pl.ds(pl.multiple_of(r + (first - low), SUB), ROWS)
-        halo = halo_sum(got_on, pl.ds(r + first, ROWS), got_off, rows, width_y, depth)
+        halo = halo_sum(got_on, rows, got_off, rows, width_y, depth)
         u = []
         for j in range(depth):
             z = depth_at(j, depth)
             change = lap_rows(lap, z, r, depth, count, width_y)
             if halo[j] is not None:
                 change = change + halo[j]
-            value = 2.0 * now_buf[z, here, :] - prior_buf[z, rows, :]
+            value = 2.0 * held[z, here, :] - prior_buf[z, rows, :]
             value = value + speed_buf[z, rows, :] * change
             part[z, rows, :] = value
             u.append(value)
@@ -356,21 +406,16 @@
     now_buf, speed_buf, *forward_bufs = bufs
     depth, width_x, width_y = now.shape
     count = now_buf.shape[1]
-    number = len(tile_parts(width_y))
     low, high = max(first - SUB, 0), min(first + count + SUB, width_x)
     copies = fetch(now, now_buf, sems.at[0], first, count)
     copies += fetch(velocity, speed_buf, sems.at[1], first, count)
     for s in range(STEPS):
         copies += fetch(forward.at[s], forward_bufs[s], sems.at[2 + s], first, count)
-    if low == first:
-        clear(tiles, count, depth, number, -SUB)
-    if high == first + count:
-        clear(tiles, count, depth, number, count)
+    prepare(1, first, count, width_x, depth, width_y, got, tiles, lap)
     for start, part in zip(starts, parts):
         row, end = max(low, start), min(high, start + part.shape[1])
         spread(tiles, count, part, row - start, row - first, end - row)
-    own_laplace(tiles, lap, depth, count, width_y)
-    inject(1, got, lap, number * depth, first, count, width_x)
+    add_laplace(tiles, lap, depth, count, width_y)
     for copy in copies:
         copy.wait()
     return parts[starts.index(first)]
@@ -515,7 +560,7 @@
 
     got_off = []
     (face,) = call(
-        functools.partial(pack_kernel, 0, False),
+        functools.partial(pack_kernel, 0),
         [HBM],
         [plane(split)],
         (buffer(split), dma((blocks(split),))),
@@ -530,31 +575,37 @@
     got = lax.all_to_all(sent, "slab", split_axis=0, concat_axis=0, tiled=True)
     sent, later = lax.optimization_barrier((sent, now))
     on_face, face = call(
-        functools.partial(pack_kernel, split, True),
+        functools.partial(pack_both_kernel, split),
         [HBM],
-        [plane(width_x), plane(width_x - split)],
+        [plane(split), plane(width_x - split)],
         (buffer(width_x), dma((blocks(width_x),))),
     )(later)
     got_off.append(swap(face, off_pairs))
     got_on = swap(on_face, on_pairs)
     parts, second_on, second_off = [], [], []
-    for (first, count), got_face in zip(chunks, got_off):
-        part, on_face, face = call(
-            functools.partial(first_kernel, first),
-            [HBM] * 3 + [SMEM, VMEM, VMEM],
-            [rows_of(count), plane(count), plane(count)],
+    more = width_x - split + SUB
+    held = now
+    for i, (first, count) in enumerate(chunks):
+        part, on_face, face, *following = call(
+            functools.partial(first_kernel, first, width_x, 0 if i else more),
+            [VMEM if i else HBM, HBM, HBM, SMEM, VMEM, VMEM],
+            [rows_of(count), plane(count), plane(count)] + ([] if i else [rows_of(more)]),
             (
                 *stencil(count),
-                buffer(count + 2 * SUB),
+                buffer(SUB if i else count + SUB),
                 buffer(count),
                 buffer(count),
-                dma((3, blocks(count + 2 * SUB))),
+                dma((4, blocks(width_x))),
             ),
-        )(now, prior, velocity, got, got_on, got_face)
+        )(held, prior, velocity, got, got_on, got_off[i])
         second_off.append(swap(face, off_pairs))
         second_on.append(swap(on_face, on_pairs))
         parts.append(part)
-        part, prior = lax.optimization_barrier((part, prior))
+        if i == 0:
+            (held,) = following
+            part, held = lax.optimization_barrier((part, held))
+            (on_face,) = call(pack_on_kernel, [VMEM], [plane(width_x - split)])(held)
+            got_on = swap(on_face, on_pairs)
     (first, count), (last, size) = chunks
     second, image, current = call(
         functools.partial(second_kernel, first, starts),

time: 64.8 us -> 65.4 us (level)
  the two profiles are of different devices: /device:TPU:9 before, /device:TPU:1 now
where the time goes in v7:
time: 65.4 us; the launch traced here: 65.1 us
  Pallas kernels  41.8 us (64%)
  starting transfers between devices  20.3 us (31%)
  waiting for transfers between devices  2.22 us (3%)
  between operations  0.84 us (1%)
    pallas_call x2, Pallas kernels, shard(): call(functools.partial(first_kernel, first, width_x, 0 if i else more), [...  17.7 us
    ppermute x8, starting transfers between devices, swap(): return lax.ppermute(face, 'slab', pairs)  14.9 us
    pallas_call x1, Pallas kernels, shard(): call(functools.partial(second_kernel, first, starts), [VMEM] * len(parts)...  10.1 us
    pallas_call x1, Pallas kernels, shard(): call(functools.partial(partial_kernel, last, starts), [VMEM] * len(parts)...  6.09 us
    all_to_all x1, starting transfers between devices, shard(): got = lax.all_to_all(sent, 'slab', split_axis=0, concat_axis=0, tiled=True)  5.39 us
    pallas_call x1, Pallas kernels, shard(): call(functools.partial(pack_both_kernel, split), [HBM], [plane(split), pl...  2.63 us
    all_to_all x1, waiting for transfers between devices, shard(): got = lax.all_to_all(sent, 'slab', split_axis=0, concat_axis=0, tiled=True)  2.2 us
    pallas_call x1, Pallas kernels, shard(): call(functools.partial(pack_kernel, 0), [HBM], [plane(split)], (buffer(sp...  1.99 us
  transfers between devices with their start and end apart: 9, of which 1 were waited for; matrix products, arithmetic and copies ran while one was open for 0% of the time, Pallas kernels for 59%

profile of v7, /device:TPU:1, one launch (start us, length us, event | category | flops | bytes accessed | tf_op | source)
XLA Modules:
  0.0 65.1 jit_solution(1409631530176601599)
XLA Ops:
  0.6 0.0 copy-start
  0.6 0.0 copy-start.3
  0.7 0.0 copy-start.2
  0.7 0.0 copy-start.1
  0.7 2.0 %shard_map.103 = bf16[192,1280]{1,0:T(8,128)(2,1)S(1)} custom-call(f32[4,320,320]{2,1,0:T(8,128)} %refs_2_.3), custom_call_target="tpu_custom_call" | custom-call | tf_op jit(solution)/shard_map/pallas_call | solution.py:562
  2.7 4.5 %collective-permute-start.1 = (bf16[192,1280]{1,0:T(8,128)(2,1)S(1)}, bf16[192,1280]{1,0:T(8,128)(2,1)S(1)}, u32[]{:S(2)}, u32[]{:S(2)}) collective-permute-start(bf16[192,1280]{1,0:T(8,128)(2,1)S(1)} %shard_map.103), channel_id=1, source_target_pairs={{1,2},{2,1},{3,4},{4,3},{5,6},{6,5},{7,8},{8,7},{9,10},{10,9},{11,... | collective-permute-start | bytes 1474568 | tf_op jit(solution)/shard_map/ppermute | solution.py:559
  7.2 0.0 copy-done
  7.2 0.0 copy-done.3
  7.2 0.0 copy-done.2
  7.2 0.0 copy-done.1
  7.2 1.0 %shard_map.104 = f32[16,1,128]{2,1,0:T(1,128)} custom-call(bf16[64,2048]{1,0:T(8,128)(2,1)S(1)} %copy-done, bf16[2,2048]{1,0:T(2,128)(2,1)S(1)} %copy-done.1, s32[1,64]{1,0:T(1,128)S(1)} %bitcast.2, s32[1,64]{1,0:T(1,128)S(1)} %bitcast.3), custom_call_target="tpu_custom_call" | custom-call | tf_op jit(solution)/shard_map/pallas_call | solution.py:570
  8.2 2.6 %shard_map.105 = (bf16[192,1280]{1,0:T(8,128)(2,1)S(1)}, bf16[128,1280]{1,0:T(8,128)(2,1)S(1)}) custom-call(f32[4,320,320]{2,1,0:T(8,128)} %refs_2_.3), custom_call_target="tpu_custom_call" | custom-call | tf_op jit(solution)/shard_map/pallas_call | solution.py:577
  10.9 0.1 collective-permute-start
  10.9 5.4 %all-to-all-start = ((f32[16,1,128]{2,1,0:T(1,128)}), f32[16,1,128]{2,1,0:T(1,128)S(1)}, u32[]{:S(2)}, u32[]{:S(2)}) async-start(f32[16,1,128]{2,1,0:T(1,128)} %shard_map.104), calls=%async_computation | async-start | bytes 16384 | tf_op jit(solution)/shard_map/all_to_all | solution.py:575
  16.3 3.5 %collective-permute-start.3 = (bf16[128,1280]{1,0:T(8,128)(2,1)S(1)}, bf16[128,1280]{1,0:T(8,128)(2,1)S(1)}, u32[]{:S(2)}, u32[]{:S(2)}) collective-permute-start(bf16[128,1280]{1,0:T(8,128)(2,1)S(1)} %get-tuple-element.30), channel_id=1, source_target_pairs={{1,2},{2,1},{3,4},{4,3},{5,6},{6,5},{7,8},{8,7},{9,10},{10,9},{11,... | collective-permute-start | bytes 983048 | tf_op jit(solution)/shard_map/ppermute | solution.py:559
  19.9 2.2 %all-to-all-done.got.refs_5_ = f32[16,1,128]{2,1,0:T(1,128)S(1)} async-done(((f32[16,1,128]{2,1,0:T(1,128)}), f32[16,1,128]{2,1,0:T(1,128)S(1)}, u32[]{:S(2)}, u32[]{:S(2)}) %all-to-all-start) | async-done | bytes 8224 | tf_op jit(solution)/shard_map/all_to_all | solution.py:575
  22.1 0.0 collective-permute-done.1.got_off
  22.1 0.0 collective-permute-done.got_on
  22.1 10.5 %shard_map.106 = (f32[4,192,320]{2,1,0:T(8,128)S(1)}, bf16[192,1280]{1,0:T(8,128)(2,1)S(1)}, bf16[192,1280]{1,0:T(8,128)(2,1)S(1)}, f32[4,136,320]{2,1,0:T(8,128)S(1)}) custom-call(f32[4,320,320]{2,1,0:T(8,128)} %refs_2_.3, f32[4,320,320]{2,1,0:T(8,128)} %prior.3, f32[4,320,320]{2,1,0:T(8,128)} %refs_3_.3, f32[16,1,128]{2,1,0:T(1,128)S(1)} %all-to-all-done.got.refs_5_, ...), custom_call_target="tpu_custom_call" | custom-call | tf_op jit(solution)/shard_map/pallas_call | solution.py:589
  32.6 0.7 %shard_map.107 = bf16[128,1280]{1,0:T(8,128)(2,1)S(1)} custom-call(f32[4,136,320]{2,1,0:T(8,128)S(1)} %get-tuple-element.29.field.now), custom_call_target="tpu_custom_call" | custom-call | tf_op jit(solution)/shard_map/pallas_call | solution.py:607
  33.3 0.7 %collective-permute-start.2 = (bf16[128,1280]{1,0:T(8,128)(2,1)S(1)}, bf16[128,1280]{1,0:T(8,128)(2,1)S(1)}, u32[]{:S(2)}, u32[]{:S(2)}) collective-permute-start(bf16[128,1280]{1,0:T(8,128)(2,1)S(1)} %shard_map.107), channel_id=1, source_target_pairs={{0,1},{1,0},{2,3},{3,2},{4,5},{5,4},{6,7},{7,6},{8,9},{9,8},{10,11... | collective-permute-start | bytes 983048 | tf_op jit(solution)/shard_map/ppermute | solution.py:559
  34.0 0.1 collective-permute-start.6
  34.1 2.4 %collective-permute-start.7 = (bf16[192,1280]{1,0:T(8,128)(2,1)S(1)}, bf16[192,1280]{1,0:T(8,128)(2,1)S(1)}, u32[]{:S(2)}, u32[]{:S(2)}) collective-permute-start(bf16[192,1280]{1,0:T(8,128)(2,1)S(1)} %get-tuple-element.39), channel_id=1, source_target_pairs={{1,2},{2,1},{3,4},{4,3},{5,6},{6,5},{7,8},{8,7},{9,10},{10,9},{11,... | collective-permute-start | bytes 1474568 | tf_op jit(solution)/shard_map/ppermute | solution.py:559
  36.5 0.0 collective-permute-done.3.got_off
  36.5 0.0 collective-permute-done.2.got_on
  36.5 7.2 %shard_map.108 = (f32[4,128,320]{2,1,0:T(8,128)S(1)}, bf16[128,1280]{1,0:T(8,128)(2,1)S(1)}, bf16[128,1280]{1,0:T(8,128)(2,1)S(1)}) custom-call(f32[4,136,320]{2,1,0:T(8,128)S(1)} %get-tuple-element.29.field.now, f32[4,320,320]{2,1,0:T(8,128)} %prior.3, f32[4,320,320]{2,1,0:T(8,128)} %refs_3_.3, f32[16,1,128]{2,1,0:T(1,128)S(1)} %all-to-all-done.got.refs_5_, ...), custom_call_target="tpu_custom_call" | custom-call | tf_op jit(solution)/shard_map/pallas_call | solution.py:589
  43.8 0.1 collective-permute-start.4
  43.9 3.5 %collective-permute-start.5 = (bf16[128,1280]{1,0:T(8,128)(2,1)S(1)}, bf16[128,1280]{1,0:T(8,128)(2,1)S(1)}, u32[]{:S(2)}, u32[]{:S(2)}) collective-permute-start(bf16[128,1280]{1,0:T(8,128)(2,1)S(1)} %get-tuple-element.37), channel_id=1, source_target_pairs={{1,2},{2,1},{3,4},{4,3},{5,6},{6,5},{7,8},{8,7},{9,10},{10,9},{11,... | collective-permute-start | bytes 983048 | tf_op jit(solution)/shard_map/ppermute | solution.py:559
  47.3 6.1 %shard_map.109 = (f32[4,128,320]{2,1,0:T(8,128)S(1)}, f32[4,128,320]{2,1,0:T(8,128)S(1)}, f32[4,128,320]{2,1,0:T(8,128)S(1)}, f32[4,128,320]{2,1,0:T(8,128)S(1)}) custom-call(f32[4,192,320]{2,1,0:T(8,128)S(1)} %get-tuple-element.27.refs_0_, f32[4,128,320]{2,1,0:T(8,128)S(1)} %get-tuple-element.31.refs_1_, f32[4,320,320]{2,1,0:T(8,128)} %refs_2_.3, ...), custom_call_target="tpu_custom_call" | custom-call | tf_op jit(solution)/shard_map/pallas_call | solution.py:623
  53.4 0.0 collective-permute-done.6.refs_6_
  53.4 0.0 collective-permute-done.7.refs_7_
  53.4 10.1 %shard_map.110 = (f32[4,320,320]{2,1,0:T(8,128)}, f32[4,320,320]{2,1,0:T(8,128)}, f32[4,320,320]{2,1,0:T(8,128)}) custom-call(f32[4,192,320]{2,1,0:T(8,128)S(1)} %get-tuple-element.27.refs_0_, f32[4,128,320]{2,1,0:T(8,128)S(1)} %get-tuple-element.31.refs_1_, f32[4,320,320]{2,1,0:T(8,128)} %refs_2_.3, f32[4,320,320]{2,1,0:T(8,128)} %refs_3_.3, ...), custom_call_target="tpu_custom_call" | custom-call | tf_op jit(solution)/shard_map/pallas_call | solution.py:610
  63.5 0.0 collective-permute-done.4.got_on
  63.5 0.0 collective-permute-done.5.got_off
  63.5 1.6 %shard_map.111 = (f32[4,320,320]{2,1,0:T(8,128)}, f32[4,320,320]{2,1,0:T(8,128)}) custom-call(f32[4,128,320]{2,1,0:T(8,128)S(1)} %get-tuple-element.32.partial, f32[4,128,320]{2,1,0:T(8,128)S(1)} %get-tuple-element.33.image_in, f32[4,128,320]{2,1,0:T(8,128)S(1)} %get-tuple-element.34.speed, ...), custom_call_target="tpu_custom_call", output_to_operand_aliasing={{0}: (6, {}), {1}: (7, {})} | custom-call | tf_op jit(solution)/shard_map/pallas_call | solution.py:629
Async XLA Ops:
  0.6 6.6 %copy-start = (bf16[64,2048]{1,0:T(8,128)(2,1)S(1)}, bf16[64,2048]{1,0:T(8,128)(2,1)}, u32[]{:S(2)}) copy-start(bf16[64,2048]{1,0:T(8,128)(2,1)} %traces) | copy-start | bytes 786436
  0.6 6.6 %copy-start.3 = (s32[64]{0:T(128)S(1)}, s32[64]{0:T(128)}, u32[]{:S(2)}) copy-start(s32[64]{0:T(128)} %param.15) | copy-start | bytes 772
  0.7 6.6 %copy-start.2 = (s32[64,1]{0,1:T(1,128)S(1)}, s32[64,1]{0,1:T(1,128)}, u32[]{:S(2)}) copy-start(s32[64,1]{0,1:T(1,128)} %param.14) | copy-start | bytes 772
  0.7 6.6 %copy-start.1 = (bf16[2,2048]{1,0:T(2,128)(2,1)S(1)}, bf16[2,2048]{1,0:T(2,128)(2,1)}, u32[]{:S(2)}) copy-start(bf16[2,2048]{1,0:T(2,128)(2,1)} %weights.1) | copy-start | bytes 24580
  2.7 19.4 %collective-permute-start.1 = (bf16[192,1280]{1,0:T(8,128)(2,1)S(1)}, bf16[192,1280]{1,0:T(8,128)(2,1)S(1)}, u32[]{:S(2)}, u32[]{:S(2)}) collective-permute-start(bf16[192,1280]{1,0:T(8,128)(2,1)S(1)} %shard_map.103), channel_id=1, source_target_pairs={{1,2},{2,1},{3,4},{4,3},{5,6},{6,5},{7,8},{8,7},{9,10},{10,9},{11,... | collective-permute-start | bytes 1474568 | tf_op jit(solution)/shard_map/ppermute | solution.py:559
  10.9 11.2 %collective-permute-start = (bf16[192,1280]{1,0:T(8,128)(2,1)S(1)}, bf16[192,1280]{1,0:T(8,128)(2,1)S(1)}, u32[]{:S(2)}, u32[]{:S(2)}) collective-permute-start(bf16[192,1280]{1,0:T(8,128)(2,1)S(1)} %get-tuple-element.26), channel_id=1, source_target_pairs={{0,1},{1,0},{2,3},{3,2},{4,5},{5,4},{6,7},{7,6},{8,9},{9,8},{10,11... | collective-permute-start | bytes 1474568 | tf_op jit(solution)/shard_map/ppermute | solution.py:559
  10.9 11.1 %all-to-all-start = ((f32[16,1,128]{2,1,0:T(1,128)}), f32[16,1,128]{2,1,0:T(1,128)S(1)}, u32[]{:S(2)}, u32[]{:S(2)}) async-start(f32[16,1,128]{2,1,0:T(1,128)} %shard_map.104), calls=%async_computation | async-start | bytes 16384 | tf_op jit(solution)/shard_map/all_to_all | solution.py:575
  16.3 20.2 %collective-permute-start.3 = (bf16[128,1280]{1,0:T(8,128)(2,1)S(1)}, bf16[128,1280]{1,0:T(8,128)(2,1)S(1)}, u32[]{:S(2)}, u32[]{:S(2)}) collective-permute-start(bf16[128,1280]{1,0:T(8,128)(2,1)S(1)} %get-tuple-element.30), channel_id=1, source_target_pairs={{1,2},{2,1},{3,4},{4,3},{5,6},{6,5},{7,8},{8,7},{9,10},{10,9},{11,... | collective-permute-start | bytes 983048 | tf_op jit(solution)/shard_map/ppermute | solution.py:559
  33.3 3.3 %collective-permute-start.2 = (bf16[128,1280]{1,0:T(8,128)(2,1)S(1)}, bf16[128,1280]{1,0:T(8,128)(2,1)S(1)}, u32[]{:S(2)}, u32[]{:S(2)}) collective-permute-start(bf16[128,1280]{1,0:T(8,128)(2,1)S(1)} %shard_map.107), channel_id=1, source_target_pairs={{0,1},{1,0},{2,3},{3,2},{4,5},{5,4},{6,7},{7,6},{8,9},{9,8},{10,11... | collective-permute-start | bytes 983048 | tf_op jit(solution)/shard_map/ppermute | solution.py:559
  34.0 19.4 %collective-permute-start.6 = (bf16[192,1280]{1,0:T(8,128)(2,1)S(1)}, bf16[192,1280]{1,0:T(8,128)(2,1)S(1)}, u32[]{:S(2)}, u32[]{:S(2)}) collective-permute-start(bf16[192,1280]{1,0:T(8,128)(2,1)S(1)} %get-tuple-element.38), channel_id=1, source_target_pairs={{0,1},{1,0},{2,3},{3,2},{4,5},{5,4},{6,7},{7,6},{8,9},{9,8},{10,11... | collective-permute-start | bytes 1474568 | tf_op jit(solution)/shard_map/ppermute | solution.py:559
  34.1 19.4 %collective-permute-start.7 = (bf16[192,1280]{1,0:T(8,128)(2,1)S(1)}, bf16[192,1280]{1,0:T(8,128)(2,1)S(1)}, u32[]{:S(2)}, u32[]{:S(2)}) collective-permute-start(bf16[192,1280]{1,0:T(8,128)(2,1)S(1)} %get-tuple-element.39), channel_id=1, source_target_pairs={{1,2},{2,1},{3,4},{4,3},{5,6},{6,5},{7,8},{8,7},{9,10},{10,9},{11,... | collective-permute-start | bytes 1474568 | tf_op jit(solution)/shard_map/ppermute | solution.py:559
  43.8 19.7 %collective-permute-start.4 = (bf16[128,1280]{1,0:T(8,128)(2,1)S(1)}, bf16[128,1280]{1,0:T(8,128)(2,1)S(1)}, u32[]{:S(2)}, u32[]{:S(2)}) collective-permute-start(bf16[128,1280]{1,0:T(8,128)(2,1)S(1)} %get-tuple-element.36), channel_id=1, source_target_pairs={{0,1},{1,0},{2,3},{3,2},{4,5},{5,4},{6,7},{7,6},{8,9},{9,8},{10,11... | collective-permute-start | bytes 983048 | tf_op jit(solution)/shard_map/ppermute | solution.py:559
  43.9 19.7 %collective-permute-start.5 = (bf16[128,1280]{1,0:T(8,128)(2,1)S(1)}, bf16[128,1280]{1,0:T(8,128)(2,1)S(1)}, u32[]{:S(2)}, u32[]{:S(2)}) collective-permute-start(bf16[128,1280]{1,0:T(8,128)(2,1)S(1)} %get-tuple-element.37), channel_id=1, source_target_pairs={{1,2},{2,1},{3,4},{4,3},{5,6},{6,5},{7,8},{8,7},{9,10},{10,9},{11,... | collective-permute-start | bytes 983048 | tf_op jit(solution)/shard_map/ppermute | solution.py:559

commit v8 on v7

--- a/solution.py
+++ b/solution.py
@@ -2,6 +2,7 @@
 
 import jax
 import jax.numpy as jnp
+import numpy as np
 from jax import lax
 from jax.experimental import pallas as pl
 from jax.experimental.pallas import tpu as pltpu
@@ -26,7 +27,7 @@
 
 
 def params():
-    return pltpu.CompilerParams(vmem_limit_bytes=16 << 20)
+    return pltpu.CompilerParams(vmem_limit_bytes=20 << 20)
 
 
 def payload_lanes(width):
@@ -133,46 +134,27 @@
     return copies
 
 
-def pack_kernel(first, now, off_ref, buf, sems):
+def pack_kernel(first, with_on, now, *refs):
+    refs = list(refs)
+    on_ref = refs.pop(0) if with_on else None
+    off_ref, buf, sems = refs
     depth = now.shape[0]
-    count = off_ref.shape[0]
-    copies = fetch(now, buf, sems, first, count)
-    for copy, (row, size) in zip(copies, blocks_of(0, count)):
+    base = 0 if with_on else first
+    copies = fetch(now, buf, sems, base, buf.shape[1])
+
+    for i, copy in enumerate(copies):
         copy.wait()
 
         def body(r):
-            rows = pl.ds(r + row, ROWS)
+            r = r + i * BLOCK
+            rows = pl.ds(r, ROWS)
             u = [buf[depth_at(j, depth), rows, :] for j in range(depth)]
-            put(off_ref, rows, encode(u[::-1][:HALO]))
-
-        row_loop(size, body)
-
-
-def pack_both_kernel(first, now, on_ref, off_ref, buf, sems):
-    depth, width_x, _ = now.shape
-    copies = fetch(now, buf, sems, 0, width_x)
-    for copy, (row, size) in zip(copies, blocks_of(0, width_x)):
-        copy.wait()
-
-        def body(r):
-            rows = pl.ds(r + row, ROWS)
-            u = [buf[depth_at(j, depth), rows, :] for j in range(depth)]
-            if row >= first:
-                put(off_ref, pl.ds(r + (row - first), ROWS), encode(u[::-1][:HALO]))
-            else:
+            if base + i * BLOCK >= first and base + i * BLOCK < first + off_ref.shape[0]:
+                put(off_ref, pl.ds(r + base - first, ROWS), encode(u[::-1][:HALO]))
+            if with_on:
                 put(on_ref, rows, encode(u[:HALO]))
 
-        row_loop(size, body)
-
-
-def pack_on_kernel(field, on_ref):
-    depth = field.shape[0]
-
-    def body(r):
-        u = [field[depth_at(j, depth), pl.ds(r + SUB, ROWS), :] for j in range(depth)]
-        put(on_ref, pl.ds(r, ROWS), encode(u[:HALO]))
-
-    row_loop(on_ref.shape[0], body)
+        row_loop(BLOCK, body)
 
 
 def route_kernel(slabs, field, traces, weights, target, cell, out):
@@ -249,21 +231,65 @@
             tiles[tile_rows(z, row, j, count, number), :] = jnp.zeros((SUB, LANES), F32)
 
 
-def add_laplace(tiles, lap, depth, count, width_y):
+def band(width_y):
     number = len(tile_parts(width_y))
-    lane = lax.broadcasted_iota(jnp.int32, (SUB, LANES), 1)
+    spot = np.arange(number * LANES)
+    away = np.abs(spot[:, None] - spot[None, :])
+    inside = (spot[:, None] < width_y) & (spot[None, :] < width_y)
+    whole = np.zeros(away.shape, np.float32)
+    for k in range(1, HALO + 1):
+        whole[(away == k) & inside] = W[k]
+    out = []
+    for w in range(number - 1):
+        part = whole[w * LANES : (w + 2) * LANES, w * LANES : (w + 2) * LANES].copy()
+        if w:
+            part[:LANES, :LANES] = 0.0
+        high = part.astype(BF16)
+        out.append([high, (part - high.astype(np.float32)).astype(BF16)])
+    return np.array(out)
+
+
+def halve(high, low, source, start, count):
+    depth, _, width_y = source.shape
+    extra = high.shape[1] - width_y
+
+    def body(r):
+        for z in range(depth):
+            value = source[z, pl.ds(pl.multiple_of(r + start, SUB), ROWS), :]
+            value = jnp.pad(value, ((0, 0), (0, extra)))
+            top = value.astype(BF16)
+            into = pl.ds(pl.multiple_of(r + z * count, ROWS), ROWS)
+            high[into, :] = top
+            low[into, :] = (value - top.astype(F32)).astype(BF16)
+
+    row_loop(count, body)
+
+
+def add_lanes(high, low, weights, lap):
+    lines = high.shape[0]
+    size = lines // 2
+
+    def product(x, y):
+        return jnp.dot(x, y, preferred_element_type=F32)
+
+    def step(i, carry):
+        rows = pl.ds(pl.multiple_of(i * size, ROWS), size)
+        for w in range(weights.shape[0]):
+            window = slice(w * LANES, (w + 2) * LANES)
+            x, y = high[rows, window], low[rows, window]
+            total = product(x, weights[w, 0]) + product(y, weights[w, 0])
+            total = total + product(x, weights[w, 1])
+            for q in range(2):
+                into = pl.ds(pl.multiple_of(i * size + (w + q) * lines, ROWS), size)
+                lap[into, :] = lap[into, :] + total[:, q * LANES : (q + 1) * LANES]
+        return carry
+
+    lax.fori_loop(0, 2, step, 0)
+
+
+def add_rows(tiles, lap, depth, count, number):
     groups = count // SUB
     unroll = max(u for u in range(1, UNROLL + 1) if groups % u == 0)
-    middle = 3.0 * W[0] - 2.0 * W[4]
-
-    def both(values, k):
-        right = [pltpu.roll(v, k, 1) for v in values]
-        left = [pltpu.roll(v, LANES - k, 1) for v in values]
-        return [
-            jnp.where(lane < k, right[j - 1], right[j])
-            + jnp.where(lane >= LANES - k, left[(j + 1) % number], left[j])
-            for j in range(number)
-        ]
 
     def one(r):
         def at(z, j, shift=0):
@@ -271,17 +297,9 @@
 
         centre = [[at(z, j) for j in range(number)] for z in range(depth)]
         for z in range(depth):
-            places = [
-                pl.ds(pl.multiple_of(r + (j * depth + z) * count, SUB), SUB) for j in range(number)
-            ]
-            once, twice = both(centre[z], 1), both(centre[z], 2)
-            inner = [
-                W[2] * centre[z][j] + W[3] * once[j] + W[4] * twice[j] for j in range(number)
-            ]
-            outer = both(inner, 2)
             for j in range(number):
-                total = lap[places[j], :] + middle * centre[z][j]
-                total = total + (W[1] - W[3]) * once[j] + outer[j]
+                place = pl.ds(pl.multiple_of(r + (j * depth + z) * count, SUB), SUB)
+                total = lap[place, :] + 3.0 * W[0] * centre[z][j]
                 for k in range(1, HALO + 1):
                     pair = at(z, j, -k) + at(z, j, k)
                     if z - k >= 0:
@@ -289,7 +307,7 @@
                     if z + k < depth:
                         pair = pair + centre[z + k][j]
                     total = total + W[k] * pair
-                lap[places[j], :] = total
+                lap[place, :] = total
 
     def step(i, carry):
         for u in range(unroll):
@@ -360,13 +378,15 @@
     inject(step, got, lap, number * depth, first, count, width_x)
 
 
-def first_kernel(first, width_x, more, now, prior, velocity, got, got_on, got_off, *refs):
+def first_kernel(first, width_x, more, now, prior, velocity, lanes, got, got_on, got_off, *refs):
     part, on_ref, off_ref = refs[:3]
     following = refs[3] if more else None
-    tiles, lap, now_buf, prior_buf, speed_buf, sems = refs[-6:]
+    tiles, lap, high_buf, low_buf, band_buf, now_buf, prior_buf, speed_buf, sems, band_sem = refs[-10:]
     depth, count, width_y = part.shape
     low, high = max(first - SUB, 0), min(first + count + SUB, width_x)
     now_copies = fetch(now, now_buf, sems.at[0], low, high - low) if more else []
+    weights = pltpu.make_async_copy(lanes, band_buf, band_sem)
+    weights.start()
     copies = fetch(prior, prior_buf, sems.at[1], first, count)
     copies += fetch(velocity, speed_buf, sems.at[2], first, count)
     if more:
@@ -378,14 +398,17 @@
     held = now_buf if more else now
     if not more:
         spread(tiles, count, now, 0, low - first, high - low)
-    add_laplace(tiles, lap, depth, count, width_y)
+    halve(high_buf, low_buf, held, first - low, count)
+    weights.wait()
+    add_lanes(high_buf, low_buf, band_buf, lap)
+    add_rows(tiles, lap, depth, count, len(tile_parts(width_y)))
     for copy in copies:
         copy.wait()
 
     def body(r):
         rows = pl.ds(r, ROWS)
         here = pl.ds(pl.multiple_of(r + (first - low), SUB), ROWS)
-        halo = halo_sum(got_on, rows, got_off, rows, width_y, depth)
+        halo = halo_sum(got_on, pl.ds(r + first, ROWS), got_off, rows, width_y, depth)
         u = []
         for j in range(depth):
             z = depth_at(j, depth)
@@ -402,10 +425,13 @@
     row_loop(count, body)
 
 
-def second_local(first, starts, parts, now, velocity, forward, got, tiles, lap, bufs, sems):
+def second_local(first, starts, parts, now, velocity, forward, lanes, got, stencil, bufs, sems):
     now_buf, speed_buf, *forward_bufs = bufs
+    tiles, lap, high_buf, low_buf, band_buf, band_sem = stencil
     depth, width_x, width_y = now.shape
     count = now_buf.shape[1]
+    weights = pltpu.make_async_copy(lanes, band_buf, band_sem)
+    weights.start()
     low, high = max(first - SUB, 0), min(first + count + SUB, width_x)
     copies = fetch(now, now_buf, sems.at[0], first, count)
     copies += fetch(velocity, speed_buf, sems.at[1], first, count)
@@ -415,10 +441,14 @@
     for start, part in zip(starts, parts):
         row, end = max(low, start), min(high, start + part.shape[1])
         spread(tiles, count, part, row - start, row - first, end - row)
-    add_laplace(tiles, lap, depth, count, width_y)
+    here = parts[starts.index(first)]
+    halve(high_buf, low_buf, here, 0, count)
+    weights.wait()
+    add_lanes(high_buf, low_buf, band_buf, lap)
+    add_rows(tiles, lap, depth, count, len(tile_parts(width_y)))
     for copy in copies:
         copy.wait()
-    return parts[starts.index(first)]
+    return here
 
 
 def send_rows(pairs, first, row, sems, n):
@@ -434,8 +464,10 @@
 
 def second_kernel(first, starts, *refs):
     parts, refs = refs[: len(starts)], refs[len(starts) :]
-    now, velocity, forward, got, got_on, got_off, out, image, current, tiles, lap = refs[:11]
-    *bufs, out_buf, image_buf, sems, out_sems, part_sems = refs[11:]
+    now, velocity, forward, lanes, got, got_on, got_off, out, image, current = refs[:10]
+    stencil, bufs = refs[10:16], refs[16:20]
+    out_buf, image_buf, sems, out_sems, part_sems = refs[20:]
+    lap = stencil[1]
     depth, _, width_y = now.shape
     count = out_buf.shape[1]
     writes = []
@@ -445,7 +477,7 @@
         )
         write.start()
         writes.append(write)
-    here = second_local(first, starts, parts, now, velocity, forward, got, tiles, lap, bufs, sems)
+    here = second_local(first, starts, parts, now, velocity, forward, lanes, got, stencil, bufs, sems)
     now_buf, speed_buf, early, late = bufs
     for n, i in enumerate(range(0, count, BLOCK)):
 
@@ -471,11 +503,13 @@
 
 def partial_kernel(first, starts, *refs):
     parts, refs = refs[: len(starts)], refs[len(starts) :]
-    now, velocity, forward, got, out, image, speed, late, tiles, lap, now_buf, early, sems = refs
+    now, velocity, forward, lanes, got, out, image, speed, late = refs[:9]
+    stencil, (now_buf, early, sems) = refs[9:15], refs[15:]
+    lap = stencil[1]
     depth, _, width_y = now.shape
     count = now_buf.shape[1]
     bufs = (now_buf, speed, early, late)
-    here = second_local(first, starts, parts, now, velocity, forward, got, tiles, lap, bufs, sems)
+    here = second_local(first, starts, parts, now, velocity, forward, lanes, got, stencil, bufs, sems)
 
     def body(r):
         rows = pl.ds(r, ROWS)
@@ -516,6 +550,7 @@
     )
     slabs = lax.axis_size("slab")
     depth, width_x, width_y = now.shape
+    lanes = pltpu.with_memory_space_constraint(jnp.asarray(band(width_y)), pltpu.HBM)
     rows = traces.shape[0]
     face_lanes = payload_lanes(width_y)
     split = width_x * SHARE[0] // (sum(SHARE) * BLOCK) * BLOCK
@@ -539,7 +574,8 @@
     def stencil(count):
         tiles = pltpu.VMEM((number * depth * (count + 2 * SUB), LANES), F32)
         lap = pltpu.VMEM((number * depth * count + SUB, LANES), F32)
-        return (tiles, lap)
+        half = pltpu.VMEM((depth * count, number * LANES), BF16)
+        return (tiles, lap, half, half, pltpu.VMEM(lanes.shape, BF16))
 
     def blocks(count):
         return -(-count // BLOCK)
@@ -560,7 +596,7 @@
 
     got_off = []
     (face,) = call(
-        functools.partial(pack_kernel, 0),
+        functools.partial(pack_kernel, 0, False),
         [HBM],
         [plane(split)],
         (buffer(split), dma((blocks(split),))),
@@ -575,9 +611,9 @@
     got = lax.all_to_all(sent, "slab", split_axis=0, concat_axis=0, tiled=True)
     sent, later = lax.optimization_barrier((sent, now))
     on_face, face = call(
-        functools.partial(pack_both_kernel, split),
+        functools.partial(pack_kernel, split, True),
         [HBM],
-        [plane(split), plane(width_x - split)],
+        [plane(width_x), plane(width_x - split)],
         (buffer(width_x), dma((blocks(width_x),))),
     )(later)
     got_off.append(swap(face, off_pairs))
@@ -588,7 +624,7 @@
     for i, (first, count) in enumerate(chunks):
         part, on_face, face, *following = call(
             functools.partial(first_kernel, first, width_x, 0 if i else more),
-            [VMEM if i else HBM, HBM, HBM, SMEM, VMEM, VMEM],
+            [VMEM if i else HBM, HBM, HBM, HBM, SMEM, VMEM, VMEM],
             [rows_of(count), plane(count), plane(count)] + ([] if i else [rows_of(more)]),
             (
                 *stencil(count),
@@ -596,36 +632,36 @@
                 buffer(count),
                 buffer(count),
                 dma((4, blocks(width_x))),
+                dma,
             ),
-        )(held, prior, velocity, got, got_on, got_off[i])
+        )(held, prior, velocity, lanes, got, got_on, got_off[i])
         second_off.append(swap(face, off_pairs))
         second_on.append(swap(on_face, on_pairs))
         parts.append(part)
         if i == 0:
             (held,) = following
-            part, held = lax.optimization_barrier((part, held))
-            (on_face,) = call(pack_on_kernel, [VMEM], [plane(width_x - split)])(held)
-            got_on = swap(on_face, on_pairs)
+            part, prior = lax.optimization_barrier((part, prior))
     (first, count), (last, size) = chunks
     second, image, current = call(
         functools.partial(second_kernel, first, starts),
-        [VMEM] * len(parts) + [HBM] * 3 + [SMEM, VMEM, VMEM],
+        [VMEM] * len(parts) + [HBM] * 4 + [SMEM, VMEM, VMEM],
         [field, field, field],
         (
             *stencil(count),
+            dma,
             *[buffer(count)] * 6,
             dma((2 + STEPS, blocks(count))),
             dma((2, blocks(count))),
             dma((len(parts),)),
         ),
         [HBM] * 3,
-    )(*parts, now, velocity, forward, got, second_on[0], second_off[0])
+    )(*parts, now, velocity, forward, lanes, got, second_on[0], second_off[0])
     partial, image_part, speed, late = call(
         functools.partial(partial_kernel, last, starts),
-        [VMEM] * len(parts) + [HBM] * 3 + [SMEM],
+        [VMEM] * len(parts) + [HBM] * 4 + [SMEM],
         [rows_of(size)] * 4,
-        (*stencil(size), buffer(size), buffer(size), dma((2 + STEPS, blocks(size)))),
-    )(*parts, now, velocity, forward, got)
+        (*stencil(size), dma, buffer(size), buffer(size), dma((2 + STEPS, blocks(size)))),
+    )(*parts, now, velocity, forward, lanes, got)
     second, image = call(
         functools.partial(last_kernel, last),
         [VMEM] * 6 + [HBM] * 2,

time: 65.4 us -> 66.1 us (1.011)
  the two profiles are of different devices: /device:TPU:1 before, /device:TPU:9 now
where the time goes in v8:
time: 66.1 us; the launch traced here: 65.8 us
  Pallas kernels  31.9 us (48%)
  blocking collectives  17 us (26%)
  starting transfers between devices  13.6 us (21%)
  waiting for transfers between devices  2.4 us (4%)
  between operations  0.81 us (1%)
    all_to_all x1, blocking collectives, shard(): got = lax.all_to_all(sent, 'slab', split_axis=0, concat_axis=0, tiled=True)  17 us
    ppermute x7, starting transfers between devices, swap(): return lax.ppermute(face, 'slab', pairs)  13.6 us
    pallas_call x2, Pallas kernels, shard(): call(functools.partial(first_kernel, first, width_x, 0 if i else more), [...  12.5 us
    pallas_call x1, Pallas kernels, shard(): call(functools.partial(second_kernel, first, starts), [VMEM] * len(parts)...  8.02 us
    pallas_call x1, Pallas kernels, shard(): call(functools.partial(partial_kernel, last, starts), [VMEM] * len(parts)...  4.57 us
    pallas_call x1, Pallas kernels, shard(): call(functools.partial(pack_kernel, split, True), [HBM], [plane(width_x),...  2.78 us
    ppermute x7, waiting for transfers between devices, swap(): return lax.ppermute(face, 'slab', pairs)  2.4 us
    pallas_call x1, Pallas kernels, shard(): call(functools.partial(pack_kernel, 0, False), [HBM], [plane(split)], (bu...  1.99 us
  transfers between devices with their start and end apart: 7, of which 1 were waited for; matrix products, arithmetic and copies ran while one was open for 0% of the time, Pallas kernels for 38%

profile of v8, /device:TPU:9, one launch (start us, length us, event | category | flops | bytes accessed | tf_op | source)
XLA Modules:
  0.0 65.8 jit_solution(14527323676715545546)
XLA Ops:
  0.6 0.0 copy-start
  0.6 0.0 copy-start.3
  0.7 0.0 copy-start.2
  0.7 0.0 copy-start.1
  0.7 2.0 %shard_map.112 = bf16[192,1280]{1,0:T(8,128)(2,1)S(1)} custom-call(f32[4,320,320]{2,1,0:T(8,128)} %refs_2_.3), custom_call_target="tpu_custom_call" | custom-call | tf_op jit(solution)/shard_map/pallas_call | solution.py:598
  2.7 0.0 copy-done
  2.7 0.0 copy-done.3
  2.7 0.0 copy-done.2
  2.7 0.0 copy-done.1
  2.7 0.4 shard_map.113
  3.1 2.8 %shard_map.114 = (bf16[320,1280]{1,0:T(8,128)(2,1)S(1)}, bf16[128,1280]{1,0:T(8,128)(2,1)S(1)}) custom-call(f32[4,320,320]{2,1,0:T(8,128)} %refs_2_.3), custom_call_target="tpu_custom_call" | custom-call | tf_op jit(solution)/shard_map/pallas_call | solution.py:613
  5.9 0.7 %collective-permute-start = (bf16[320,1280]{1,0:T(8,128)(2,1)S(1)}, bf16[320,1280]{1,0:T(8,128)(2,1)S(1)}, u32[]{:S(2)}, u32[]{:S(2)}) collective-permute-start(bf16[320,1280]{1,0:T(8,128)(2,1)S(1)} %get-tuple-element.26), channel_id=1, source_target_pairs={{0,1},{1,0},{2,3},{3,2},{4,5},{5,4},{6,7},{7,6},{8,9},{9,8},{10,11... | collective-permute-start | bytes 2457608 | tf_op jit(solution)/shard_map/ppermute | solution.py:595
  6.6 3.0 %collective-permute-start.1 = (bf16[192,1280]{1,0:T(8,128)(2,1)S(1)}, bf16[192,1280]{1,0:T(8,128)(2,1)S(1)}, u32[]{:S(2)}, u32[]{:S(2)}) collective-permute-start(bf16[192,1280]{1,0:T(8,128)(2,1)S(1)} %shard_map.112), channel_id=1, source_target_pairs={{1,2},{2,1},{3,4},{4,3},{5,6},{6,5},{7,8},{8,7},{9,10},{10,9},{11,... | collective-permute-start | bytes 1474568 | tf_op jit(solution)/shard_map/ppermute | solution.py:595
  9.7 2.5 %collective-permute-start.2 = (bf16[128,1280]{1,0:T(8,128)(2,1)S(1)}, bf16[128,1280]{1,0:T(8,128)(2,1)S(1)}, u32[]{:S(2)}, u32[]{:S(2)}) collective-permute-start(bf16[128,1280]{1,0:T(8,128)(2,1)S(1)} %get-tuple-element.30), channel_id=1, source_target_pairs={{1,2},{2,1},{3,4},{4,3},{5,6},{6,5},{7,8},{8,7},{9,10},{10,9},{11,... | collective-permute-start | bytes 983048 | tf_op jit(solution)/shard_map/ppermute | solution.py:595
  12.2 17.0 %all_to_all.5.got.refs_6_ = f32[16,1,128]{2,1,0:T(1,128)S(1)} all-to-all(f32[16,1,128]{2,1,0:T(1,128)S(1)} %shard_map.113), channel_id=1, replica_groups=mesh['groups'=2,'slab'=16] {'slab'}, dimensions={0} | all-to-all | bytes 16384 | tf_op jit(solution)/shard_map/all_to_all | solution.py:611
  29.2 0.0 collective-permute-done.1.got_off
  29.2 0.0 collective-permute-done.got_on
  29.2 7.3 %shard_map.115 = (f32[4,192,320]{2,1,0:T(8,128)S(1)}, bf16[192,1280]{1,0:T(8,128)(2,1)S(1)}, bf16[192,1280]{1,0:T(8,128)(2,1)S(1)}, f32[4,136,320]{2,1,0:T(8,128)S(1)}) custom-call(f32[4,320,320]{2,1,0:T(8,128)} %refs_2_.3, f32[4,320,320]{2,1,0:T(8,128)} %prior.2, f32[4,320,320]{2,1,0:T(8,128)} %refs_3_.3, ...), custom_call_target="tpu_custom_call" | custom-call | tf_op jit(solution)/shard_map/pallas_call | solution.py:625
  36.5 0.7 %collective-permute-start.5 = (bf16[192,1280]{1,0:T(8,128)(2,1)S(1)}, bf16[192,1280]{1,0:T(8,128)(2,1)S(1)}, u32[]{:S(2)}, u32[]{:S(2)}) collective-permute-start(bf16[192,1280]{1,0:T(8,128)(2,1)S(1)} %get-tuple-element.38), channel_id=1, source_target_pairs={{0,1},{1,0},{2,3},{3,2},{4,5},{5,4},{6,7},{7,6},{8,9},{9,8},{10,11... | collective-permute-start | bytes 1474568 | tf_op jit(solution)/shard_map/ppermute | solution.py:595
  37.2 2.5 %collective-permute-start.6 = (bf16[192,1280]{1,0:T(8,128)(2,1)S(1)}, bf16[192,1280]{1,0:T(8,128)(2,1)S(1)}, u32[]{:S(2)}, u32[]{:S(2)}) collective-permute-start(bf16[192,1280]{1,0:T(8,128)(2,1)S(1)} %get-tuple-element.39), channel_id=1, source_target_pairs={{1,2},{2,1},{3,4},{4,3},{5,6},{6,5},{7,8},{8,7},{9,10},{10,9},{11,... | collective-permute-start | bytes 1474568 | tf_op jit(solution)/shard_map/ppermute | solution.py:595
  39.7 0.0 collective-permute-done.2.got_off
  39.7 5.3 %shard_map.116 = (f32[4,128,320]{2,1,0:T(8,128)S(1)}, bf16[128,1280]{1,0:T(8,128)(2,1)S(1)}, bf16[128,1280]{1,0:T(8,128)(2,1)S(1)}) custom-call(f32[4,136,320]{2,1,0:T(8,128)S(1)} %get-tuple-element.28.now, f32[4,320,320]{2,1,0:T(8,128)} %prior.2, f32[4,320,320]{2,1,0:T(8,128)} %refs_3_.3, bf16[2,2,256,256]{3,2,1,0:T(8,128)(2,1)} %constant.2.clone.lanes.refs_5_, ...), custom_call_target="tpu_custom_call" | custom-call | tf_op jit(solution)/shard_map/pallas_call | solution.py:625
  44.9 0.4 collective-permute-start.3
  45.4 3.7 %collective-permute-start.4 = (bf16[128,1280]{1,0:T(8,128)(2,1)S(1)}, bf16[128,1280]{1,0:T(8,128)(2,1)S(1)}, u32[]{:S(2)}, u32[]{:S(2)}) collective-permute-start(bf16[128,1280]{1,0:T(8,128)(2,1)S(1)} %get-tuple-element.37), channel_id=1, source_target_pairs={{1,2},{2,1},{3,4},{4,3},{5,6},{6,5},{7,8},{8,7},{9,10},{10,9},{11,... | collective-permute-start | bytes 983048 | tf_op jit(solution)/shard_map/ppermute | solution.py:595
  49.1 4.6 %shard_map.117 = (f32[4,128,320]{2,1,0:T(8,128)S(1)}, f32[4,128,320]{2,1,0:T(8,128)S(1)}, f32[4,128,320]{2,1,0:T(8,128)S(1)}, f32[4,128,320]{2,1,0:T(8,128)S(1)}) custom-call(f32[4,192,320]{2,1,0:T(8,128)S(1)} %get-tuple-element.27.refs_0_, f32[4,128,320]{2,1,0:T(8,128)S(1)} %get-tuple-element.31.refs_1_, f32[4,320,320]{2,1,0:T(8,128)} %refs_2_.3, ...), custom_call_target="tpu_custom_call" | custom-call | tf_op jit(solution)/shard_map/pallas_call | solution.py:659
  53.7 0.0 collective-permute-done.5.refs_7_
  53.7 2.4 %collective-permute-done.6.refs_8_ = bf16[192,1280]{1,0:T(8,128)(2,1)S(1)} collective-permute-done((bf16[192,1280]{1,0:T(8,128)(2,1)S(1)}, bf16[192,1280]{1,0:T(8,128)(2,1)S(1)}, u32[]{:S(2)}, u32[]{:S(2)}) %collective-permute-start.6) | collective-permute-done | bytes 491552 | tf_op jit(solution)/shard_map/ppermute | solution.py:595
  56.1 8.0 %shard_map.118 = (f32[4,320,320]{2,1,0:T(8,128)}, f32[4,320,320]{2,1,0:T(8,128)}, f32[4,320,320]{2,1,0:T(8,128)}) custom-call(f32[4,192,320]{2,1,0:T(8,128)S(1)} %get-tuple-element.27.refs_0_, f32[4,128,320]{2,1,0:T(8,128)S(1)} %get-tuple-element.31.refs_1_, f32[4,320,320]{2,1,0:T(8,128)} %refs_2_.3, f32[4,320,320]{2,1,0:T(8,128)} %refs_3_.3, ...), custom_call_target="tpu_custom_call" | custom-call | tf_op jit(solution)/shard_map/pallas_call | solution.py:645
  64.1 0.0 collective-permute-done.3.got_on
  64.1 0.0 collective-permute-done.4.got_off
  64.1 1.6 %shard_map.119 = (f32[4,320,320]{2,1,0:T(8,128)}, f32[4,320,320]{2,1,0:T(8,128)}) custom-call(f32[4,128,320]{2,1,0:T(8,128)S(1)} %get-tuple-element.32.partial, f32[4,128,320]{2,1,0:T(8,128)S(1)} %get-tuple-element.33.image_in, f32[4,128,320]{2,1,0:T(8,128)S(1)} %get-tuple-element.34.speed, ...), custom_call_target="tpu_custom_call", output_to_operand_aliasing={{0}: (6, {}), {1}: (7, {})} | custom-call | tf_op jit(solution)/shard_map/pallas_call | solution.py:665
Async XLA Ops:
  0.6 2.0 %copy-start = (bf16[64,2048]{1,0:T(8,128)(2,1)S(1)}, bf16[64,2048]{1,0:T(8,128)(2,1)}, u32[]{:S(2)}) copy-start(bf16[64,2048]{1,0:T(8,128)(2,1)} %traces) | copy-start | bytes 786436
  0.6 2.0 %copy-start.3 = (s32[64]{0:T(128)S(1)}, s32[64]{0:T(128)}, u32[]{:S(2)}) copy-start(s32[64]{0:T(128)} %param.16) | copy-start | bytes 772
  0.7 2.0 %copy-start.2 = (s32[64,1]{0,1:T(1,128)S(1)}, s32[64,1]{0,1:T(1,128)}, u32[]{:S(2)}) copy-start(s32[64,1]{0,1:T(1,128)} %param.15) | copy-start | bytes 772
  0.7 2.0 %copy-start.1 = (bf16[2,2048]{1,0:T(2,128)(2,1)S(1)}, bf16[2,2048]{1,0:T(2,128)(2,1)}, u32[]{:S(2)}) copy-start(bf16[2,2048]{1,0:T(2,128)(2,1)} %weights.1) | copy-start | bytes 24580
  5.9 23.3 %collective-permute-start = (bf16[320,1280]{1,0:T(8,128)(2,1)S(1)}, bf16[320,1280]{1,0:T(8,128)(2,1)S(1)}, u32[]{:S(2)}, u32[]{:S(2)}) collective-permute-start(bf16[320,1280]{1,0:T(8,128)(2,1)S(1)} %get-tuple-element.26), channel_id=1, source_target_pairs={{0,1},{1,0},{2,3},{3,2},{4,5},{5,4},{6,7},{7,6},{8,9},{9,8},{10,11... | collective-permute-start | bytes 2457608 | tf_op jit(solution)/shard_map/ppermute | solution.py:595
  6.6 22.6 %collective-permute-start.1 = (bf16[192,1280]{1,0:T(8,128)(2,1)S(1)}, bf16[192,1280]{1,0:T(8,128)(2,1)S(1)}, u32[]{:S(2)}, u32[]{:S(2)}) collective-permute-start(bf16[192,1280]{1,0:T(8,128)(2,1)S(1)} %shard_map.112), channel_id=1, source_target_pairs={{1,2},{2,1},{3,4},{4,3},{5,6},{6,5},{7,8},{8,7},{9,10},{10,9},{11,... | collective-permute-start | bytes 1474568 | tf_op jit(solution)/shard_map/ppermute | solution.py:595
  9.7 30.0 %collective-permute-start.2 = (bf16[128,1280]{1,0:T(8,128)(2,1)S(1)}, bf16[128,1280]{1,0:T(8,128)(2,1)S(1)}, u32[]{:S(2)}, u32[]{:S(2)}) collective-permute-start(bf16[128,1280]{1,0:T(8,128)(2,1)S(1)} %get-tuple-element.30), channel_id=1, source_target_pairs={{1,2},{2,1},{3,4},{4,3},{5,6},{6,5},{7,8},{8,7},{9,10},{10,9},{11,... | collective-permute-start | bytes 983048 | tf_op jit(solution)/shard_map/ppermute | solution.py:595
  36.5 17.2 %collective-permute-start.5 = (bf16[192,1280]{1,0:T(8,128)(2,1)S(1)}, bf16[192,1280]{1,0:T(8,128)(2,1)S(1)}, u32[]{:S(2)}, u32[]{:S(2)}) collective-permute-start(bf16[192,1280]{1,0:T(8,128)(2,1)S(1)} %get-tuple-element.38), channel_id=1, source_target_pairs={{0,1},{1,0},{2,3},{3,2},{4,5},{5,4},{6,7},{7,6},{8,9},{9,8},{10,11... | collective-permute-start | bytes 1474568 | tf_op jit(solution)/shard_map/ppermute | solution.py:595
  37.2 18.9 %collective-permute-start.6 = (bf16[192,1280]{1,0:T(8,128)(2,1)S(1)}, bf16[192,1280]{1,0:T(8,128)(2,1)S(1)}, u32[]{:S(2)}, u32[]{:S(2)}) collective-permute-start(bf16[192,1280]{1,0:T(8,128)(2,1)S(1)} %get-tuple-element.39), channel_id=1, source_target_pairs={{1,2},{2,1},{3,4},{4,3},{5,6},{6,5},{7,8},{8,7},{9,10},{10,9},{11,... | collective-permute-start | bytes 1474568 | tf_op jit(solution)/shard_map/ppermute | solution.py:595
  44.9 19.2 %collective-permute-start.3 = (bf16[128,1280]{1,0:T(8,128)(2,1)S(1)}, bf16[128,1280]{1,0:T(8,128)(2,1)S(1)}, u32[]{:S(2)}, u32[]{:S(2)}) collective-permute-start(bf16[128,1280]{1,0:T(8,128)(2,1)S(1)} %get-tuple-element.36), channel_id=1, source_target_pairs={{0,1},{1,0},{2,3},{3,2},{4,5},{5,4},{6,7},{7,6},{8,9},{9,8},{10,11... | collective-permute-start | bytes 983048 | tf_op jit(solution)/shard_map/ppermute | solution.py:595
  45.4 18.8 %collective-permute-start.4 = (bf16[128,1280]{1,0:T(8,128)(2,1)S(1)}, bf16[128,1280]{1,0:T(8,128)(2,1)S(1)}, u32[]{:S(2)}, u32[]{:S(2)}) collective-permute-start(bf16[128,1280]{1,0:T(8,128)(2,1)S(1)} %get-tuple-element.37), channel_id=1, source_target_pairs={{1,2},{2,1},{3,4},{4,3},{5,6},{6,5},{7,8},{8,7},{9,10},{10,9},{11,... | collective-permute-start | bytes 983048 | tf_op jit(solution)/shard_map/ppermute | solution.py:595

commit v9 on v8

--- a/solution.py
+++ b/solution.py
@@ -378,29 +378,26 @@
     inject(step, got, lap, number * depth, first, count, width_x)
 
 
-def first_kernel(first, width_x, more, now, prior, velocity, lanes, got, got_on, got_off, *refs):
-    part, on_ref, off_ref = refs[:3]
-    following = refs[3] if more else None
-    tiles, lap, high_buf, low_buf, band_buf, now_buf, prior_buf, speed_buf, sems, band_sem = refs[-10:]
+def first_kernel(first, width_x, now, prior, velocity, lanes, got, got_on, got_off, *refs):
+    part, on_ref, off_ref, held, speed = refs[:5]
+    tiles, lap, high_buf, low_buf, prior_buf, sems, band_sem = refs[-7:]
     depth, count, width_y = part.shape
     low, high = max(first - SUB, 0), min(first + count + SUB, width_x)
-    now_copies = fetch(now, now_buf, sems.at[0], low, high - low) if more else []
-    weights = pltpu.make_async_copy(lanes, band_buf, band_sem)
-    weights.start()
+    now_copies = fetch(now, held, sems.at[0], low, high - low)
+    keep_band = len(refs) > 12
+    if keep_band:
+        weights = pltpu.make_async_copy(lanes, refs[5], band_sem)
+        weights.start()
     copies = fetch(prior, prior_buf, sems.at[1], first, count)
-    copies += fetch(velocity, speed_buf, sems.at[2], first, count)
-    if more:
-        copies += fetch(now, following, sems.at[3], width_x - more, more)
+    copies += fetch(velocity, speed, sems.at[2], first, count)
     prepare(0, first, count, width_x, depth, width_y, got, tiles, lap)
     for copy, (row, size) in zip(now_copies, blocks_of(low, high - low)):
         copy.wait()
-        spread(tiles, count, now_buf, row - low, row - first, size)
-    held = now_buf if more else now
-    if not more:
-        spread(tiles, count, now, 0, low - first, high - low)
+        spread(tiles, count, held, row - low, row - first, size)
     halve(high_buf, low_buf, held, first - low, count)
-    weights.wait()
-    add_lanes(high_buf, low_buf, band_buf, lap)
+    if keep_band:
+        weights.wait()
+    add_lanes(high_buf, low_buf, refs[5] if keep_band else lanes, lap)
     add_rows(tiles, lap, depth, count, len(tile_parts(width_y)))
     for copy in copies:
         copy.wait()
@@ -416,7 +413,7 @@
             if halo[j] is not None:
                 change = change + halo[j]
             value = 2.0 * held[z, here, :] - prior_buf[z, rows, :]
-            value = value + speed_buf[z, rows, :] * change
+            value = value + speed[z, rows, :] * change
             part[z, rows, :] = value
             u.append(value)
         put(off_ref, rows, encode(u[::-1][:HALO]))
@@ -425,29 +422,18 @@
     row_loop(count, body)
 
 
-def second_local(first, starts, parts, now, velocity, forward, lanes, got, stencil, bufs, sems):
-    now_buf, speed_buf, *forward_bufs = bufs
-    tiles, lap, high_buf, low_buf, band_buf, band_sem = stencil
-    depth, width_x, width_y = now.shape
-    count = now_buf.shape[1]
-    weights = pltpu.make_async_copy(lanes, band_buf, band_sem)
-    weights.start()
+def second_local(first, starts, parts, width_x, lanes, got, stencil):
+    tiles, lap, high_buf, low_buf = stencil
+    here = parts[starts.index(first)]
+    depth, count, width_y = here.shape
     low, high = max(first - SUB, 0), min(first + count + SUB, width_x)
-    copies = fetch(now, now_buf, sems.at[0], first, count)
-    copies += fetch(velocity, speed_buf, sems.at[1], first, count)
-    for s in range(STEPS):
-        copies += fetch(forward.at[s], forward_bufs[s], sems.at[2 + s], first, count)
     prepare(1, first, count, width_x, depth, width_y, got, tiles, lap)
     for start, part in zip(starts, parts):
         row, end = max(low, start), min(high, start + part.shape[1])
         spread(tiles, count, part, row - start, row - first, end - row)
-    here = parts[starts.index(first)]
     halve(high_buf, low_buf, here, 0, count)
-    weights.wait()
-    add_lanes(high_buf, low_buf, band_buf, lap)
+    add_lanes(high_buf, low_buf, lanes, lap)
     add_rows(tiles, lap, depth, count, len(tile_parts(width_y)))
-    for copy in copies:
-        copy.wait()
     return here
 
 
@@ -464,26 +450,22 @@
 
 def second_kernel(first, starts, *refs):
     parts, refs = refs[: len(starts)], refs[len(starts) :]
-    now, velocity, forward, lanes, got, got_on, got_off, out, image, current = refs[:10]
-    stencil, bufs = refs[10:16], refs[16:20]
-    out_buf, image_buf, sems, out_sems, part_sems = refs[20:]
+    held, speed, forward, lanes, got, got_on, got_off, out, image = refs[:9]
+    stencil = refs[9:13]
+    out_buf, image_buf, out_sems = refs[13:]
     lap = stencil[1]
-    depth, _, width_y = now.shape
+    depth, width_x, width_y = out.shape
     count = out_buf.shape[1]
+    back = first - max(first - SUB, 0)
     writes = []
-    for i, (start, part) in enumerate(zip(starts, parts)):
-        write = pltpu.make_async_copy(
-            part, current.at[:, pl.ds(start, part.shape[1])], part_sems.at[i]
-        )
-        write.start()
-        writes.append(write)
-    here = second_local(first, starts, parts, now, velocity, forward, lanes, got, stencil, bufs, sems)
-    now_buf, speed_buf, early, late = bufs
+    here = second_local(first, starts, parts, width_x, lanes, got, stencil)
     for n, i in enumerate(range(0, count, BLOCK)):
 
         def body(r):
             r = r + i
             rows = pl.ds(r, ROWS)
+            whole = pl.ds(r + first, ROWS)
+            before = pl.ds(pl.multiple_of(r + back, SUB), ROWS)
             halo = halo_sum(got_on, rows, got_off, rows, width_y, depth)
             for j in range(depth):
                 z = depth_at(j, depth)
@@ -491,9 +473,9 @@
                 if halo[j] is not None:
                     change = change + halo[j]
                 mine = here[z, rows, :]
-                value = 2.0 * mine - now_buf[z, rows, :] + speed_buf[z, rows, :] * change
+                value = 2.0 * mine - held[z, before, :] + speed[z, rows, :] * change
                 out_buf[z, rows, :] = value
-                image_buf[z, rows, :] = early[z, rows, :] * mine + late[z, rows, :] * value
+                image_buf[z, rows, :] = forward[0, z, whole, :] * mine + forward[1, z, whole, :] * value
 
         row_loop(BLOCK, body)
         writes += send_rows(((out_buf, out), (image_buf, image)), first, i, out_sems, n)
@@ -503,27 +485,36 @@
 
 def partial_kernel(first, starts, *refs):
     parts, refs = refs[: len(starts)], refs[len(starts) :]
-    now, velocity, forward, lanes, got, out, image, speed, late = refs[:9]
-    stencil, (now_buf, early, sems) = refs[9:15], refs[15:]
+    held, speed, forward, lanes, got, current, out, image = refs[:8]
+    stencil, sems = refs[8:12], refs[12]
     lap = stencil[1]
-    depth, _, width_y = now.shape
-    count = now_buf.shape[1]
-    bufs = (now_buf, speed, early, late)
-    here = second_local(first, starts, parts, now, velocity, forward, lanes, got, stencil, bufs, sems)
+    width_x = current.shape[1]
+    depth, count, width_y = out.shape
+    back = first - max(first - SUB, 0)
+    writes = []
+    for i, (start, part) in enumerate(zip(starts, parts)):
+        write = pltpu.make_async_copy(part, current.at[:, pl.ds(start, part.shape[1])], sems.at[i])
+        write.start()
+        writes.append(write)
+    here = second_local(first, starts, parts, width_x, lanes, got, stencil)
 
     def body(r):
         rows = pl.ds(r, ROWS)
+        whole = pl.ds(r + first, ROWS)
+        before = pl.ds(pl.multiple_of(r + back, SUB), ROWS)
         for z in range(depth):
             change = lap_rows(lap, z, r, depth, count, width_y)
             mine = here[z, rows, :]
-            value = 2.0 * mine - now_buf[z, rows, :] + speed[z, rows, :] * change
+            value = 2.0 * mine - held[z, before, :] + speed[z, rows, :] * change
             out[z, rows, :] = value
-            image[z, rows, :] = early[z, rows, :] * mine + late[z, rows, :] * value
+            image[z, rows, :] = forward[0, z, whole, :] * mine + forward[1, z, whole, :] * value
 
     row_loop(count, body)
-
-
-def last_kernel(first, partial, image_in, speed, late, got_on, got_off, *refs):
+    for write in writes:
+        write.wait()
+
+
+def last_kernel(first, partial, image_in, speed, forward, got_on, got_off, *refs):
     out, image, out_buf, image_buf, sems = refs[-5:]
     depth, count, width_y = out_buf.shape
     writes = []
@@ -531,12 +522,13 @@
 
         def body(r):
             rows = pl.ds(r + i, ROWS)
+            whole = pl.ds(r + (first + i), ROWS)
             halo = halo_sum(got_on, rows, got_off, rows, width_y, depth)
             for j in range(depth):
                 z = depth_at(j, depth)
                 extra = speed[z, rows, :] * halo[j] if halo[j] is not None else 0.0
                 out_buf[z, rows, :] = partial[z, rows, :] + extra
-                image_buf[z, rows, :] = image_in[z, rows, :] + late[z, rows, :] * extra
+                image_buf[z, rows, :] = image_in[z, rows, :] + forward[1, z, whole, :] * extra
 
         row_loop(BLOCK, body)
         writes += send_rows(((out_buf, out), (image_buf, image)), first, i, sems, n)
@@ -545,8 +537,8 @@
 
 
 def shard(now, prior, velocity, forward, traces, weights, target, cell):
-    now, prior, velocity, forward = (
-        pltpu.with_memory_space_constraint(x, pltpu.HBM) for x in (now, prior, velocity, forward)
+    now, prior, velocity = (
+        pltpu.with_memory_space_constraint(x, pltpu.HBM) for x in (now, prior, velocity)
     )
     slabs = lax.axis_size("slab")
     depth, width_x, width_y = now.shape
@@ -575,7 +567,7 @@
         tiles = pltpu.VMEM((number * depth * (count + 2 * SUB), LANES), F32)
         lap = pltpu.VMEM((number * depth * count + SUB, LANES), F32)
         half = pltpu.VMEM((depth * count, number * LANES), BF16)
-        return (tiles, lap, half, half, pltpu.VMEM(lanes.shape, BF16))
+        return (tiles, lap, half, half)
 
     def blocks(count):
         return -(-count // BLOCK)
@@ -618,50 +610,38 @@
     )(later)
     got_off.append(swap(face, off_pairs))
     got_on = swap(on_face, on_pairs)
-    parts, second_on, second_off = [], [], []
-    more = width_x - split + SUB
-    held = now
+    parts, held, speed, second_on, second_off = [], [], [], [], []
     for i, (first, count) in enumerate(chunks):
-        part, on_face, face, *following = call(
-            functools.partial(first_kernel, first, width_x, 0 if i else more),
-            [VMEM if i else HBM, HBM, HBM, HBM, SMEM, VMEM, VMEM],
-            [rows_of(count), plane(count), plane(count)] + ([] if i else [rows_of(more)]),
-            (
-                *stencil(count),
-                buffer(SUB if i else count + SUB),
-                buffer(count),
-                buffer(count),
-                dma((4, blocks(width_x))),
-                dma,
-            ),
-        )(held, prior, velocity, lanes, got, got_on, got_off[i])
+        near = min(first + count + SUB, width_x) - max(first - SUB, 0)
+        keep = [] if i else [jax.ShapeDtypeStruct(lanes.shape, BF16)]
+        part, on_face, face, rows_held, rows_speed, *kept = call(
+            functools.partial(first_kernel, first, width_x),
+            [HBM] * 3 + [VMEM if i else HBM, SMEM, VMEM, VMEM],
+            [rows_of(count), plane(count), plane(count), rows_of(near), rows_of(count)] + keep,
+            (*stencil(count), buffer(count), dma((3, blocks(near))), dma),
+        )(now, prior, velocity, lanes, got, got_on, got_off[i])
+        lanes = kept[0] if kept else lanes
         second_off.append(swap(face, off_pairs))
         second_on.append(swap(on_face, on_pairs))
         parts.append(part)
-        if i == 0:
-            (held,) = following
-            part, prior = lax.optimization_barrier((part, prior))
+        held.append(rows_held)
+        speed.append(rows_speed)
+    parts[-1], forward = lax.optimization_barrier((parts[-1], forward))
     (first, count), (last, size) = chunks
-    second, image, current = call(
+    current, partial, image_part = call(
+        functools.partial(partial_kernel, last, starts),
+        [VMEM] * (len(parts) + 4) + [SMEM],
+        [field, rows_of(size), rows_of(size)],
+        (*stencil(size), dma((len(parts),))),
+        [HBM, VMEM, VMEM],
+    )(*parts, held[1], speed[1], forward, lanes, got)
+    second, image = call(
         functools.partial(second_kernel, first, starts),
-        [VMEM] * len(parts) + [HBM] * 4 + [SMEM, VMEM, VMEM],
-        [field, field, field],
-        (
-            *stencil(count),
-            dma,
-            *[buffer(count)] * 6,
-            dma((2 + STEPS, blocks(count))),
-            dma((2, blocks(count))),
-            dma((len(parts),)),
-        ),
-        [HBM] * 3,
-    )(*parts, now, velocity, forward, lanes, got, second_on[0], second_off[0])
-    partial, image_part, speed, late = call(
-        functools.partial(partial_kernel, last, starts),
-        [VMEM] * len(parts) + [HBM] * 4 + [SMEM],
-        [rows_of(size)] * 4,
-        (*stencil(size), dma, buffer(size), buffer(size), dma((2 + STEPS, blocks(size)))),
-    )(*parts, now, velocity, forward, lanes, got)
+        [VMEM] * (len(parts) + 4) + [SMEM, VMEM, VMEM],
+        [field, field],
+        (*stencil(count), buffer(count), buffer(count), dma((2, blocks(count)))),
+        [HBM] * 2,
+    )(*parts, held[0], speed[0], forward, lanes, got, second_on[0], second_off[0])
     second, image = call(
         functools.partial(last_kernel, last),
         [VMEM] * 6 + [HBM] * 2,
@@ -669,7 +649,7 @@
         (buffer(size), buffer(size), dma((2, blocks(size)))),
         [HBM] * 2,
         input_output_aliases={6: 0, 7: 1},
-    )(partial, image_part, speed, late, second_on[1], second_off[1], second, image)
+    )(partial, image_part, speed[1], forward, second_on[1], second_off[1], second, image)
     return (image, second, current)
 
 

time: 66.1 us -> 63.2 us (0.956)
  Pallas kernels: 31.9 us -> 27.7 us
  waiting for transfers between devices: 2.4 us -> 3.74 us
    pallas_call x4, Pallas kernels: 25.1 us -> 21 us  [the longest x2 12 us: shard(): call(functools.partial(first_kernel, first, width_x), [HBM] * 3 + [VMEM i...]
    ppermute x7, waiting for transfers between devices: 2.4 us -> 3.74 us  [swap(): return lax.ppermute(face, 'slab', pairs)]
  transfers between devices with their start and end apart: 7 -> 7, of which waited for: 1 -> 1; matrix products, arithmetic and copies ran while one was open for 0% -> 0% of each run, Pallas kernels for 38% -> 33%
where the time goes in v9:
time: 63.2 us; the launch traced here: 62.9 us
  Pallas kernels  27.7 us (44%)
  blocking collectives  17 us (27%)
  starting transfers between devices  13.6 us (22%)
  waiting for transfers between devices  3.74 us (6%)
  between operations  0.83 us (1%)
    all_to_all x1, blocking collectives, shard(): got = lax.all_to_all(sent, 'slab', split_axis=0, concat_axis=0, tiled=True)  17 us
    ppermute x7, starting transfers between devices, swap(): return lax.ppermute(face, 'slab', pairs)  13.6 us
    pallas_call x2, Pallas kernels, shard(): call(functools.partial(first_kernel, first, width_x), [HBM] * 3 + [VMEM i...  12 us
    pallas_call x1, Pallas kernels, shard(): call(functools.partial(second_kernel, first, starts), [VMEM] * (len(parts...  5.66 us
    ppermute x7, waiting for transfers between devices, swap(): return lax.ppermute(face, 'slab', pairs)  3.74 us
    pallas_call x1, Pallas kernels, shard(): call(functools.partial(partial_kernel, last, starts), [VMEM] * (len(parts...  3.29 us
    pallas_call x1, Pallas kernels, shard(): call(functools.partial(pack_kernel, split, True), [HBM], [plane(width_x),...  2.78 us
    pallas_call x1, Pallas kernels, shard(): call(functools.partial(pack_kernel, 0, False), [HBM], [plane(split)], (bu...  1.99 us
  transfers between devices with their start and end apart: 7, of which 1 were waited for; matrix products, arithmetic and copies ran while one was open for 0% of the time, Pallas kernels for 33%

profile of v9, /device:TPU:9, one launch (start us, length us, event | category | flops | bytes accessed | tf_op | source)
XLA Modules:
  0.0 62.9 jit_solution(6328178261027935957)
XLA Ops:
  0.6 0.0 copy-start.1
  0.6 0.0 copy-start.4
  0.7 0.0 copy-start.3
  0.7 0.0 copy-start.2
  0.7 2.0 %shard_map.112 = bf16[192,1280]{1,0:T(8,128)(2,1)S(1)} custom-call(f32[4,320,320]{2,1,0:T(8,128)} %now.6), custom_call_target="tpu_custom_call" | custom-call | tf_op jit(solution)/shard_map/pallas_call | solution.py:590
  2.7 0.0 copy-done.1
  2.7 0.0 copy-done.4
  2.7 0.0 copy-done.3
  2.7 0.0 copy-done.2
  2.7 0.4 shard_map.113
  3.1 2.8 %shard_map.114 = (bf16[320,1280]{1,0:T(8,128)(2,1)S(1)}, bf16[128,1280]{1,0:T(8,128)(2,1)S(1)}) custom-call(f32[4,320,320]{2,1,0:T(8,128)} %now.6), custom_call_target="tpu_custom_call" | custom-call | tf_op jit(solution)/shard_map/pallas_call | solution.py:605
  5.9 0.7 %collective-permute-start = (bf16[320,1280]{1,0:T(8,128)(2,1)S(1)}, bf16[320,1280]{1,0:T(8,128)(2,1)S(1)}, u32[]{:S(2)}, u32[]{:S(2)}) collective-permute-start(bf16[320,1280]{1,0:T(8,128)(2,1)S(1)} %get-tuple-element.29), channel_id=1, source_target_pairs={{0,1},{1,0},{2,3},{3,2},{4,5},{5,4},{6,7},{7,6},{8,9},{9,8},{10,11... | collective-permute-start | bytes 2457608 | tf_op jit(solution)/shard_map/ppermute | solution.py:587
  6.6 3.0 %collective-permute-start.1 = (bf16[192,1280]{1,0:T(8,128)(2,1)S(1)}, bf16[192,1280]{1,0:T(8,128)(2,1)S(1)}, u32[]{:S(2)}, u32[]{:S(2)}) collective-permute-start(bf16[192,1280]{1,0:T(8,128)(2,1)S(1)} %shard_map.112), channel_id=1, source_target_pairs={{1,2},{2,1},{3,4},{4,3},{5,6},{6,5},{7,8},{8,7},{9,10},{10,9},{11,... | collective-permute-start | bytes 1474568 | tf_op jit(solution)/shard_map/ppermute | solution.py:587
  9.7 2.5 %collective-permute-start.2 = (bf16[128,1280]{1,0:T(8,128)(2,1)S(1)}, bf16[128,1280]{1,0:T(8,128)(2,1)S(1)}, u32[]{:S(2)}, u32[]{:S(2)}) collective-permute-start(bf16[128,1280]{1,0:T(8,128)(2,1)S(1)} %get-tuple-element.32), channel_id=1, source_target_pairs={{1,2},{2,1},{3,4},{4,3},{5,6},{6,5},{7,8},{8,7},{9,10},{10,9},{11,... | collective-permute-start | bytes 983048 | tf_op jit(solution)/shard_map/ppermute | solution.py:587
  12.2 17.0 %all_to_all.5.got.refs_6_ = f32[16,1,128]{2,1,0:T(1,128)S(1)} all-to-all(f32[16,1,128]{2,1,0:T(1,128)S(1)} %shard_map.113), channel_id=1, replica_groups=mesh['groups'=2,'slab'=16] {'slab'}, dimensions={0} | all-to-all | bytes 16384 | tf_op jit(solution)/shard_map/all_to_all | solution.py:603
  29.2 0.0 collective-permute-done.1.got_off
  29.2 0.0 collective-permute-done.got_on
  29.2 6.8 %shard_map.115 = (f32[4,192,320]{2,1,0:T(8,128)S(1)}, bf16[192,1280]{1,0:T(8,128)(2,1)S(1)}, bf16[192,1280]{1,0:T(8,128)(2,1)S(1)}, f32[4,200,320]{2,1,0:T(8,128...) custom-call(f32[4,320,320]{2,1,0:T(8,128)} %now.6, f32[4,320,320]{2,1,0:T(8,128)} %prior.3, ...), custom_call_target="tpu_custom_call" | custom-call | tf_op jit(solution)/shard_map/pallas_call | solution.py:617
  36.1 0.7 %collective-permute-start.5 = (bf16[192,1280]{1,0:T(8,128)(2,1)S(1)}, bf16[192,1280]{1,0:T(8,128)(2,1)S(1)}, u32[]{:S(2)}, u32[]{:S(2)}) collective-permute-start(bf16[192,1280]{1,0:T(8,128)(2,1)S(1)} %get-tuple-element.44), channel_id=1, source_target_pairs={{0,1},{1,0},{2,3},{3,2},{4,5},{5,4},{6,7},{7,6},{8,9},{9,8},{10,11... | collective-permute-start | bytes 1474568 | tf_op jit(solution)/shard_map/ppermute | solution.py:587
  36.7 2.5 %collective-permute-start.6 = (bf16[192,1280]{1,0:T(8,128)(2,1)S(1)}, bf16[192,1280]{1,0:T(8,128)(2,1)S(1)}, u32[]{:S(2)}, u32[]{:S(2)}) collective-permute-start(bf16[192,1280]{1,0:T(8,128)(2,1)S(1)} %get-tuple-element.45), channel_id=1, source_target_pairs={{1,2},{2,1},{3,4},{4,3},{5,6},{6,5},{7,8},{8,7},{9,10},{10,9},{11,... | collective-permute-start | bytes 1474568 | tf_op jit(solution)/shard_map/ppermute | solution.py:587
  39.2 0.0 collective-permute-done.2.got_off
  39.2 0.0 copy-start
  39.2 5.2 %shard_map.116 = (f32[4,128,320]{2,1,0:T(8,128)S(1)}, bf16[128,1280]{1,0:T(8,128)(2,1)S(1)}, bf16[128,1280]{1,0:T(8,128)(2,1)S(1)}, f32[4,136,320]{2,1,0:T(8,128)S(1)}, f32[4,128,320]{2,1,0:T(8,128)S(1)}) custom-call(f32[4,320,320]{2,1,0:T(8,128)} %now.6, f32[4,320,320]{2,1,0:T(8,128)} %prior.3, f32[4,320,320]{2,1,0:T(8,128)} %velocity.3, ...), custom_call_target="tpu_custom_call" | custom-call | tf_op jit(solution)/shard_map/pallas_call | solution.py:617
  44.4 0.4 collective-permute-start.3
  44.9 3.7 %collective-permute-start.4 = (bf16[128,1280]{1,0:T(8,128)(2,1)S(1)}, bf16[128,1280]{1,0:T(8,128)(2,1)S(1)}, u32[]{:S(2)}, u32[]{:S(2)}) collective-permute-start(bf16[128,1280]{1,0:T(8,128)(2,1)S(1)} %get-tuple-element.41), channel_id=1, source_target_pairs={{1,2},{2,1},{3,4},{4,3},{5,6},{6,5},{7,8},{8,7},{9,10},{10,9},{11,... | collective-permute-start | bytes 983048 | tf_op jit(solution)/shard_map/ppermute | solution.py:587
  48.6 0.0 copy-done
  48.6 3.3 %shard_map.117 = (f32[4,320,320]{2,1,0:T(8,128)}, f32[4,128,320]{2,1,0:T(8,128)S(1)}, f32[4,128,320]{2,1,0:T(8,128)S(1)}) custom-call(f32[4,192,320]{2,1,0:T(8,128)S(1)} %get-tuple-element.30.refs_0_, f32[4,128,320]{2,1,0:T(8,128)S(1)} %get-tuple-element.34.refs_1_, f32[4,136,320]{2,1,0:T(8,128)S(1)} %get-tuple-element.35.refs_2_, ...), custom_call_target="tpu_custom_call" | custom-call | tf_op jit(solution)/shard_map/pallas_call | solution.py:631
  51.9 0.0 collective-permute-done.5.refs_7_
  51.9 3.7 %collective-permute-done.6.refs_8_ = bf16[192,1280]{1,0:T(8,128)(2,1)S(1)} collective-permute-done((bf16[192,1280]{1,0:T(8,128)(2,1)S(1)}, bf16[192,1280]{1,0:T(8,128)(2,1)S(1)}, u32[]{:S(2)}, u32[]{:S(2)}) %collective-permute-start.6) | collective-permute-done | bytes 491552 | tf_op jit(solution)/shard_map/ppermute | solution.py:587
  55.6 5.7 %shard_map.118 = (f32[4,320,320]{2,1,0:T(8,128)}, f32[4,320,320]{2,1,0:T(8,128)}) custom-call(f32[4,192,320]{2,1,0:T(8,128)S(1)} %get-tuple-element.30.refs_0_, f32[4,128,320]{2,1,0:T(8,128)S(1)} %get-tuple-element.34.refs_1_, f32[4,200,320]{2,1,0:T(8,128)S(1)} %get-tuple-element.42.refs_2_, f32[4,192,320]{2,1,0:T(8,128)S(1)} %get-tuple-element.43.refs_3_, ...), custom_call_target="tpu_custom_call" | custom-call | tf_op jit(solution)/shard_map/pallas_call | solution.py:638
  61.3 0.0 collective-permute-done.3.got_on
  61.3 0.0 collective-permute-done.4.got_off
  61.3 1.6 %shard_map.119 = (f32[4,320,320]{2,1,0:T(8,128)}, f32[4,320,320]{2,1,0:T(8,128)}) custom-call(f32[4,128,320]{2,1,0:T(8,128)S(1)} %get-tuple-element.38.partial, f32[4,128,320]{2,1,0:T(8,128)S(1)} %get-tuple-element.39.image_in, f32[4,128,320]{2,1,0:T(8,128)S(1)} %get-tuple-element.36.refs_3_.speed, ...), custom_call_target="tpu_custom_call", output_to_operand_aliasing={{0}: (6, {}), {1}: (7, {})} | custom-call | tf_op jit(solution)/shard_map/pallas_call | solution.py:645
Async XLA Ops:
  0.6 2.0 %copy-start.1 = (bf16[64,2048]{1,0:T(8,128)(2,1)S(1)}, bf16[64,2048]{1,0:T(8,128)(2,1)}, u32[]{:S(2)}) copy-start(bf16[64,2048]{1,0:T(8,128)(2,1)} %traces) | copy-start | bytes 786436
  0.6 2.0 %copy-start.4 = (s32[64]{0:T(128)S(1)}, s32[64]{0:T(128)}, u32[]{:S(2)}) copy-start(s32[64]{0:T(128)} %param.16) | copy-start | bytes 772
  0.7 2.0 %copy-start.3 = (s32[64,1]{0,1:T(1,128)S(1)}, s32[64,1]{0,1:T(1,128)}, u32[]{:S(2)}) copy-start(s32[64,1]{0,1:T(1,128)} %param.15) | copy-start | bytes 772
  0.7 2.0 %copy-start.2 = (bf16[2,2048]{1,0:T(2,128)(2,1)S(1)}, bf16[2,2048]{1,0:T(2,128)(2,1)}, u32[]{:S(2)}) copy-start(bf16[2,2048]{1,0:T(2,128)(2,1)} %weights.1) | copy-start | bytes 24580
  5.9 23.3 %collective-permute-start = (bf16[320,1280]{1,0:T(8,128)(2,1)S(1)}, bf16[320,1280]{1,0:T(8,128)(2,1)S(1)}, u32[]{:S(2)}, u32[]{:S(2)}) collective-permute-start(bf16[320,1280]{1,0:T(8,128)(2,1)S(1)} %get-tuple-element.29), channel_id=1, source_target_pairs={{0,1},{1,0},{2,3},{3,2},{4,5},{5,4},{6,7},{7,6},{8,9},{9,8},{10,11... | collective-permute-start | bytes 2457608 | tf_op jit(solution)/shard_map/ppermute | solution.py:587
  6.6 22.6 %collective-permute-start.1 = (bf16[192,1280]{1,0:T(8,128)(2,1)S(1)}, bf16[192,1280]{1,0:T(8,128)(2,1)S(1)}, u32[]{:S(2)}, u32[]{:S(2)}) collective-permute-start(bf16[192,1280]{1,0:T(8,128)(2,1)S(1)} %shard_map.112), channel_id=1, source_target_pairs={{1,2},{2,1},{3,4},{4,3},{5,6},{6,5},{7,8},{8,7},{9,10},{10,9},{11,... | collective-permute-start | bytes 1474568 | tf_op jit(solution)/shard_map/ppermute | solution.py:587
  9.7 29.5 %collective-permute-start.2 = (bf16[128,1280]{1,0:T(8,128)(2,1)S(1)}, bf16[128,1280]{1,0:T(8,128)(2,1)S(1)}, u32[]{:S(2)}, u32[]{:S(2)}) collective-permute-start(bf16[128,1280]{1,0:T(8,128)(2,1)S(1)} %get-tuple-element.32), channel_id=1, source_target_pairs={{1,2},{2,1},{3,4},{4,3},{5,6},{6,5},{7,8},{8,7},{9,10},{10,9},{11,... | collective-permute-start | bytes 983048 | tf_op jit(solution)/shard_map/ppermute | solution.py:587
  36.1 15.8 %collective-permute-start.5 = (bf16[192,1280]{1,0:T(8,128)(2,1)S(1)}, bf16[192,1280]{1,0:T(8,128)(2,1)S(1)}, u32[]{:S(2)}, u32[]{:S(2)}) collective-permute-start(bf16[192,1280]{1,0:T(8,128)(2,1)S(1)} %get-tuple-element.44), channel_id=1, source_target_pairs={{0,1},{1,0},{2,3},{3,2},{4,5},{5,4},{6,7},{7,6},{8,9},{9,8},{10,11... | collective-permute-start | bytes 1474568 | tf_op jit(solution)/shard_map/ppermute | solution.py:587
  36.7 18.9 %collective-permute-start.6 = (bf16[192,1280]{1,0:T(8,128)(2,1)S(1)}, bf16[192,1280]{1,0:T(8,128)(2,1)S(1)}, u32[]{:S(2)}, u32[]{:S(2)}) collective-permute-start(bf16[192,1280]{1,0:T(8,128)(2,1)S(1)} %get-tuple-element.45), channel_id=1, source_target_pairs={{1,2},{2,1},{3,4},{4,3},{5,6},{6,5},{7,8},{8,7},{9,10},{10,9},{11,... | collective-permute-start | bytes 1474568 | tf_op jit(solution)/shard_map/ppermute | solution.py:587
  39.2 9.4 %copy-start = (f32[2,4,320,320]{3,2,1,0:T(8,128)S(1)}, f32[2,4,320,320]{3,2,1,0:T(8,128)}, u32[]{:S(2)}) copy-start(f32[2,4,320,320]{3,2,1,0:T(8,128)} %forward) | copy-start | bytes 9830404
  44.4 16.9 %collective-permute-start.3 = (bf16[128,1280]{1,0:T(8,128)(2,1)S(1)}, bf16[128,1280]{1,0:T(8,128)(2,1)S(1)}, u32[]{:S(2)}, u32[]{:S(2)}) collective-permute-start(bf16[128,1280]{1,0:T(8,128)(2,1)S(1)} %get-tuple-element.40), channel_id=1, source_target_pairs={{0,1},{1,0},{2,3},{3,2},{4,5},{5,4},{6,7},{7,6},{8,9},{9,8},{10,11... | collective-permute-start | bytes 983048 | tf_op jit(solution)/shard_map/ppermute | solution.py:587
  44.9 16.5 %collective-permute-start.4 = (bf16[128,1280]{1,0:T(8,128)(2,1)S(1)}, bf16[128,1280]{1,0:T(8,128)(2,1)S(1)}, u32[]{:S(2)}, u32[]{:S(2)}) collective-permute-start(bf16[128,1280]{1,0:T(8,128)(2,1)S(1)} %get-tuple-element.41), channel_id=1, source_target_pairs={{1,2},{2,1},{3,4},{4,3},{5,6},{6,5},{7,8},{8,7},{9,10},{10,9},{11,... | collective-permute-start | bytes 983048 | tf_op jit(solution)/shard_map/ppermute | solution.py:587

commit v10 on v9

--- a/solution.py
+++ b/solution.py
@@ -18,6 +18,7 @@
 SUB = 8
 UNROLL = 4
 SHARE = (3, 2)
+LATER = (1, 1)
 LANES = 128
 F32 = jnp.float32
 BF16 = jnp.bfloat16
@@ -378,7 +379,8 @@
     inject(step, got, lap, number * depth, first, count, width_x)
 
 
-def first_kernel(first, width_x, now, prior, velocity, lanes, got, got_on, got_off, *refs):
+def first_kernel(first, width_x, pieces, now, prior, velocity, lanes, got, got_on, *refs):
+    faces, refs = refs[: len(pieces)], refs[len(pieces) :]
     part, on_ref, off_ref, held, speed = refs[:5]
     tiles, lap, high_buf, low_buf, prior_buf, sems, band_sem = refs[-7:]
     depth, count, width_y = part.shape
@@ -402,24 +404,29 @@
     for copy in copies:
         copy.wait()
 
-    def body(r):
-        rows = pl.ds(r, ROWS)
-        here = pl.ds(pl.multiple_of(r + (first - low), SUB), ROWS)
-        halo = halo_sum(got_on, pl.ds(r + first, ROWS), got_off, rows, width_y, depth)
-        u = []
-        for j in range(depth):
-            z = depth_at(j, depth)
-            change = lap_rows(lap, z, r, depth, count, width_y)
-            if halo[j] is not None:
-                change = change + halo[j]
-            value = 2.0 * held[z, here, :] - prior_buf[z, rows, :]
-            value = value + speed[z, rows, :] * change
-            part[z, rows, :] = value
-            u.append(value)
-        put(off_ref, rows, encode(u[::-1][:HALO]))
-        put(on_ref, rows, encode(u[:HALO]))
-
-    row_loop(count, body)
+    for got_off, (start, size) in zip(faces, pieces):
+        row, end = max(first, start), min(first + count, start + size)
+
+        def body(r):
+            r = r + (row - first)
+            rows = pl.ds(r, ROWS)
+            here = pl.ds(pl.multiple_of(r + (first - low), SUB), ROWS)
+            there = pl.ds(r + (first - start), ROWS)
+            halo = halo_sum(got_on, pl.ds(r + first, ROWS), got_off, there, width_y, depth)
+            u = []
+            for j in range(depth):
+                z = depth_at(j, depth)
+                change = lap_rows(lap, z, r, depth, count, width_y)
+                if halo[j] is not None:
+                    change = change + halo[j]
+                value = 2.0 * held[z, here, :] - prior_buf[z, rows, :]
+                value = value + speed[z, rows, :] * change
+                part[z, rows, :] = value
+                u.append(value)
+            put(off_ref, rows, encode(u[::-1][:HALO]))
+            put(on_ref, rows, encode(u[:HALO]))
+
+        row_loop(end - row, body)
 
 
 def second_local(first, starts, parts, width_x, lanes, got, stencil):
@@ -536,6 +543,10 @@
         write.wait()
 
 
+def cut(width_x, share):
+    return width_x * share[0] // (sum(share) * BLOCK) * BLOCK
+
+
 def shard(now, prior, velocity, forward, traces, weights, target, cell):
     now, prior, velocity = (
         pltpu.with_memory_space_constraint(x, pltpu.HBM) for x in (now, prior, velocity)
@@ -545,8 +556,9 @@
     lanes = pltpu.with_memory_space_constraint(jnp.asarray(band(width_y)), pltpu.HBM)
     rows = traces.shape[0]
     face_lanes = payload_lanes(width_y)
-    split = width_x * SHARE[0] // (sum(SHARE) * BLOCK) * BLOCK
-    chunks = ((0, split), (split, width_x - split))
+    split = cut(width_x, SHARE)
+    early_chunks = ((0, split), (split, width_x - split))
+    chunks = ((0, cut(width_x, LATER)), (cut(width_x, LATER), width_x - cut(width_x, LATER)))
     starts = tuple(first for first, _ in chunks)
     field = jax.ShapeDtypeStruct(now.shape, F32)
     number = len(tile_parts(width_y))
@@ -612,14 +624,19 @@
     got_on = swap(on_face, on_pairs)
     parts, held, speed, second_on, second_off = [], [], [], [], []
     for i, (first, count) in enumerate(chunks):
+        pieces, faces = [], []
+        for piece, face in zip(early_chunks, got_off):
+            if piece[0] < first + count and first < sum(piece):
+                pieces.append(piece)
+                faces.append(face)
         near = min(first + count + SUB, width_x) - max(first - SUB, 0)
         keep = [] if i else [jax.ShapeDtypeStruct(lanes.shape, BF16)]
         part, on_face, face, rows_held, rows_speed, *kept = call(
-            functools.partial(first_kernel, first, width_x),
-            [HBM] * 3 + [VMEM if i else HBM, SMEM, VMEM, VMEM],
+            functools.partial(first_kernel, first, width_x, tuple(pieces)),
+            [HBM] * 3 + [VMEM if i else HBM, SMEM] + [VMEM] * (1 + len(faces)),
             [rows_of(count), plane(count), plane(count), rows_of(near), rows_of(count)] + keep,
             (*stencil(count), buffer(count), dma((3, blocks(near))), dma),
-        )(now, prior, velocity, lanes, got, got_on, got_off[i])
+        )(now, prior, velocity, lanes, got, got_on, *faces)
         lanes = kept[0] if kept else lanes
         second_off.append(swap(face, off_pairs))
         second_on.append(swap(on_face, on_pairs))

time: 63.2 us -> 60.7 us (0.960)
  waiting for transfers between devices: 3.74 us -> 1.13 us
    ppermute x7, waiting for transfers between devices: 3.74 us -> 1.13 us  [swap(): return lax.ppermute(face, 'slab', pairs)]
  transfers between devices with their start and end apart: 7 -> 7, of which waited for: 1 -> 1; matrix products, arithmetic and copies ran while one was open for 0% -> 0% of each run, Pallas kernels for 33% -> 34%
where the time goes in v10:
time: 60.7 us; the launch traced here: 60.3 us
  Pallas kernels  27.7 us (46%)
  blocking collectives  17 us (28%)
  starting transfers between devices  13.6 us (22%)
  waiting for transfers between devices  1.13 us (2%)
  between operations  0.83 us (1%)
    all_to_all x1, blocking collectives, shard(): got = lax.all_to_all(sent, 'slab', split_axis=0, concat_axis=0, tiled=True)  17 us
    ppermute x7, starting transfers between devices, swap(): return lax.ppermute(face, 'slab', pairs)  13.6 us
    pallas_call x2, Pallas kernels, shard(): call(functools.partial(first_kernel, first, width_x, tuple(pieces)), [HBM...  11.9 us
    pallas_call x1, Pallas kernels, shard(): call(functools.partial(second_kernel, first, starts), [VMEM] * (len(parts...  5.1 us
    pallas_call x1, Pallas kernels, shard(): call(functools.partial(partial_kernel, last, starts), [VMEM] * (len(parts...  3.74 us
    pallas_call x1, Pallas kernels, shard(): call(functools.partial(pack_kernel, split, True), [HBM], [plane(width_x),...  2.78 us
    pallas_call x1, Pallas kernels, shard(): call(functools.partial(pack_kernel, 0, False), [HBM], [plane(split)], (bu...  1.99 us
    pallas_call x1, Pallas kernels, shard(): call(functools.partial(last_kernel, last), [VMEM] * 6 + [HBM] * 2, [field...  1.81 us
  transfers between devices with their start and end apart: 7, of which 1 were waited for; matrix products, arithmetic and copies ran while one was open for 0% of the time, Pallas kernels for 34%

profile of v10, /device:TPU:9, one launch (start us, length us, event | category | flops | bytes accessed | tf_op | source)
XLA Modules:
  0.0 60.3 jit_solution(1431319024323416282)
XLA Ops:
  0.6 0.0 copy-start.1
  0.6 0.0 copy-start.4
  0.7 0.0 copy-start.3
  0.7 0.0 copy-start.2
  0.7 2.0 %shard_map.112 = bf16[192,1280]{1,0:T(8,128)(2,1)S(1)} custom-call(f32[4,320,320]{2,1,0:T(8,128)} %now.6), custom_call_target="tpu_custom_call" | custom-call | tf_op jit(solution)/shard_map/pallas_call | solution.py:602
  2.7 0.0 copy-done.1
  2.7 0.0 copy-done.4
  2.7 0.0 copy-done.3
  2.7 0.0 copy-done.2
  2.7 0.4 shard_map.113
  3.1 2.8 %shard_map.114 = (bf16[320,1280]{1,0:T(8,128)(2,1)S(1)}, bf16[128,1280]{1,0:T(8,128)(2,1)S(1)}) custom-call(f32[4,320,320]{2,1,0:T(8,128)} %now.6), custom_call_target="tpu_custom_call" | custom-call | tf_op jit(solution)/shard_map/pallas_call | solution.py:617
  5.9 0.7 %collective-permute-start = (bf16[320,1280]{1,0:T(8,128)(2,1)S(1)}, bf16[320,1280]{1,0:T(8,128)(2,1)S(1)}, u32[]{:S(2)}, u32[]{:S(2)}) collective-permute-start(bf16[320,1280]{1,0:T(8,128)(2,1)S(1)} %get-tuple-element.29), channel_id=1, source_target_pairs={{0,1},{1,0},{2,3},{3,2},{4,5},{5,4},{6,7},{7,6},{8,9},{9,8},{10,11... | collective-permute-start | bytes 2457608 | tf_op jit(solution)/shard_map/ppermute | solution.py:599
  6.6 3.0 %collective-permute-start.1 = (bf16[192,1280]{1,0:T(8,128)(2,1)S(1)}, bf16[192,1280]{1,0:T(8,128)(2,1)S(1)}, u32[]{:S(2)}, u32[]{:S(2)}) collective-permute-start(bf16[192,1280]{1,0:T(8,128)(2,1)S(1)} %shard_map.112), channel_id=1, source_target_pairs={{1,2},{2,1},{3,4},{4,3},{5,6},{6,5},{7,8},{8,7},{9,10},{10,9},{11,... | collective-permute-start | bytes 1474568 | tf_op jit(solution)/shard_map/ppermute | solution.py:599
  9.7 2.5 %collective-permute-start.2 = (bf16[128,1280]{1,0:T(8,128)(2,1)S(1)}, bf16[128,1280]{1,0:T(8,128)(2,1)S(1)}, u32[]{:S(2)}, u32[]{:S(2)}) collective-permute-start(bf16[128,1280]{1,0:T(8,128)(2,1)S(1)} %get-tuple-element.32), channel_id=1, source_target_pairs={{1,2},{2,1},{3,4},{4,3},{5,6},{6,5},{7,8},{8,7},{9,10},{10,9},{11,... | collective-permute-start | bytes 983048 | tf_op jit(solution)/shard_map/ppermute | solution.py:599
  12.2 17.0 %all_to_all.5.got.refs_6_ = f32[16,1,128]{2,1,0:T(1,128)S(1)} all-to-all(f32[16,1,128]{2,1,0:T(1,128)S(1)} %shard_map.113), channel_id=1, replica_groups=mesh['groups'=2,'slab'=16] {'slab'}, dimensions={0} | all-to-all | bytes 16384 | tf_op jit(solution)/shard_map/all_to_all | solution.py:615
  29.2 0.0 collective-permute-done.1.refs_0_
  29.2 0.0 collective-permute-done.got_on
  29.2 6.1 %shard_map.115 = (f32[4,160,320]{2,1,0:T(8,128)S(1)}, bf16[160,1280]{1,0:T(8,128)(2,1)S(1)}, bf16[160,1280]{1,0:T(8,128)(2,1)S(1)}, f32[4,168,320]{2,1,0:T(8,128...) custom-call(f32[4,320,320]{2,1,0:T(8,128)} %now.6, f32[4,320,320]{2,1,0:T(8,128)} %prior.3, ...), custom_call_target="tpu_custom_call" | custom-call | tf_op jit(solution)/shard_map/pallas_call | solution.py:634
  35.3 0.7 %collective-permute-start.5 = (bf16[160,1280]{1,0:T(8,128)(2,1)S(1)}, bf16[160,1280]{1,0:T(8,128)(2,1)S(1)}, u32[]{:S(2)}, u32[]{:S(2)}) collective-permute-start(bf16[160,1280]{1,0:T(8,128)(2,1)S(1)} %get-tuple-element.44), channel_id=1, source_target_pairs={{0,1},{1,0},{2,3},{3,2},{4,5},{5,4},{6,7},{7,6},{8,9},{9,8},{10,11... | collective-permute-start | bytes 1228808 | tf_op jit(solution)/shard_map/ppermute | solution.py:599
  35.9 2.5 %collective-permute-start.6 = (bf16[160,1280]{1,0:T(8,128)(2,1)S(1)}, bf16[160,1280]{1,0:T(8,128)(2,1)S(1)}, u32[]{:S(2)}, u32[]{:S(2)}) collective-permute-start(bf16[160,1280]{1,0:T(8,128)(2,1)S(1)} %get-tuple-element.45), channel_id=1, source_target_pairs={{1,2},{2,1},{3,4},{4,3},{5,6},{6,5},{7,8},{8,7},{9,10},{10,9},{11,... | collective-permute-start | bytes 1228808 | tf_op jit(solution)/shard_map/ppermute | solution.py:599
  38.4 0.0 collective-permute-done.2.refs_1_
  38.4 0.0 copy-start
  38.5 5.9 %shard_map.116 = (f32[4,160,320]{2,1,0:T(8,128)S(1)}, bf16[160,1280]{1,0:T(8,128)(2,1)S(1)}, bf16[160,1280]{1,0:T(8,128)(2,1)S(1)}, f32[4,168,320]{2,1,0:T(8,128)S(1)}, f32[4,160,320]{2,1,0:T(8,128)S(1)}) custom-call(f32[4,320,320]{2,1,0:T(8,128)} %now.6, f32[4,320,320]{2,1,0:T(8,128)} %prior.3, f32[4,320,320]{2,1,0:T(8,128)} %velocity.3, ...), custom_call_target="tpu_custom_call" | custom-call | tf_op jit(solution)/shard_map/pallas_call | solution.py:634
  44.3 0.4 collective-permute-start.3
  44.8 3.7 %collective-permute-start.4 = (bf16[160,1280]{1,0:T(8,128)(2,1)S(1)}, bf16[160,1280]{1,0:T(8,128)(2,1)S(1)}, u32[]{:S(2)}, u32[]{:S(2)}) collective-permute-start(bf16[160,1280]{1,0:T(8,128)(2,1)S(1)} %get-tuple-element.41), channel_id=1, source_target_pairs={{1,2},{2,1},{3,4},{4,3},{5,6},{6,5},{7,8},{8,7},{9,10},{10,9},{11,... | collective-permute-start | bytes 1228808 | tf_op jit(solution)/shard_map/ppermute | solution.py:599
  48.5 0.0 copy-done
  48.5 3.7 %shard_map.117 = (f32[4,320,320]{2,1,0:T(8,128)}, f32[4,160,320]{2,1,0:T(8,128)S(1)}, f32[4,160,320]{2,1,0:T(8,128)S(1)}) custom-call(f32[4,160,320]{2,1,0:T(8,128)S(1)} %get-tuple-element.30.refs_0_, f32[4,160,320]{2,1,0:T(8,128)S(1)} %get-tuple-element.34.refs_1_, f32[4,168,320]{2,1,0:T(8,128)S(1)} %get-tuple-element.35.refs_2_, ...), custom_call_target="tpu_custom_call" | custom-call | tf_op jit(solution)/shard_map/pallas_call | solution.py:648
  52.3 0.0 collective-permute-done.5.refs_7_
  52.3 0.0 collective-permute-done.6.refs_8_
  52.3 5.1 %shard_map.118 = (f32[4,320,320]{2,1,0:T(8,128)}, f32[4,320,320]{2,1,0:T(8,128)}) custom-call(f32[4,160,320]{2,1,0:T(8,128)S(1)} %get-tuple-element.30.refs_0_, f32[4,160,320]{2,1,0:T(8,128)S(1)} %get-tuple-element.34.refs_1_, f32[4,168,320]{2,1,0:T(8,128)S(1)} %get-tuple-element.42.refs_2_, f32[4,160,320]{2,1,0:T(8,128)S(1)} %get-tuple-element.43.refs_3_, ...), custom_call_target="tpu_custom_call" | custom-call | tf_op jit(solution)/shard_map/pallas_call | solution.py:655
  57.4 0.0 collective-permute-done.3.got_on
  57.4 1.1 %collective-permute-done.4.got_off = bf16[160,1280]{1,0:T(8,128)(2,1)S(1)} collective-permute-done((bf16[160,1280]{1,0:T(8,128)(2,1)S(1)}, bf16[160,1280]{1,0:T(8,128)(2,1)S(1)}, u32[]{:S(2)}, u32[]{:S(2)}) %collective-permute-start.4) | collective-permute-done | bytes 409632 | tf_op jit(solution)/shard_map/ppermute | solution.py:599
  58.5 1.8 %shard_map.119 = (f32[4,320,320]{2,1,0:T(8,128)}, f32[4,320,320]{2,1,0:T(8,128)}) custom-call(f32[4,160,320]{2,1,0:T(8,128)S(1)} %get-tuple-element.38.partial, f32[4,160,320]{2,1,0:T(8,128)S(1)} %get-tuple-element.39.image_in, f32[4,160,320]{2,1,0:T(8,128)S(1)} %get-tuple-element.36.refs_3_.speed, ...), custom_call_target="tpu_custom_call", output_to_operand_aliasing={{0}: (6, {}), {1}: (7, {})} | custom-call | tf_op jit(solution)/shard_map/pallas_call | solution.py:662
Async XLA Ops:
  0.6 2.0 %copy-start.1 = (bf16[64,2048]{1,0:T(8,128)(2,1)S(1)}, bf16[64,2048]{1,0:T(8,128)(2,1)}, u32[]{:S(2)}) copy-start(bf16[64,2048]{1,0:T(8,128)(2,1)} %traces) | copy-start | bytes 786436
  0.6 2.0 %copy-start.4 = (s32[64]{0:T(128)S(1)}, s32[64]{0:T(128)}, u32[]{:S(2)}) copy-start(s32[64]{0:T(128)} %param.16) | copy-start | bytes 772
  0.7 2.0 %copy-start.3 = (s32[64,1]{0,1:T(1,128)S(1)}, s32[64,1]{0,1:T(1,128)}, u32[]{:S(2)}) copy-start(s32[64,1]{0,1:T(1,128)} %param.15) | copy-start | bytes 772
  0.7 2.0 %copy-start.2 = (bf16[2,2048]{1,0:T(2,128)(2,1)S(1)}, bf16[2,2048]{1,0:T(2,128)(2,1)}, u32[]{:S(2)}) copy-start(bf16[2,2048]{1,0:T(2,128)(2,1)} %weights.1) | copy-start | bytes 24580
  5.9 23.3 %collective-permute-start = (bf16[320,1280]{1,0:T(8,128)(2,1)S(1)}, bf16[320,1280]{1,0:T(8,128)(2,1)S(1)}, u32[]{:S(2)}, u32[]{:S(2)}) collective-permute-start(bf16[320,1280]{1,0:T(8,128)(2,1)S(1)} %get-tuple-element.29), channel_id=1, source_target_pairs={{0,1},{1,0},{2,3},{3,2},{4,5},{5,4},{6,7},{7,6},{8,9},{9,8},{10,11... | collective-permute-start | bytes 2457608 | tf_op jit(solution)/shard_map/ppermute | solution.py:599
  6.6 22.6 %collective-permute-start.1 = (bf16[192,1280]{1,0:T(8,128)(2,1)S(1)}, bf16[192,1280]{1,0:T(8,128)(2,1)S(1)}, u32[]{:S(2)}, u32[]{:S(2)}) collective-permute-start(bf16[192,1280]{1,0:T(8,128)(2,1)S(1)} %shard_map.112), channel_id=1, source_target_pairs={{1,2},{2,1},{3,4},{4,3},{5,6},{6,5},{7,8},{8,7},{9,10},{10,9},{11,... | collective-permute-start | bytes 1474568 | tf_op jit(solution)/shard_map/ppermute | solution.py:599
  9.7 28.8 %collective-permute-start.2 = (bf16[128,1280]{1,0:T(8,128)(2,1)S(1)}, bf16[128,1280]{1,0:T(8,128)(2,1)S(1)}, u32[]{:S(2)}, u32[]{:S(2)}) collective-permute-start(bf16[128,1280]{1,0:T(8,128)(2,1)S(1)} %get-tuple-element.32), channel_id=1, source_target_pairs={{1,2},{2,1},{3,4},{4,3},{5,6},{6,5},{7,8},{8,7},{9,10},{10,9},{11,... | collective-permute-start | bytes 983048 | tf_op jit(solution)/shard_map/ppermute | solution.py:599
  35.3 17.0 %collective-permute-start.5 = (bf16[160,1280]{1,0:T(8,128)(2,1)S(1)}, bf16[160,1280]{1,0:T(8,128)(2,1)S(1)}, u32[]{:S(2)}, u32[]{:S(2)}) collective-permute-start(bf16[160,1280]{1,0:T(8,128)(2,1)S(1)} %get-tuple-element.44), channel_id=1, source_target_pairs={{0,1},{1,0},{2,3},{3,2},{4,5},{5,4},{6,7},{7,6},{8,9},{9,8},{10,11... | collective-permute-start | bytes 1228808 | tf_op jit(solution)/shard_map/ppermute | solution.py:599
  35.9 16.3 %collective-permute-start.6 = (bf16[160,1280]{1,0:T(8,128)(2,1)S(1)}, bf16[160,1280]{1,0:T(8,128)(2,1)S(1)}, u32[]{:S(2)}, u32[]{:S(2)}) collective-permute-start(bf16[160,1280]{1,0:T(8,128)(2,1)S(1)} %get-tuple-element.45), channel_id=1, source_target_pairs={{1,2},{2,1},{3,4},{4,3},{5,6},{6,5},{7,8},{8,7},{9,10},{10,9},{11,... | collective-permute-start | bytes 1228808 | tf_op jit(solution)/shard_map/ppermute | solution.py:599
  38.4 10.1 %copy-start = (f32[2,4,320,320]{3,2,1,0:T(8,128)S(1)}, f32[2,4,320,320]{3,2,1,0:T(8,128)}, u32[]{:S(2)}) copy-start(f32[2,4,320,320]{3,2,1,0:T(8,128)} %forward) | copy-start | bytes 9830404
  44.3 13.1 %collective-permute-start.3 = (bf16[160,1280]{1,0:T(8,128)(2,1)S(1)}, bf16[160,1280]{1,0:T(8,128)(2,1)S(1)}, u32[]{:S(2)}, u32[]{:S(2)}) collective-permute-start(bf16[160,1280]{1,0:T(8,128)(2,1)S(1)} %get-tuple-element.40), channel_id=1, source_target_pairs={{0,1},{1,0},{2,3},{3,2},{4,5},{5,4},{6,7},{7,6},{8,9},{9,8},{10,11... | collective-permute-start | bytes 1228808 | tf_op jit(solution)/shard_map/ppermute | solution.py:599
  44.8 13.8 %collective-permute-start.4 = (bf16[160,1280]{1,0:T(8,128)(2,1)S(1)}, bf16[160,1280]{1,0:T(8,128)(2,1)S(1)}, u32[]{:S(2)}, u32[]{:S(2)}) collective-permute-start(bf16[160,1280]{1,0:T(8,128)(2,1)S(1)} %get-tuple-element.41), channel_id=1, source_target_pairs={{1,2},{2,1},{3,4},{4,3},{5,6},{6,5},{7,8},{8,7},{9,10},{10,9},{11,... | collective-permute-start | bytes 1228808 | tf_op jit(solution)/shard_map/ppermute | solution.py:599

commit v11 on v10

--- a/solution.py
+++ b/solution.py
@@ -135,27 +135,26 @@
     return copies
 
 
-def pack_kernel(first, with_on, now, *refs):
-    refs = list(refs)
-    on_ref = refs.pop(0) if with_on else None
-    off_ref, buf, sems = refs
-    depth = now.shape[0]
-    base = 0 if with_on else first
-    copies = fetch(now, buf, sems, base, buf.shape[1])
-
-    for i, copy in enumerate(copies):
+def pack_rows(first, with_on, copies, buf, base, on_ref, off_ref):
+    depth, count, _ = buf.shape
+    for copy, (row, size) in zip(copies, blocks_of(0, count)):
         copy.wait()
 
         def body(r):
-            r = r + i * BLOCK
+            r = r + row
             rows = pl.ds(r, ROWS)
             u = [buf[depth_at(j, depth), rows, :] for j in range(depth)]
-            if base + i * BLOCK >= first and base + i * BLOCK < first + off_ref.shape[0]:
-                put(off_ref, pl.ds(r + base - first, ROWS), encode(u[::-1][:HALO]))
+            if base + row >= first and base + row < first + off_ref.shape[0]:
+                put(off_ref, pl.ds(r + (base - first), ROWS), encode(u[::-1][:HALO]))
             if with_on:
                 put(on_ref, rows, encode(u[:HALO]))
 
-        row_loop(BLOCK, body)
+        row_loop(size, body)
+
+
+def pack_kernel(first, now, off_ref, buf, sems):
+    copies = fetch(now, buf, sems, first, buf.shape[1])
+    pack_rows(first, False, copies, buf, first, None, off_ref)
 
 
 def route_kernel(slabs, field, traces, weights, target, cell, out):
@@ -193,6 +192,14 @@
     out[...] = picked.reshape(out.shape)
 
 
+def route_pack_kernel(
+    slabs, first, traces, weights, target, cell, now, out, on_ref, off_ref, buf, sems
+):
+    copies = fetch(now, buf, sems, 0, now.shape[1])
+    route_kernel(slabs, now.shape, traces, weights, target, cell, out)
+    pack_rows(first, True, copies, buf, 0, on_ref, off_ref)
+
+
 def tile_parts(width_y):
     return [(lo, min(lo + LANES, width_y)) for lo in range(0, width_y + HALO, LANES)]
 
@@ -600,26 +607,24 @@
 
     got_off = []
     (face,) = call(
-        functools.partial(pack_kernel, 0, False),
+        functools.partial(pack_kernel, 0),
         [HBM],
         [plane(split)],
         (buffer(split), dma((blocks(split),))),
     )(now)
     got_off.append(swap(face, off_pairs))
     face, traces = lax.optimization_barrier((face, traces))
-    (sent,) = call(
-        functools.partial(route_kernel, slabs, now.shape),
-        [VMEM] * 4,
-        [jax.ShapeDtypeStruct((slabs, 1, LANES), F32)],
-    )(traces, weights, target.reshape(1, rows), cell.reshape(1, rows))
+    sent, on_face, face = call(
+        functools.partial(route_pack_kernel, slabs, split),
+        [VMEM] * 4 + [HBM],
+        [
+            jax.ShapeDtypeStruct((slabs, 1, LANES), F32),
+            plane(width_x),
+            plane(width_x - split),
+        ],
+        (buffer(width_x), dma((blocks(width_x),))),
+    )(traces, weights, target.reshape(1, rows), cell.reshape(1, rows), now)
     got = lax.all_to_all(sent, "slab", split_axis=0, concat_axis=0, tiled=True)
-    sent, later = lax.optimization_barrier((sent, now))
-    on_face, face = call(
-        functools.partial(pack_kernel, split, True),
-        [HBM],
-        [plane(width_x), plane(width_x - split)],
-        (buffer(width_x), dma((blocks(width_x),))),
-    )(later)
     got_off.append(swap(face, off_pairs))
     got_on = swap(on_face, on_pairs)
     parts, held, speed, second_on, second_off = [], [], [], [], []

time: 60.7 us -> 60.5 us (level)
    pallas_call x3 -> x2, Pallas kernels: 5.15 us -> 4.99 us  [the longest x1 3 us: shard(): call(functools.partial(route_pack_kernel, slabs, split), [VMEM] * 4 + [HB...]
where the time goes in v11:
time: 60.5 us; the launch traced here: 60.2 us
  Pallas kernels  27.6 us (46%)
  blocking collectives  17 us (28%)
  starting transfers between devices  13.6 us (22%)
  waiting for transfers between devices  1.13 us (2%)
  between operations  0.82 us (1%)
    all_to_all x1, blocking collectives, shard(): got = lax.all_to_all(sent, 'slab', split_axis=0, concat_axis=0, tiled=True)  17 us
    ppermute x7, starting transfers between devices, swap(): return lax.ppermute(face, 'slab', pairs)  13.6 us
    pallas_call x2, Pallas kernels, shard(): call(functools.partial(first_kernel, first, width_x, tuple(pieces)), [HBM...  11.9 us
    pallas_call x1, Pallas kernels, shard(): call(functools.partial(second_kernel, first, starts), [VMEM] * (len(parts...  5.09 us
    pallas_call x1, Pallas kernels, shard(): call(functools.partial(partial_kernel, last, starts), [VMEM] * (len(parts...  3.75 us
    pallas_call x1, Pallas kernels, shard(): call(functools.partial(route_pack_kernel, slabs, split), [VMEM] * 4 + [HB...  3 us
    pallas_call x1, Pallas kernels, shard(): call(functools.partial(pack_kernel, 0), [HBM], [plane(split)], (buffer(sp...  1.99 us
    pallas_call x1, Pallas kernels, shard(): call(functools.partial(last_kernel, last), [VMEM] * 6 + [HBM] * 2, [field...  1.81 us
  transfers between devices with their start and end apart: 7, of which 1 were waited for; matrix products, arithmetic and copies ran while one was open for 0% of the time, Pallas kernels for 34%

profile of v11, /device:TPU:9, one launch (start us, length us, event | category | flops | bytes accessed | tf_op | source)
XLA Modules:
  0.0 60.2 jit_solution(3501329182663759150)
XLA Ops:
  0.6 0.0 copy-start.1
  0.6 0.0 copy-start.4
  0.7 0.0 copy-start.3
  0.7 0.0 copy-start.2
  0.7 2.0 %shard_map.112 = bf16[192,1280]{1,0:T(8,128)(2,1)S(1)} custom-call(f32[4,320,320]{2,1,0:T(8,128)} %now.7), custom_call_target="tpu_custom_call" | custom-call | tf_op jit(solution)/shard_map/pallas_call | solution.py:609
  2.7 0.0 copy-done.1
  2.7 0.0 copy-done.4
  2.7 0.0 copy-done.3
  2.7 0.0 copy-done.2
  2.7 3.0 %shard_map.113 = (f32[16,1,128]{2,1,0:T(1,128)S(1)}, bf16[320,1280]{1,0:T(8,128)(2,1)S(1)}, bf16[128,1280]{1,0:T(8,128)(2,1)S(1)}) custom-call(bf16[64,2048]{1,0:T(8,128)(2,1)S(1)} %copy-done.1, bf16[2,2048]{1,0:T(2,128)(2,1)S(1)} %copy-done.2, s32[1,64]{1,0:T(1,128)S(1)} %bitcast.2, s32[1,64]{1,0:T(1,128)S(1)} %bitcast.3, f32[4,320,320]{2,1,0:T(8,128)} %now.7), custom_call_target="tpu_custom_call" | custom-call | tf_op jit(solution)/shard_map/pallas_call | solution.py:617
  5.7 0.7 %collective-permute-start = (bf16[320,1280]{1,0:T(8,128)(2,1)S(1)}, bf16[320,1280]{1,0:T(8,128)(2,1)S(1)}, u32[]{:S(2)}, u32[]{:S(2)}) collective-permute-start(bf16[320,1280]{1,0:T(8,128)(2,1)S(1)} %get-tuple-element.29), channel_id=1, source_target_pairs={{0,1},{1,0},{2,3},{3,2},{4,5},{5,4},{6,7},{7,6},{8,9},{9,8},{10,11... | collective-permute-start | bytes 2457608 | tf_op jit(solution)/shard_map/ppermute | solution.py:606
  6.5 3.0 %collective-permute-start.1 = (bf16[192,1280]{1,0:T(8,128)(2,1)S(1)}, bf16[192,1280]{1,0:T(8,128)(2,1)S(1)}, u32[]{:S(2)}, u32[]{:S(2)}) collective-permute-start(bf16[192,1280]{1,0:T(8,128)(2,1)S(1)} %shard_map.112), channel_id=1, source_target_pairs={{1,2},{2,1},{3,4},{4,3},{5,6},{6,5},{7,8},{8,7},{9,10},{10,9},{11,... | collective-permute-start | bytes 1474568 | tf_op jit(solution)/shard_map/ppermute | solution.py:606
  9.5 2.5 %collective-permute-start.2 = (bf16[128,1280]{1,0:T(8,128)(2,1)S(1)}, bf16[128,1280]{1,0:T(8,128)(2,1)S(1)}, u32[]{:S(2)}, u32[]{:S(2)}) collective-permute-start(bf16[128,1280]{1,0:T(8,128)(2,1)S(1)} %get-tuple-element.32), channel_id=1, source_target_pairs={{1,2},{2,1},{3,4},{4,3},{5,6},{6,5},{7,8},{8,7},{9,10},{10,9},{11,... | collective-permute-start | bytes 983048 | tf_op jit(solution)/shard_map/ppermute | solution.py:606
  12.0 17.0 %all_to_all.5.got.refs_6_ = f32[16,1,128]{2,1,0:T(1,128)S(1)} all-to-all(f32[16,1,128]{2,1,0:T(1,128)S(1)} %get-tuple-element.28), channel_id=1, replica_groups=mesh['groups'=2,'slab'=16] {'slab'}, dimensions={0} | all-to-all | bytes 16384 | tf_op jit(solution)/shard_map/all_to_all | solution.py:627
  29.1 0.0 collective-permute-done.1.refs_0_
  29.1 0.0 collective-permute-done.got_on
  29.1 6.0 %shard_map.114 = (f32[4,160,320]{2,1,0:T(8,128)S(1)}, bf16[160,1280]{1,0:T(8,128)(2,1)S(1)}, bf16[160,1280]{1,0:T(8,128)(2,1)S(1)}, f32[4,168,320]{2,1,0:T(8,128...) custom-call(f32[4,320,320]{2,1,0:T(8,128)} %now.7, f32[4,320,320]{2,1,0:T(8,128)} %prior.3, ...), custom_call_target="tpu_custom_call" | custom-call | tf_op jit(solution)/shard_map/pallas_call | solution.py:639
  35.1 0.7 %collective-permute-start.5 = (bf16[160,1280]{1,0:T(8,128)(2,1)S(1)}, bf16[160,1280]{1,0:T(8,128)(2,1)S(1)}, u32[]{:S(2)}, u32[]{:S(2)}) collective-permute-start(bf16[160,1280]{1,0:T(8,128)(2,1)S(1)} %get-tuple-element.44), channel_id=1, source_target_pairs={{0,1},{1,0},{2,3},{3,2},{4,5},{5,4},{6,7},{7,6},{8,9},{9,8},{10,11... | collective-permute-start | bytes 1228808 | tf_op jit(solution)/shard_map/ppermute | solution.py:606
  35.8 2.5 %collective-permute-start.6 = (bf16[160,1280]{1,0:T(8,128)(2,1)S(1)}, bf16[160,1280]{1,0:T(8,128)(2,1)S(1)}, u32[]{:S(2)}, u32[]{:S(2)}) collective-permute-start(bf16[160,1280]{1,0:T(8,128)(2,1)S(1)} %get-tuple-element.45), channel_id=1, source_target_pairs={{1,2},{2,1},{3,4},{4,3},{5,6},{6,5},{7,8},{8,7},{9,10},{10,9},{11,... | collective-permute-start | bytes 1228808 | tf_op jit(solution)/shard_map/ppermute | solution.py:606
  38.3 0.0 collective-permute-done.2.refs_1_
  38.3 0.0 copy-start
  38.3 5.9 %shard_map.115 = (f32[4,160,320]{2,1,0:T(8,128)S(1)}, bf16[160,1280]{1,0:T(8,128)(2,1)S(1)}, bf16[160,1280]{1,0:T(8,128)(2,1)S(1)}, f32[4,168,320]{2,1,0:T(8,128)S(1)}, f32[4,160,320]{2,1,0:T(8,128)S(1)}) custom-call(f32[4,320,320]{2,1,0:T(8,128)} %now.7, f32[4,320,320]{2,1,0:T(8,128)} %prior.3, f32[4,320,320]{2,1,0:T(8,128)} %velocity.3, ...), custom_call_target="tpu_custom_call" | custom-call | tf_op jit(solution)/shard_map/pallas_call | solution.py:639
  44.2 0.4 collective-permute-start.3
  44.6 3.7 %collective-permute-start.4 = (bf16[160,1280]{1,0:T(8,128)(2,1)S(1)}, bf16[160,1280]{1,0:T(8,128)(2,1)S(1)}, u32[]{:S(2)}, u32[]{:S(2)}) collective-permute-start(bf16[160,1280]{1,0:T(8,128)(2,1)S(1)} %get-tuple-element.41), channel_id=1, source_target_pairs={{1,2},{2,1},{3,4},{4,3},{5,6},{6,5},{7,8},{8,7},{9,10},{10,9},{11,... | collective-permute-start | bytes 1228808 | tf_op jit(solution)/shard_map/ppermute | solution.py:606
  48.4 0.0 copy-done
  48.4 3.7 %shard_map.116 = (f32[4,320,320]{2,1,0:T(8,128)}, f32[4,160,320]{2,1,0:T(8,128)S(1)}, f32[4,160,320]{2,1,0:T(8,128)S(1)}) custom-call(f32[4,160,320]{2,1,0:T(8,128)S(1)} %get-tuple-element.30.refs_0_, f32[4,160,320]{2,1,0:T(8,128)S(1)} %get-tuple-element.34.refs_1_, f32[4,168,320]{2,1,0:T(8,128)S(1)} %get-tuple-element.35.refs_2_, ...), custom_call_target="tpu_custom_call" | custom-call | tf_op jit(solution)/shard_map/pallas_call | solution.py:653
  52.1 0.0 collective-permute-done.5.refs_7_
  52.1 0.0 collective-permute-done.6.refs_8_
  52.1 5.1 %shard_map.117 = (f32[4,320,320]{2,1,0:T(8,128)}, f32[4,320,320]{2,1,0:T(8,128)}) custom-call(f32[4,160,320]{2,1,0:T(8,128)S(1)} %get-tuple-element.30.refs_0_, f32[4,160,320]{2,1,0:T(8,128)S(1)} %get-tuple-element.34.refs_1_, f32[4,168,320]{2,1,0:T(8,128)S(1)} %get-tuple-element.42.refs_2_, f32[4,160,320]{2,1,0:T(8,128)S(1)} %get-tuple-element.43.refs_3_, ...), custom_call_target="tpu_custom_call" | custom-call | tf_op jit(solution)/shard_map/pallas_call | solution.py:660
  57.2 0.0 collective-permute-done.3.got_on
  57.2 1.1 %collective-permute-done.4.got_off = bf16[160,1280]{1,0:T(8,128)(2,1)S(1)} collective-permute-done((bf16[160,1280]{1,0:T(8,128)(2,1)S(1)}, bf16[160,1280]{1,0:T(8,128)(2,1)S(1)}, u32[]{:S(2)}, u32[]{:S(2)}) %collective-permute-start.4) | collective-permute-done | bytes 409632 | tf_op jit(solution)/shard_map/ppermute | solution.py:606
  58.4 1.8 %shard_map.118 = (f32[4,320,320]{2,1,0:T(8,128)}, f32[4,320,320]{2,1,0:T(8,128)}) custom-call(f32[4,160,320]{2,1,0:T(8,128)S(1)} %get-tuple-element.38.partial, f32[4,160,320]{2,1,0:T(8,128)S(1)} %get-tuple-element.39.image_in, f32[4,160,320]{2,1,0:T(8,128)S(1)} %get-tuple-element.36.refs_3_.speed, ...), custom_call_target="tpu_custom_call", output_to_operand_aliasing={{0}: (6, {}), {1}: (7, {})} | custom-call | tf_op jit(solution)/shard_map/pallas_call | solution.py:667
Async XLA Ops:
  0.6 2.0 %copy-start.1 = (bf16[64,2048]{1,0:T(8,128)(2,1)S(1)}, bf16[64,2048]{1,0:T(8,128)(2,1)}, u32[]{:S(2)}) copy-start(bf16[64,2048]{1,0:T(8,128)(2,1)} %traces) | copy-start | bytes 786436
  0.6 2.0 %copy-start.4 = (s32[64]{0:T(128)S(1)}, s32[64]{0:T(128)}, u32[]{:S(2)}) copy-start(s32[64]{0:T(128)} %param.16) | copy-start | bytes 772
  0.7 2.0 %copy-start.3 = (s32[64,1]{0,1:T(1,128)S(1)}, s32[64,1]{0,1:T(1,128)}, u32[]{:S(2)}) copy-start(s32[64,1]{0,1:T(1,128)} %param.15) | copy-start | bytes 772
  0.7 2.0 %copy-start.2 = (bf16[2,2048]{1,0:T(2,128)(2,1)S(1)}, bf16[2,2048]{1,0:T(2,128)(2,1)}, u32[]{:S(2)}) copy-start(bf16[2,2048]{1,0:T(2,128)(2,1)} %weights.1) | copy-start | bytes 24580
  5.7 23.3 %collective-permute-start = (bf16[320,1280]{1,0:T(8,128)(2,1)S(1)}, bf16[320,1280]{1,0:T(8,128)(2,1)S(1)}, u32[]{:S(2)}, u32[]{:S(2)}) collective-permute-start(bf16[320,1280]{1,0:T(8,128)(2,1)S(1)} %get-tuple-element.29), channel_id=1, source_target_pairs={{0,1},{1,0},{2,3},{3,2},{4,5},{5,4},{6,7},{7,6},{8,9},{9,8},{10,11... | collective-permute-start | bytes 2457608 | tf_op jit(solution)/shard_map/ppermute | solution.py:606
  6.5 22.6 %collective-permute-start.1 = (bf16[192,1280]{1,0:T(8,128)(2,1)S(1)}, bf16[192,1280]{1,0:T(8,128)(2,1)S(1)}, u32[]{:S(2)}, u32[]{:S(2)}) collective-permute-start(bf16[192,1280]{1,0:T(8,128)(2,1)S(1)} %shard_map.112), channel_id=1, source_target_pairs={{1,2},{2,1},{3,4},{4,3},{5,6},{6,5},{7,8},{8,7},{9,10},{10,9},{11,... | collective-permute-start | bytes 1474568 | tf_op jit(solution)/shard_map/ppermute | solution.py:606
  9.5 28.8 %collective-permute-start.2 = (bf16[128,1280]{1,0:T(8,128)(2,1)S(1)}, bf16[128,1280]{1,0:T(8,128)(2,1)S(1)}, u32[]{:S(2)}, u32[]{:S(2)}) collective-permute-start(bf16[128,1280]{1,0:T(8,128)(2,1)S(1)} %get-tuple-element.32), channel_id=1, source_target_pairs={{1,2},{2,1},{3,4},{4,3},{5,6},{6,5},{7,8},{8,7},{9,10},{10,9},{11,... | collective-permute-start | bytes 983048 | tf_op jit(solution)/shard_map/ppermute | solution.py:606
  35.1 17.0 %collective-permute-start.5 = (bf16[160,1280]{1,0:T(8,128)(2,1)S(1)}, bf16[160,1280]{1,0:T(8,128)(2,1)S(1)}, u32[]{:S(2)}, u32[]{:S(2)}) collective-permute-start(bf16[160,1280]{1,0:T(8,128)(2,1)S(1)} %get-tuple-element.44), channel_id=1, source_target_pairs={{0,1},{1,0},{2,3},{3,2},{4,5},{5,4},{6,7},{7,6},{8,9},{9,8},{10,11... | collective-permute-start | bytes 1228808 | tf_op jit(solution)/shard_map/ppermute | solution.py:606
  35.8 16.4 %collective-permute-start.6 = (bf16[160,1280]{1,0:T(8,128)(2,1)S(1)}, bf16[160,1280]{1,0:T(8,128)(2,1)S(1)}, u32[]{:S(2)}, u32[]{:S(2)}) collective-permute-start(bf16[160,1280]{1,0:T(8,128)(2,1)S(1)} %get-tuple-element.45), channel_id=1, source_target_pairs={{1,2},{2,1},{3,4},{4,3},{5,6},{6,5},{7,8},{8,7},{9,10},{10,9},{11,... | collective-permute-start | bytes 1228808 | tf_op jit(solution)/shard_map/ppermute | solution.py:606
  38.3 10.1 %copy-start = (f32[2,4,320,320]{3,2,1,0:T(8,128)S(1)}, f32[2,4,320,320]{3,2,1,0:T(8,128)}, u32[]{:S(2)}) copy-start(f32[2,4,320,320]{3,2,1,0:T(8,128)} %forward) | copy-start | bytes 9830404
  44.2 13.1 %collective-permute-start.3 = (bf16[160,1280]{1,0:T(8,128)(2,1)S(1)}, bf16[160,1280]{1,0:T(8,128)(2,1)S(1)}, u32[]{:S(2)}, u32[]{:S(2)}) collective-permute-start(bf16[160,1280]{1,0:T(8,128)(2,1)S(1)} %get-tuple-element.40), channel_id=1, source_target_pairs={{0,1},{1,0},{2,3},{3,2},{4,5},{5,4},{6,7},{7,6},{8,9},{9,8},{10,11... | collective-permute-start | bytes 1228808 | tf_op jit(solution)/shard_map/ppermute | solution.py:606
  44.6 13.8 %collective-permute-start.4 = (bf16[160,1280]{1,0:T(8,128)(2,1)S(1)}, bf16[160,1280]{1,0:T(8,128)(2,1)S(1)}, u32[]{:S(2)}, u32[]{:S(2)}) collective-permute-start(bf16[160,1280]{1,0:T(8,128)(2,1)S(1)} %get-tuple-element.41), channel_id=1, source_target_pairs={{1,2},{2,1},{3,4},{4,3},{5,6},{6,5},{7,8},{8,7},{9,10},{10,9},{11,... | collective-permute-start | bytes 1228808 | tf_op jit(solution)/shard_map/ppermute | solution.py:606
